TPU v7x, 32 devices: a whole 2x2x4 slice. The times are simulated.
32 devices in a mesh: parts: 2 (over y), sub: 4 (over z), row: 2 (over x), col: 2 (over core).
Axes of the slice: x: 2, y: 2, z: 4, core: 2. Of those that a mesh axis runs over, the one named last changes fastest.
Arguments:
- loads: float32 [8, 32, 1024], P(('parts', 'sub'), 'col'), parts along dimension 0, may hold values from -6 to 6
- weights: float32 [8, 1024], P(('parts', 'sub')), parts along dimension 0, may hold values from 0.25 to 4
- dual_ops: bfloat16 [8, 2048, 2048], P(('parts', 'sub'), 'row'), parts along dimension 0, as said below
- corner_maps: bfloat16 [8, 24, 2048], P(('parts', 'sub'), None, 'row'), parts along dimension 0, may hold values from -0.25 to 0.25
- coarse_inverse: float32 [96, 48], P('parts'), parts along dimension 0, as said below
- corner_ids: int32 [8, 24], P('parts'), parts along dimension 0, may hold values from 0 to 47, as said below
- iface_sizes: int32 [8], P('parts'), parts along dimension 0, may hold values from 512 to 1024, as said below
- left_partner: int32 [8, 1024], P(('parts', 'sub')), parts along dimension 0, may hold values from 0 to 1023, as said below
- right_partner: int32 [8, 1024], P(('parts', 'sub')), parts along dimension 0, may hold values from 0 to 1023, as said below
Outputs:
- solution: float32 [8, 32, 1024], P(('parts', 'sub'), 'col'), parts along dimension 0
- residual: float32 [8, 32, 1024], P(('parts', 'sub'), 'col'), parts along dimension 0
There are 2 independent parts, one for each index of `parts`. A program takes and returns all parts, laid end to end along the dimension named above; each array names one. Nothing has to cross between parts.
Inputs may be any that keep to these rules, and one draw needn't show every extreme that they name: Global indices 24/2 * s to 24/2 * s + 24/2 - 1 are the corners of the interface between s and s+1; the first half of subdomain s's corner_ids is a permutation of those of interface s-1, the second half a permutation of those of interface s. `left_partner`: each row s is a permutation that maps the slots below iface_sizes[s-1] onto slots below it. `right_partner`: each row s is a permutation that maps the slots below iface_sizes[s] onto slots below it, and is the inverse of left_partner[s+1]. `dual_ops`: symmetric positive definite. `coarse_inverse`: symmetric positive definite. For each s < 2, one of iface_sizes[s] and iface_sizes[s + 2] is 896 or more and the other 640 or less.
All inputs are finite; a program needn't handle non-finite values.
Results may differ from a plain program's by a relative error of at most 0.015.
Values may be sent and summed in bfloat16 or wider, within the bound.
No kernel may reach another device: no remote copies, remote signals or barrier semaphores. Data moves between devices by JAX's collectives and lax.ppermute only.
A program may use at most 64 MiB of HBM per device.

v0:
```python
import jax
import jax.numpy as jnp
from jax import lax
from jax.sharding import PartitionSpec as P

TILE = 128
ITERS = 2


def shifted(value, axis, steps):
    count = lax.axis_size(axis)
    pairs = [(source, (source + steps) % count) for source in range(count)]
    return lax.ppermute(value, axis, pairs)


def inner(first, second, half):
    return jnp.sum(first[:, :half] * second[:, :half], axis=1)


def paired_totals(residual, precond, image, half):
    return lax.psum((inner(residual, precond, half), inner(precond, image, half)), "sub")


def tile_products(vector, rows_op, first_tile, last_tile, output):

    def one_tile(tile_at, acc):
        piece = lax.dynamic_slice_in_dim(rows_op, tile_at * TILE, TILE, 0)
        product = lax.dot_general(
            vector, piece, (((1,), (1,)), ((), ())), preferred_element_type=jnp.float32
        )
        return lax.dynamic_update_slice_in_dim(acc, product, tile_at * TILE, 1)

    return lax.fori_loop(first_tile, last_tile, one_tile, output)


def live_tiles(size_before, size_after, block_start, block, half):
    left_live = jnp.clip(size_before - block_start, 0, block)
    right_live = jnp.clip(size_after - (block_start - half), 0, block)
    live_cols = jnp.where(block_start < half, left_live, right_live)
    return (live_cols + TILE - 1) // TILE


def per_device(
    loads,
    weights,
    dual_ops,
    corner_maps,
    coarse_inverse,
    corner_ids,
    iface_sizes,
    left_partner,
    right_partner,
):
    half = loads.shape[2]
    block = dual_ops.shape[1]
    width = coarse_inverse.shape[0]
    subdomain = lax.axis_index("sub")
    count = lax.axis_size("sub")
    row_index = lax.axis_index("row")
    left_map = left_partner[0]
    right_map = right_partner[0]
    slots = jnp.arange(half, dtype=jnp.int32)
    size_before = iface_sizes[(subdomain + count - 1) % count]
    size_after = iface_sizes[subdomain]
    live_left = (slots < size_before).astype(jnp.float32)
    live_right = (right_map < size_after).astype(jnp.float32)
    columns = jnp.arange(width, dtype=jnp.int32)
    own_hot = (corner_ids[subdomain][:, None] == columns[None, :]).astype(jnp.float32)
    operator = dual_ops[0]
    coupling = corner_maps[0]
    block_start = row_index * block
    own_tiles = live_tiles(size_before, size_after, block_start, block, half)

    def apply_operator(vec):
        halfway = vec.astype(jnp.bfloat16)
        empty = jnp.zeros((halfway.shape[0], block), jnp.float32)
        local = tile_products(halfway, operator, jnp.int32(0), own_tiles, empty)
        own_slots = lax.dynamic_slice_in_dim(halfway, row_index * block, block, 1)
        corner = lax.dot_general(
            own_slots, coupling, (((1,), (1,)), ((), ())), preferred_element_type=jnp.float32
        )
        scattered = jnp.dot(corner, own_hot, precision=lax.Precision.HIGHEST)
        coarse = lax.psum(scattered, ("sub", "row"))
        solved = jnp.dot(coarse, coarse_inverse, precision=lax.Precision.HIGHEST)
        back = lax.dot_general(
            solved, own_hot, (((1,), (1,)), ((), ())), precision=lax.Precision.HIGHEST
        ).astype(jnp.bfloat16)
        united = local + jnp.dot(back, coupling, preferred_element_type=jnp.float32)
        whole = lax.all_gather(united.astype(jnp.bfloat16), "row", axis=1, tiled=True).astype(
            united.dtype
        )
        lower = whole[:, :half]
        upper = whole[:, half:]
        arrived_left = shifted(upper.astype(jnp.bfloat16), "sub", 1).astype(upper.dtype)
        arrived_right = shifted(lower.astype(jnp.bfloat16), "sub", -1).astype(lower.dtype)
        result_left = (lower + jnp.take(arrived_left, left_map, axis=1)) * live_left
        result_right = (upper + jnp.take(arrived_right, right_map, axis=1)) * live_right
        return jnp.concatenate([result_left, result_right], axis=1)

    received = (
        shifted(loads[0].astype(jnp.bfloat16), "sub", -1).astype(jnp.float32),
        shifted(weights.astype(jnp.bfloat16), "sub", -1).astype(weights.dtype),
    )
    right_load = jnp.take(received[0], right_map, axis=1) * live_right
    right_weight = jnp.take(received[1], right_map, axis=1)
    residual = jnp.concatenate([loads[0] * live_left, right_load], axis=1)
    scaling = jnp.concatenate([weights, right_weight], axis=1)
    solution = jnp.zeros_like(residual)
    precond = scaling * residual
    image = apply_operator(precond)
    gamma, delta = paired_totals(residual, precond, image, half)
    alpha = gamma / delta
    direction = precond
    along = image
    for step in range(ITERS):
        solution = solution + alpha[:, None] * direction
        residual = residual - alpha[:, None] * along
        if step + 1 < ITERS:
            precond = scaling * residual
            image = apply_operator(precond)
            gamma_next, delta = paired_totals(residual, precond, image, half)
            ratio = gamma_next / gamma
            alpha = gamma_next / (delta - ratio * gamma_next / alpha)
            direction = precond + ratio[:, None] * direction
            along = image + ratio[:, None] * along
            gamma = gamma_next
    return (solution[:, :half][None], residual[:, :half][None])


def solution(mesh):
    placed = (
        P(("parts", "sub"), "col", None),
        P(("parts", "sub"), None),
        P(("parts", "sub"), "row", None),
        P(("parts", "sub"), None, "row"),
        P("parts", None),
        P("parts", None),
        P("parts"),
        P(("parts", "sub"), None),
        P(("parts", "sub"), None),
    )
    return jax.shard_map(
        per_device,
        mesh=mesh,
        in_specs=placed,
        out_specs=(P(("parts", "sub"), "col", None), P(("parts", "sub"), "col", None)),
        check_vma=False,
    )
```

profile of v0, /device:TPU:0, one launch (start us, length us, event | category | flops | bytes accessed | tf_op | source)
XLA Modules:
  0.0 136.2 jit_solution(17909804324471528583)
XLA Ops:
  0.7 0.9 bitcast_convert_fusion
  1.5 5.1 %collective-permute-start.1 = (bf16[16,1024]{1,0:T(8,128)(2,1)S(1)}, bf16[16,1024]{1,0:T(8,128)(2,1)S(1)}, u32[]{:S(2)}, u32[]{:S(2)}) collective-permute-start(bf16[16,1024]{1,0:T(8,128)(2,1)S(1)} %bitcast_convert_fusion), channel_id=1, source_target_pairs={{0,12},{4,0},{8,4},{12,8},{1,13},{5,1},{9,5},{13,9},{2,14},{6,2},{... | collective-permute-start | bytes 98312 | tf_op jit(solution)/shard_map/ppermute | solution.py:13
  6.6 0.7 convert_element_type.71
  7.3 0.4 collective-permute-start
  7.8 0.7 compare_select_fusion
  8.4 0.7 fusion.36
  9.1 1.3 fusion.49
  10.5 1.3 fusion.35
  11.8 1.3 compare_convert_fusion
  13.1 0.8 bitcast_multiply_fusion.1
  14.0 0.7 fusion.40
  14.7 0.7 fusion.37
  16.7 4.5 %gather_fusion = f32[1024]{0:T(1024)S(1)} fusion(f32[1024]{0:T(1024)S(1)} %bitcast.80, s32[1024]{0:T(1024)S(1)} %broadcast_clamp_fusion), kind=kCustom, calls=%fused_computation.5 | custom fusion | bytes 12288 | tf_op jit(solution)/shard_map/jit(_take)/gather | solution.py:105
  21.4 0.1 copy.21
  21.5 2.8 %gather_fusion.1 = f32[1024,16]{1,0:T(8,128)S(1)} fusion(f32[16,1024]{0,1:T(8,128)S(1)} %copy.21, s32[1024]{0:T(1024)S(1)} %fusion.36), kind=kCustom, calls=%fused_computation.clone | custom fusion | bytes 135168 | tf_op jit(solution)/shard_map/jit(_take)/gather | solution.py:104
  24.3 0.2 copy.22
  24.5 10.4 %while.20 = (s32[]{:T(128)}, f32[16,1024]{1,0:T(8,128)S(1)}, s32[]{:T(128)}, bf16[1024,2048]{1,0:T(8,128)(2,1)}, bf16[16,2048]{1,0:T(8,128)(2,1)S(1)}, /*index=5*/s32[]{:T(128)}, s32[]{:T(128)}, s32[]{:T(128)}, s32[]{:T(128)}) while((s32[]{:T(128)}, f32[16,1024]{1,0:T(8,128)S(1)}, s32[]{:T(128)}, bf16[1024,2048]{1,0:T(8,128)(2,1)}, ...), condition=%wide.region_3.5_spmd, body=%wide.region_2.4_spmd.sunk | while | flops 8388614 | bytes 599179 | solution.py:33
  24.6 1.3 fusion.72
  25.9 1.3 fusion.72
  27.1 1.3 fusion.72
  28.4 1.3 fusion.72
  29.7 1.3 fusion.72
  31.0 1.3 fusion.72
  32.3 1.3 fusion.72
  33.6 1.3 fusion.72
  34.9 0.1 fusion.25
  35.1 0.2 fusion.30
  35.3 18.7 %psum.43 = f32[16,48]{1,0:T(8,128)S(1)} all-reduce(f32[16,48]{1,0:T(8,128)S(1)} %fusion.30), channel_id=1, replica_groups=mesh['parts'=2,'sub'=4,'row'=2,'col'=2] {'sub','row'}, use_global_device_ids=true, to_apply=%region_4.6 | all-reduce | flops 768 | bytes 6144 | tf_op jit(solution)/shard_map/psum | solution.py:83
  54.2 0.2 convolution_convert_fusion.1
  54.4 0.1 fusion.6
  54.5 4.6 %all_gather.6 = bf16[16,2048]{1,0:T(8,128)(2,1)S(1)} all-gather(bf16[16,1024]{1,0:T(8,128)(2,1)S(1)} %fusion.6), channel_id=1, replica_groups=mesh['parts'=2,'sub'=4,'row'=2,'col'=2] {'row'}, dimensions={1}, use_global_device_ids=true | all-gather | bytes 98304 | tf_op jit(solution)/shard_map/all_gather | solution.py:89
  59.1 3.8 %collective-permute-start.3 = (bf16[16,1024]{1,0:T(8,128)(2,1)S(1)}, bf16[16,1024]{1,0:T(8,128)(2,1)S(1)}, u32[]{:S(2)}, u32[]{:S(2)}) collective-permute-start(bf16[16,1024]{1,0:T(8,128)(2,1)S(1)} %get-tuple-element.103), channel_id=1, source_target_pairs={{0,12},{4,0},{8,4},{12,8},{1,13},{5,1},{9,5},{13,9},{2,14},{6,2},{... | collective-permute-start | bytes 98312 | tf_op jit(solution)/shard_map/ppermute | solution.py:13
  63.0 1.9 %collective-permute-done.2 = bf16[16,1024]{1,0:T(8,128)(2,1)S(1)} collective-permute-done((bf16[16,1024]{1,0:T(8,128)(2,1)S(1)}, bf16[16,1024]{1,0:T(8,128)(2,1)S(1)}, u32[]{:S(2)}, u32[]{:S(2)}) %collective-permute-start.2) | collective-permute-done | bytes 32800 | tf_op jit(solution)/shard_map/ppermute | solution.py:13
  64.9 2.8 %gather_fusion.2 = f32[1024,16]{1,0:T(8,128)S(1)} fusion(f32[16,1024]{0,1:T(8,128)S(1)} %copy.23, s32[1024]{0:T(1024)S(1)} %fusion.37), kind=kCustom, calls=%fused_computation.1.clone | custom fusion | bytes 135168 | tf_op jit(solution)/shard_map/jit(_take)/gather | solution.py:96
  67.8 0.2 copy.24
  67.9 0.1 copy.25
  68.1 2.8 %gather_fusion.3 = f32[1024,16]{1,0:T(8,128)S(1)} fusion(f32[16,1024]{0,1:T(8,128)S(1)} %copy.25, s32[1024]{0:T(1024)S(1)} %fusion.36), kind=kCustom, calls=%fused_computation.2.clone | custom fusion | bytes 135168 | tf_op jit(solution)/shard_map/jit(_take)/gather | solution.py:97
  70.9 0.2 copy.26
  71.1 0.1 multiply_reduce_fusion.2
  71.2 9.1 %all-reduce.1 = (f32[16]{0:T(128)S(1)}, f32[16]{0:T(128)S(1)}) all-reduce(f32[16]{0:T(128)S(1)} %get-tuple-element.64, f32[16]{0:T(128)S(1)} %get-tuple-element.63), channel_id=1, replica_groups=mesh['parts'=2,'sub'=4,'row'=2,'col'=2] {'sub'}, use_global_device_ids=true, to_apply=%region_1.3 | all-reduce | flops 32 | bytes 256 | tf_op jit(solution)/shard_map/psum | solution.py:21
  80.5 10.3 %while.21 = (s32[]{:T(128)}, f32[16,1024]{1,0:T(8,128)S(1)}, s32[]{:T(128)}, bf16[1024,2048]{1,0:T(8,128)(2,1)}, bf16[16,2048]{1,0:T(8,128)(2,1)S(1)}, /*index=5*/s32[]{:T(128)}, s32[]{:T(128)}, s32[]{:T(128)}, s32[]{:T(128)}) while((s32[]{:T(128)}, f32[16,1024]{1,0:T(8,128)S(1)}, s32[]{:T(128)}, bf16[1024,2048]{1,0:T(8,128)(2,1)}, ...), condition=%wide.region_10.12_spmd, body=%wide.region_9.11_spmd.sunk | while | flops 8388614 | bytes 599179 | solution.py:33
  80.5 1.3 fusion.75
  81.8 1.3 fusion.75
  83.1 1.3 fusion.75
  84.4 1.3 fusion.75
  85.7 1.3 fusion.75
  87.0 1.3 fusion.75
  88.3 1.3 fusion.75
  89.6 1.3 fusion.75
  90.9 0.2 fusion.29
  91.1 18.8 %psum.46 = f32[16,48]{1,0:T(8,128)S(1)} all-reduce(f32[16,48]{1,0:T(8,128)S(1)} %fusion.29), channel_id=1, replica_groups=mesh['parts'=2,'sub'=4,'row'=2,'col'=2] {'sub','row'}, use_global_device_ids=true, to_apply=%region_11.13 | all-reduce | flops 768 | bytes 6144 | tf_op jit(solution)/shard_map/psum | solution.py:83
  110.0 0.2 convolution_convert_fusion
  110.2 0.1 fusion.7
  110.3 4.6 %all_gather.7 = bf16[16,2048]{1,0:T(8,128)(2,1)S(1)} all-gather(bf16[16,1024]{1,0:T(8,128)(2,1)S(1)} %fusion.7), channel_id=1, replica_groups=mesh['parts'=2,'sub'=4,'row'=2,'col'=2] {'row'}, dimensions={1}, use_global_device_ids=true | all-gather | bytes 98304 | tf_op jit(solution)/shard_map/all_gather | solution.py:89
  114.9 2.0 %collective-permute-start.4 = (bf16[16,1024]{1,0:T(8,128)(2,1)S(1)}, bf16[16,1024]{1,0:T(8,128)(2,1)S(1)}, u32[]{:S(2)}, u32[]{:S(2)}) collective-permute-start(bf16[16,1024]{1,0:T(8,128)(2,1)S(1)} %get-tuple-element.101), channel_id=1, source_target_pairs={{0,4},{4,8},{8,12},{12,0},{1,5},{5,9},{9,13},{13,1},{2,6},{6,10},{... | collective-permute-start | bytes 98312 | tf_op jit(solution)/shard_map/ppermute | solution.py:13
  117.0 1.9 %collective-permute-done.5 = bf16[16,1024]{1,0:T(8,128)(2,1)S(1)} collective-permute-done((bf16[16,1024]{1,0:T(8,128)(2,1)S(1)}, bf16[16,1024]{1,0:T(8,128)(2,1)S(1)}, u32[]{:S(2)}, u32[]{:S(2)}) %collective-permute-start.5) | collective-permute-done | bytes 32800 | tf_op jit(solution)/shard_map/ppermute | solution.py:13
  119.0 2.8 %gather_fusion.5 = f32[1024,16]{1,0:T(8,128)S(1)} fusion(f32[16,1024]{0,1:T(8,128)S(1)} %copy.29, s32[1024]{0:T(1024)S(1)} %fusion.36), kind=kCustom, calls=%fused_computation.4.clone | custom fusion | bytes 135168 | tf_op jit(solution)/shard_map/jit(_take)/gather | solution.py:97
  121.8 0.2 copy.30
  122.0 0.1 copy.27
  122.1 2.8 %gather_fusion.4 = f32[1024,16]{1,0:T(8,128)S(1)} fusion(f32[16,1024]{0,1:T(8,128)S(1)} %copy.27, s32[1024]{0:T(1024)S(1)} %fusion.37), kind=kCustom, calls=%fused_computation.3.clone | custom fusion | bytes 135168 | tf_op jit(solution)/shard_map/jit(_take)/gather | solution.py:96
  124.9 0.2 copy.28
  125.1 0.1 multiply_reduce_fusion
  125.2 10.2 %all-reduce = (f32[16]{0:T(128)S(1)}, f32[16]{0:T(128)S(1)}) all-reduce(f32[16]{0:T(128)S(1)} %get-tuple-element.62, f32[16]{0:T(128)S(1)} %get-tuple-element.61), channel_id=1, replica_groups=mesh['parts'=2,'sub'=4,'row'=2,'col'=2] {'sub'}, use_global_device_ids=true, to_apply=%region_8.10 | all-reduce | flops 32 | bytes 256 | tf_op jit(solution)/shard_map/psum | solution.py:21
  135.4 0.7 fusion.16
  (39 shorter events, 1.0 us)
Async XLA Ops:
  0.6 34.3 %copy-start = (bf16[1,24,1024]{2,1,0:T(8,128)(2,1)S(1)}, bf16[1,24,1024]{2,1,0:T(8,128)(2,1)}, u32[]{:S(2)}) copy-start(bf16[1,24,1024]{2,1,0:T(8,128)(2,1)} %param.18) | copy-start | bytes 147460
  0.6 20.7 %copy-start.5 = (f32[1,1024]{1,0:T(1,128)S(1)}, f32[1,1024]{1,0:T(1,128)}, u32[]{:S(2)}) copy-start(f32[1,1024]{1,0:T(1,128)} %param.16) | copy-start | bytes 12292
  0.7 20.6 %copy-start.2 = (s32[1,1024]{1,0:T(1,128)S(1)}, s32[1,1024]{1,0:T(1,128)}, u32[]{:S(2)}) copy-start(s32[1,1024]{1,0:T(1,128)} %param.23) | copy-start | bytes 12292
  1.5 19.8 %collective-permute-start.1 = (bf16[16,1024]{1,0:T(8,128)(2,1)S(1)}, bf16[16,1024]{1,0:T(8,128)(2,1)S(1)}, u32[]{:S(2)}, u32[]{:S(2)}) collective-permute-start(bf16[16,1024]{1,0:T(8,128)(2,1)S(1)} %bitcast_convert_fusion), channel_id=1, source_target_pairs={{0,12},{4,0},{8,4},{12,8},{1,13},{5,1},{9,5},{13,9},{2,14},{6,2},{... | collective-permute-start | bytes 98312 | tf_op jit(solution)/shard_map/ppermute | solution.py:13
  7.3 9.4 %collective-permute-start = (bf16[1,1024]{1,0:T(2,128)(2,1)S(1)}, bf16[1,1024]{1,0:T(2,128)(2,1)S(1)}, u32[]{:S(2)}, u32[]{:S(2)}) collective-permute-start(bf16[1,1024]{1,0:T(2,128)(2,1)S(1)} %convert_element_type.71), channel_id=1, source_target_pairs={{0,12},{4,0},{8,4},{12,8},{1,13},{5,1},{9,5},{13,9},{2,14},{6,2},{... | collective-permute-start | bytes 6152 | tf_op jit(solution)/shard_map/ppermute | solution.py:13
  16.7 37.3 %copy-start.3 = (f32[48,48]{1,0:T(8,128)S(1)}, f32[48,48]{1,0:T(8,128)}, u32[]{:S(2)}) copy-start(f32[48,48]{1,0:T(8,128)} %param.19) | copy-start | bytes 27652
  16.7 46.2 %copy-start.4 = (s32[1,1024]{1,0:T(1,128)S(1)}, s32[1,1024]{1,0:T(1,128)}, u32[]{:S(2)}) copy-start(s32[1,1024]{1,0:T(1,128)} %param.22) | copy-start | bytes 12292
  24.5 46.6 %copy-start.1 = (f32[1,16,1024]{2,1,0:T(8,128)S(1)}, f32[1,16,1024]{2,1,0:T(8,128)}, u32[]{:S(2)}) copy-start(f32[1,16,1024]{2,1,0:T(8,128)} %param.15) | copy-start | bytes 196612
  59.1 5.7 %collective-permute-start.2 = (bf16[16,1024]{1,0:T(8,128)(2,1)S(1)}, bf16[16,1024]{1,0:T(8,128)(2,1)S(1)}, u32[]{:S(2)}, u32[]{:S(2)}) collective-permute-start(bf16[16,1024]{1,0:T(8,128)(2,1)S(1)} %get-tuple-element.102), channel_id=1, source_target_pairs={{0,4},{4,8},{8,12},{12,0},{1,5},{5,9},{9,13},{13,1},{2,6},{6,10},{... | collective-permute-start | bytes 98312 | tf_op jit(solution)/shard_map/ppermute | solution.py:13
  59.1 8.8 %collective-permute-start.3 = (bf16[16,1024]{1,0:T(8,128)(2,1)S(1)}, bf16[16,1024]{1,0:T(8,128)(2,1)S(1)}, u32[]{:S(2)}, u32[]{:S(2)}) collective-permute-start(bf16[16,1024]{1,0:T(8,128)(2,1)S(1)} %get-tuple-element.103), channel_id=1, source_target_pairs={{0,12},{4,0},{8,4},{12,8},{1,13},{5,1},{9,5},{13,9},{2,14},{6,2},{... | collective-permute-start | bytes 98312 | tf_op jit(solution)/shard_map/ppermute | solution.py:13
  114.9 3.9 %collective-permute-start.5 = (bf16[16,1024]{1,0:T(8,128)(2,1)S(1)}, bf16[16,1024]{1,0:T(8,128)(2,1)S(1)}, u32[]{:S(2)}, u32[]{:S(2)}) collective-permute-start(bf16[16,1024]{1,0:T(8,128)(2,1)S(1)} %get-tuple-element.100), channel_id=1, source_target_pairs={{0,12},{4,0},{8,4},{12,8},{1,13},{5,1},{9,5},{13,9},{2,14},{6,2},{... | collective-permute-start | bytes 98312 | tf_op jit(solution)/shard_map/ppermute | solution.py:13
  114.9 7.0 %collective-permute-start.4 = (bf16[16,1024]{1,0:T(8,128)(2,1)S(1)}, bf16[16,1024]{1,0:T(8,128)(2,1)S(1)}, u32[]{:S(2)}, u32[]{:S(2)}) collective-permute-start(bf16[16,1024]{1,0:T(8,128)(2,1)S(1)} %get-tuple-element.101), channel_id=1, source_target_pairs={{0,4},{4,8},{8,12},{12,0},{1,5},{5,9},{9,13},{13,1},{2,6},{6,10},{... | collective-permute-start | bytes 98312 | tf_op jit(solution)/shard_map/ppermute | solution.py:13
where the time goes:
time: 137 us; the launch traced here: 136 us
  blocking collectives  65.9 us (48%)
  matrix products  22.3 us (16%)
  local copies, waits for them, and re-layouts  22.1 us (16%)
  starting transfers between devices  11.4 us (8%)
  other arithmetic  8.41 us (6%)
  waiting for transfers between devices  3.74 us (3%)
  between operations  2.25 us (2%)
    psum x2, blocking collectives, apply_operator(): coarse = lax.psum(scattered, ('sub', 'row'))  37.5 us
    dot_general x16, matrix products, one_tile(): lax.dot_general(vector, piece, (((1,), (1,)), ((), ())), preferred_elemen...  20.7 us
    psum x2, blocking collectives, paired_totals(): lax.psum((inner(residual, precond, half), inner(precond, image, half)), '...  19.2 us
    ppermute x6, starting transfers between devices, shifted(): return lax.ppermute(value, axis, pairs)  11.4 us
    all_gather x2, blocking collectives, apply_operator(): lax.all_gather(united.astype(jnp.bfloat16), 'row', axis=1, tiled=True)  9.15 us
    gather x4, local copies, waits for them, and re-layouts, apply_operator(): jnp.take(arrived_right, right_map, axis=1)  5.95 us
    gather x4, local copies, waits for them, and re-layouts, apply_operator(): result_left = (lower + jnp.take(arrived_left, left_map, axis=1)) * live_left  5.95 us
    gather x1, local copies, waits for them, and re-layouts, per_device(): right_weight = jnp.take(received[1], right_map, axis=1)  4.53 us
  transfers between devices with their start and end apart: 6, of which 2 were waited for; matrix products, arithmetic and copies ran while one was open for 14% of the time, Pallas kernels for 0%

commit v1 on v0

--- a/solution.py
+++ b/solution.py
@@ -1,10 +1,18 @@
 import jax
 import jax.numpy as jnp
 from jax import lax
+from jax.experimental import pallas as pl
+from jax.experimental.pallas import tpu as pltpu
 from jax.sharding import PartitionSpec as P
 
 TILE = 128
+LANES = 128
 ITERS = 2
+F32 = jnp.float32
+BF16 = jnp.bfloat16
+HIGH = lax.Precision.HIGHEST
+VMEM = pl.BlockSpec(memory_space=pltpu.VMEM)
+SMEM = pl.BlockSpec(memory_space=pltpu.SMEM)
 
 
 def shifted(value, axis, steps):
@@ -40,7 +48,7 @@
     return (live_cols + TILE - 1) // TILE
 
 
-def per_device(
+def general(
     loads,
     weights,
     dual_ops,
@@ -127,6 +135,469 @@
     return (solution[:, :half][None], residual[:, :half][None])
 
 
+def cost(flops, moved):
+    return pl.CostEstimate(flops=flops, bytes_accessed=moved, transcendentals=0)
+
+
+def nt(first, second, precision=None):
+    return lax.dot_general(
+        first, second, (((1,), (1,)), ((), ())), preferred_element_type=F32, precision=precision
+    )
+
+
+def nn(first, second, precision=None):
+    return jnp.dot(first, second, preferred_element_type=F32, precision=precision)
+
+
+def halves(value):
+    high = value.astype(BF16)
+    return high, (value - high.astype(F32)).astype(BF16)
+
+
+def stacked(value):
+    return jnp.concatenate(halves(value), axis=0)
+
+
+def folded(value):
+    rows = value.shape[0] // 2
+    return value[:rows] + value[rows:]
+
+
+def thirds(value):
+    high = value.astype(BF16)
+    rest = value - high.astype(F32)
+    middle = rest.astype(BF16)
+    return high, middle, (rest - middle.astype(F32)).astype(BF16)
+
+
+def pieces_sum(ref, rows, half, count):
+    total = ref[rows, half : half + LANES].astype(F32)
+    for piece in range(1, count):
+        at = half + piece * LANES
+        total = total + ref[rows, at : at + LANES].astype(F32)
+    return total
+
+
+def hot_rows(ids_ref, subdomain, extent):
+    ids = ids_ref[pl.ds(subdomain, 1), :]
+    names = lax.broadcasted_iota(jnp.int32, (extent, ids.shape[1]), 0)
+    return (names == ids).astype(F32)
+
+
+def neighbours(sub_ref):
+    subdomain = lax.axis_index("sub")
+    count = lax.axis_size("sub")
+    return lax.rem(subdomain + count - 1, count), subdomain, lax.rem(subdomain + 1, count)
+
+
+def live_row(sizes_ref, interface, half):
+    slots = lax.broadcasted_iota(jnp.int32, (1, half), 1)
+    return slots < sizes_ref[interface]
+
+
+def open_kernel(sizes_ref, loads_ref, weights_ref, maps_ref, first_ref, pack_ref):
+    before, _, _ = neighbours(None)
+    half = loads_ref.shape[1]
+    scale = weights_ref[...]
+    loaded = jnp.where(live_row(sizes_ref, before, half), loads_ref[...], 0.0)
+    first = loaded * scale
+    first_ref[...] = first.astype(BF16)
+    high = scale.astype(BF16).astype(F32)
+    which = lax.broadcasted_iota(jnp.int32, (8, half), 0)
+    spare = jnp.where(which == 0, high, jnp.where(which == 1, scale - high, 0.0))
+    pack_ref[...] = jnp.concatenate([first, maps_ref[...].astype(F32), spare], axis=0).astype(BF16)
+
+
+def select_kernel(right_ref, left_ref, right_hot_ref, left_hot_ref):
+    half = right_ref.shape[1]
+
+    def one(at, carry):
+        start = pl.multiple_of(at * LANES, LANES)
+        names = lax.broadcasted_iota(jnp.int32, (LANES, half), 0) + start
+        rows = pl.ds(start, LANES)
+        right_hot_ref[rows, :] = (names == right_ref[...]).astype(F32).astype(BF16)
+        left_hot_ref[rows, :] = (names == left_ref[...]).astype(F32).astype(BF16)
+        return carry
+
+    lax.fori_loop(0, half // LANES, one, 0)
+
+
+def first_kernel(
+    ids_ref,
+    operator_ref,
+    right_hot_ref,
+    left_hot_ref,
+    first_ref,
+    across_ref,
+    pack_ref,
+    ahead_ref,
+    send_ref,
+    pair_ref,
+    ordered_ref,
+):
+    before, subdomain, after = neighbours(None)
+    lower = lax.axis_index("row") == 0
+    columns, half = first_ref.shape
+    corners = ids_ref.shape[1]
+    left = first_ref[...]
+    right = jnp.where(lower, pack_ref[:columns, :], ahead_ref[...])
+    slotted = nn(right, right_hot_ref[...]).astype(BF16)
+    local = nt(left, operator_ref[:, :half]) + nt(slotted, operator_ref[:, half:])
+    ordered_ref[...] = local.astype(BF16)
+    pair_ref[columns:, :half] = pack_ref[columns:, :]
+
+    @pl.when(jnp.logical_not(lower))
+    def _():
+        ordered_ref[...] = nt(ordered_ref[...], right_hot_ref[...]).astype(BF16)
+        pair_ref[columns:, :half] = nn(pack_ref[columns:, :], left_hot_ref[...]).astype(BF16)
+
+    beside = pair_ref[columns : columns + corners, :half]
+    one = nt(jnp.where(lower, slotted, left), across_ref[...])
+    two = nt(jnp.where(lower, right, left), beside)
+    coarse = nt(one, hot_rows(ids_ref, subdomain, LANES), HIGH) + nt(
+        two, hot_rows(ids_ref, jnp.where(lower, after, before), LANES), HIGH
+    )
+    high, low = halves(coarse)
+    send = jnp.concatenate([ordered_ref[...], high, low], axis=1)
+    send_ref[...] = send
+    pair_ref[:columns, :] = send
+    pair_ref[columns:, half:] = jnp.zeros((pair_ref.shape[0] - columns, 2 * LANES), BF16)
+
+
+def order_kernel(own_ref, across_ref, right_hot_ref, out_ref):
+    lower = lax.axis_index("row") == 0
+    raw = jnp.where(lower, across_ref[...], own_ref[...])
+    out_ref[...] = nt(raw, right_hot_ref[...]).astype(BF16)
+
+
+def second_kernel(
+    sizes_ref,
+    ids_ref,
+    inverse_ref,
+    operator_ref,
+    right_hot_ref,
+    loads_ref,
+    weights_ref,
+    own_map_ref,
+    across_ref,
+    ordered_map_ref,
+    pack_ref,
+    send_ref,
+    kept_ref,
+    pair_ref,
+    along_ref,
+    slant_ref,
+    image_ref,
+    next_ref,
+    up_ref,
+    small_ref,
+    ordered_ref,
+):
+    before, subdomain, after = neighbours(None)
+    lower = lax.axis_index("row") == 0
+    columns, half = loads_ref.shape
+    corners = ids_ref.shape[1]
+    width = inverse_ref.shape[0]
+    everyone = slice(0, columns)
+    top = slice(0, half)
+    own, other = send_ref[:, top].astype(F32), pair_ref[everyone, top].astype(F32)
+    along, slant = along_ref[:, top].astype(F32), slant_ref[:, top].astype(F32)
+    own_c = pieces_sum(send_ref, everyone, half, 2)
+    other_c = pieces_sum(pair_ref, everyone, half, 2)
+    along_c = pieces_sum(along_ref, everyone, half, 2)
+    slant_c = pieces_sum(slant_ref, everyone, half, 2)
+    coarse = (jnp.where(lower, own_c, other_c) + jnp.where(lower, other_c, own_c)) + (
+        jnp.where(lower, along_c, slant_c) + jnp.where(lower, slant_c, along_c)
+    )
+    solved = nn(coarse[:, :width], inverse_ref[...], HIGH)
+    hot_own = hot_rows(ids_ref, subdomain, width)
+    hot_after = hot_rows(ids_ref, after, width)
+    hot_before = hot_rows(ids_ref, before, width)
+    back_own = nn(solved, hot_own, HIGH).astype(BF16)
+    back_after = nn(solved, hot_after, HIGH).astype(BF16)
+    back_before = nn(solved, hot_before, HIGH).astype(BF16)
+    maps = slice(columns, columns + corners)
+    kept, relayed = kept_ref[maps, top], pair_ref[maps, top]
+    left_map = jnp.where(lower, own_map_ref[...], across_ref[...])
+    map_after = jnp.where(lower, kept, relayed)
+    map_before = jnp.where(lower, relayed, kept)
+    fix_left = nn(back_own, left_map) + nn(back_before, map_before)
+    fix_right = nn(back_own, ordered_map_ref[...]) + nn(back_after, map_after)
+    live_left = live_row(sizes_ref, before, half)
+    live_right = live_row(sizes_ref, subdomain, half)
+    image = jnp.where(lower, own, other) + jnp.where(lower, slant, along) + fix_left
+    image = jnp.where(live_left, image, 0.0)
+    image_right = jnp.where(lower, other, own) + jnp.where(lower, along, slant) + fix_right
+    image_right = jnp.where(live_right, image_right, 0.0)
+    scale = weights_ref[...]
+    spare = columns + corners
+    scales = jnp.where(
+        lower,
+        pack_ref[spare : spare + 8, :].astype(F32),
+        pair_ref[spare : spare + 8, top].astype(F32),
+    )
+    left = scale * image
+    right = (scales[0:1] + scales[1:2]) * image_right
+    image_ref[...] = image
+    next_ref[...] = left
+    left_2, right_2 = stacked(left), stacked(right)
+    slotted_2 = nn(right_2, right_hot_ref[...]).astype(BF16)
+    local = folded(nt(left_2, operator_ref[:, :half]) + nt(slotted_2, operator_ref[:, half:]))
+    block = folded(jnp.where(lower, left_2, slotted_2).astype(F32))
+    energy = jnp.sum(block * local, axis=1, keepdims=True)
+    ordered_ref[...] = local.astype(BF16)
+
+    @pl.when(jnp.logical_not(lower))
+    def _():
+        ordered_ref[...] = nt(ordered_ref[...], right_hot_ref[...]).astype(BF16)
+
+    one = folded(nt(jnp.where(lower, slotted_2, left_2), across_ref[...]))
+    two = folded(nt(jnp.where(lower, right_2, left_2), kept))
+    coarse = nt(one, hot_rows(ids_ref, subdomain, LANES), HIGH) + nt(
+        two, hot_rows(ids_ref, jnp.where(lower, after, before), LANES), HIGH
+    )
+    loaded = jnp.where(live_left, loads_ref[...], 0.0)
+    first = loaded * scale
+    sums = (
+        jnp.sum(loaded * first, axis=1, keepdims=True),
+        jnp.sum(first * image, axis=1, keepdims=True),
+        jnp.sum(image * left, axis=1, keepdims=True),
+        energy,
+    )
+    lane = lax.broadcasted_iota(jnp.int32, (columns, LANES), 1)
+    small = jnp.where(lane < width, coarse, 0.0)
+    for at, value in enumerate(sums):
+        small = jnp.where(lane == width + at, value, small)
+    small_ref[...] = small
+    up_ref[...] = jnp.concatenate([ordered_ref[...], *thirds(small)], axis=1)
+
+
+def relay_kernel(up_own_ref, up_ref, down_ref, far_ref, own_ref, out_ref):
+    lower = lax.axis_index("row") == 0
+    columns = up_ref.shape[0]
+    half = up_ref.shape[1] - 3 * LANES
+    total = own_ref[...] + pieces_sum(up_ref, slice(0, columns), half, 3)
+    total = total + down_ref[...] + far_ref[...]
+    bulk = jnp.where(lower, up_own_ref[:, :half], up_ref[:, :half])
+    out_ref[...] = jnp.concatenate([bulk, *thirds(total)], axis=1)
+
+
+def close_kernel(
+    sizes_ref,
+    ids_ref,
+    inverse_ref,
+    loads_ref,
+    weights_ref,
+    own_map_ref,
+    across_ref,
+    kept_ref,
+    pair_ref,
+    image_ref,
+    next_ref,
+    mine_ref,
+    theirs_ref,
+    solution_ref,
+    residual_ref,
+):
+    before, subdomain, _ = neighbours(None)
+    lower = lax.axis_index("row") == 0
+    columns, half = loads_ref.shape
+    corners = ids_ref.shape[1]
+    width = inverse_ref.shape[0]
+    everyone = slice(0, columns)
+    top = slice(0, half)
+    mine = pieces_sum(mine_ref, everyone, half, 3)
+    theirs = pieces_sum(theirs_ref, everyone, half, 3)
+    total = jnp.where(lower, mine, theirs)
+    rest = jnp.where(lower, theirs, mine)
+    coarse = total[:, :width]
+    solved = nn(coarse, inverse_ref[...], HIGH)
+    back_own = nn(solved, hot_rows(ids_ref, subdomain, width), HIGH).astype(BF16)
+    back_before = nn(solved, hot_rows(ids_ref, before, width), HIGH).astype(BF16)
+    maps = slice(columns, columns + corners)
+    left_map = jnp.where(lower, own_map_ref[...], across_ref[...])
+    map_before = jnp.where(lower, pair_ref[maps, top], kept_ref[maps, top])
+    fix = nn(back_own, left_map) + nn(back_before, map_before)
+    image_next = mine_ref[:, top].astype(F32) + theirs_ref[:, top].astype(F32) + fix
+    live = live_row(sizes_ref, before, half)
+    image_next = jnp.where(live, image_next, 0.0)
+    lane = lax.broadcasted_iota(jnp.int32, (columns, LANES), 1)
+
+    def column(values, at):
+        return jnp.sum(jnp.where(lane == width + at, values, 0.0), axis=1, keepdims=True)
+
+    gamma = column(total, 0)
+    delta = column(total, 1)
+    cross = column(total, 2)
+    energy = column(total, 3) + column(rest, 3) + jnp.sum(coarse * solved, axis=1, keepdims=True)
+    alpha = gamma / delta
+    gamma_next = gamma - 2.0 * alpha * delta + alpha * alpha * cross
+    ratio = gamma_next / gamma
+    grown = 1.0 + ratio
+    curvature = grown * grown * delta - 2.0 * grown * alpha * cross + alpha * alpha * energy
+    alpha_next = gamma_next / curvature
+    loaded = jnp.where(live, loads_ref[...], 0.0)
+    first = loaded * weights_ref[...]
+    direction = grown * first - alpha * next_ref[...]
+    along = grown * image_ref[...] - alpha * image_next
+    solution_ref[...] = alpha * first + alpha_next * direction
+    residual_ref[...] = loaded - alpha * image_ref[...] - alpha_next * along
+
+
+def ring(
+    loads,
+    weights,
+    dual_ops,
+    corner_maps,
+    coarse_inverse,
+    corner_ids,
+    iface_sizes,
+    left_partner,
+    right_partner,
+):
+    count = lax.axis_size("sub")
+    sides = lax.axis_size("row")
+    columns, half = loads.shape[1:]
+    corners = corner_maps.shape[1]
+    operator = dual_ops[0]
+    own_map = corner_maps[0]
+    loaded = loads[0]
+    block = operator.shape[0]
+    shape = jax.ShapeDtypeStruct
+    grid = ("sub", "row")
+    big = 2 * columns * block * 2 * half
+
+    def pairs(target):
+        listed = []
+        for at in range(count):
+            for side in range(sides):
+                to_at, to_side = target(at, side)
+                listed.append((at * sides + side, (to_at % count) * sides + to_side))
+        return listed
+
+    across = pairs(lambda at, side: (at, 1 - side))
+    along = pairs(lambda at, side: (at - 1, 0) if side == 0 else (at + 1, 1))
+    slant = pairs(lambda at, side: (at - 1, 1) if side == 0 else (at + 1, 0))
+
+    def call(kernel, specs, outs, scratch=(), flops=0, moved=0):
+        return pl.pallas_call(
+            kernel,
+            in_specs=specs,
+            out_specs=[VMEM] * len(outs),
+            out_shape=outs,
+            scratch_shapes=scratch,
+            cost_estimate=cost(flops, moved),
+        )
+
+    rows = columns + corners + 8
+    first, pack = call(
+        open_kernel,
+        [SMEM, VMEM, VMEM, VMEM],
+        [shape((columns, half), BF16), shape((rows, half), BF16)],
+        moved=4 * rows * half,
+    )(iface_sizes, loaded, weights, own_map)
+    other_map = lax.ppermute(own_map, grid, across)
+    pack_in = lax.ppermute(pack, grid, along)
+    ahead = lax.ppermute(first, grid, slant)
+    right_hot, left_hot = call(
+        select_kernel,
+        [VMEM, VMEM],
+        [shape((half, half), BF16), shape((half, half), BF16)],
+        flops=4 * half * half,
+        moved=4 * half * half,
+    )(right_partner, left_partner)
+    send, kept = call(
+        first_kernel,
+        [VMEM] * 8,
+        [shape((columns, half + 2 * LANES), BF16), shape((rows, half + 2 * LANES), BF16)],
+        scratch=[pltpu.VMEM((columns, block), BF16)],
+        flops=2 * big,
+        moved=4 * block * half,
+    )(corner_ids, operator, right_hot, left_hot, first, other_map, pack_in, ahead)
+    pair_in = lax.ppermute(kept, grid, across)
+    along_in = lax.ppermute(send, grid, along)
+    slant_in = lax.ppermute(send, grid, slant)
+    (ordered_map,) = call(
+        order_kernel,
+        [VMEM] * 3,
+        [shape((corners, half), BF16)],
+        flops=2 * corners * half * half,
+        moved=2 * half * half,
+    )(own_map, other_map, right_hot)
+    image, following, up, small = call(
+        second_kernel,
+        [SMEM] + [VMEM] * 15,
+        [
+            shape((columns, half), F32),
+            shape((columns, half), F32),
+            shape((columns, half + 3 * LANES), BF16),
+            shape((columns, LANES), F32),
+        ],
+        scratch=[pltpu.VMEM((columns, block), BF16)],
+        flops=2 * big,
+        moved=4 * block * half,
+    )(
+        iface_sizes,
+        corner_ids,
+        coarse_inverse,
+        operator,
+        right_hot,
+        loaded,
+        weights,
+        own_map,
+        other_map,
+        ordered_map,
+        pack_in,
+        send,
+        kept,
+        pair_in,
+        along_in,
+        slant_in,
+    )
+    up_in = shifted(up, "sub", 1)
+    down_in = shifted(small, "sub", -1)
+    far_in = shifted(small, "sub", 2)
+    (mine,) = call(
+        relay_kernel,
+        [VMEM] * 5,
+        [shape((columns, half + 3 * LANES), BF16)],
+        moved=8 * columns * half,
+    )(up, up_in, down_in, far_in, small)
+    theirs = lax.ppermute(mine, grid, across)
+    solution, residual = call(
+        close_kernel,
+        [SMEM] + [VMEM] * 12,
+        [shape((columns, half), F32), shape((columns, half), F32)],
+        moved=24 * columns * half,
+    )(
+        iface_sizes,
+        corner_ids,
+        coarse_inverse,
+        loaded,
+        weights,
+        own_map,
+        other_map,
+        kept,
+        pair_in,
+        image,
+        following,
+        mine,
+        theirs,
+    )
+    return solution[None], residual[None]
+
+
+def per_device(*arrays):
+    loads, _, dual_ops, _, coarse_inverse = arrays[:5]
+    half = loads.shape[2]
+    neighbourly = lax.axis_size("sub") == 4 and lax.axis_size("row") == 2
+    sided = dual_ops.shape[1] == half and half % LANES == 0
+    narrow = coarse_inverse.shape[0] + 4 <= LANES
+    if neighbourly and sided and narrow and ITERS == 2:
+        return ring(*arrays)
+    return general(*arrays)
+
+
 def solution(mesh):
     placed = (
         P(("parts", "sub"), "col", None),

time: 137 us -> 53 us (0.39)
  blocking collectives: 65.9 us -> 0 us
  Pallas kernels: 0 us -> 24.1 us
  matrix products: 22.3 us -> 0 us
  local copies, waits for them, and re-layouts: 22.1 us -> 3.74 us
  other arithmetic: 8.41 us -> 0 us
  waiting for transfers between devices: 3.74 us -> 8.37 us
  starting transfers between devices: 11.4 us -> 15.8 us
  between operations: 2.25 us -> 0.68 us
    psum x4 -> x0, blocking collectives: 56.7 us -> none  [the longest x2 37.5 us: apply_operator(): coarse = lax.psum(scattered, ('sub', 'row'))]
    pallas_call x0 -> x7, Pallas kernels: none -> 24.1 us  [the longest x1 6.39 us: ring(): call(second_kernel, [SMEM] + [VMEM] * 15, [shape((columns, half), F32), s...]
    dot_general x26 -> x0, matrix products: 22.3 us -> none  [the longest x16 20.7 us: one_tile(): lax.dot_general(vector, piece, (((1,), (1,)), ((), ())), preferred_elemen...]
    gather x11 -> x0, local copies, waits for them, and re-layouts: 19.4 us -> none  [the longest x4 5.95 us: apply_operator(): jnp.take(arrived_right, right_map, axis=1)]
    ppermute x0 -> x7, starting transfers between devices: none -> 12 us  [the longest x1 5.08 us: ring(): pack_in = lax.ppermute(pack, grid, along)]
    all_gather x2 -> x0, blocking collectives: 9.15 us -> none  [apply_operator(): lax.all_gather(united.astype(jnp.bfloat16), 'row', axis=1, tiled=True)]
    ppermute x6 -> x3, starting transfers between devices: 11.4 us -> 3.82 us  [shifted(): return lax.ppermute(value, axis, pairs)]
    ppermute x0 -> x7, waiting for transfers between devices: none -> 5.94 us  [the longest x1 2.7 us: ring(): theirs = lax.ppermute(mine, grid, across)]
  transfers between devices with their start and end apart: 6 -> 10, of which waited for: 2 -> 5; matrix products, arithmetic and copies ran while one was open for 14% -> 0% of each run, Pallas kernels for 0% -> 12%
where the time goes in v1:
time: 53 us; the launch traced here: 52.7 us
  Pallas kernels  24.1 us (45%)
  starting transfers between devices  15.8 us (30%)
  waiting for transfers between devices  8.37 us (16%)
  local copies, waits for them, and re-layouts  3.74 us (7%)
  between operations  0.68 us (1%)
    pallas_call x1, Pallas kernels, ring(): call(second_kernel, [SMEM] + [VMEM] * 15, [shape((columns, half), F32), s...  6.39 us
    pallas_call x1, Pallas kernels, ring(): call(first_kernel, [VMEM] * 8, [shape((columns, half + 2 * LANES), BF16),...  6.12 us
    ppermute x1, starting transfers between devices, ring(): pack_in = lax.ppermute(pack, grid, along)  5.08 us
    ppermute x3, starting transfers between devices, shifted(): return lax.ppermute(value, axis, pairs)  3.82 us
    unnamed x20, local copies, waits for them, and re-layouts  3.74 us
    pallas_call x1, Pallas kernels, ring(): call(select_kernel, [VMEM, VMEM], [shape((half, half), BF16), shape((half...  3.35 us
    pallas_call x1, Pallas kernels, ring(): call(order_kernel, [VMEM] * 3, [shape((corners, half), BF16)], flops=2 *...  3 us
    ppermute x1, waiting for transfers between devices, ring(): theirs = lax.ppermute(mine, grid, across)  2.7 us
  transfers between devices with their start and end apart: 10, of which 5 were waited for; matrix products, arithmetic and copies ran while one was open for 0% of the time, Pallas kernels for 12%

profile of v1, /device:TPU:0, one launch (start us, length us, event | category | flops | bytes accessed | tf_op | source)
XLA Modules:
  0.0 52.7 jit_solution(471644693083630427)
XLA Ops:
  0.6 1.5 %shard_map.105 = (bf16[16,1024]{1,0:T(8,128)(2,1)}, bf16[48,1024]{1,0:T(8,128)(2,1)}) custom-call(s32[4]{0:T(128)} %sizes_ref.5, f32[16,1024]{1,0:T(8,128)} %bitcast.12, f32[1,1024]{1,0:T(1,128)} %weights_ref.5, bf16[24,1024]{1,0:T(8,128)(2,1)} %bitcast.7), custom_call_target="tpu_custom_call" | custom-call | bytes 196608 | tf_op jit(solution)/shard_map/pallas_call | solution.py:493
  2.2 5.1 %collective-permute-start.1 = (bf16[48,1024]{1,0:T(8,128)(2,1)}, bf16[48,1024]{1,0:T(8,128)(2,1)S(1)}, u32[]{:S(2)}, u32[]{:S(2)}) collective-permute-start(bf16[48,1024]{1,0:T(8,128)(2,1)} %get-tuple-element.17), channel_id=1, source_target_pairs={{0,12},{2,6},{4,0},{6,10},{8,4},{10,14},{12,8},{14,2},{1,13},{3,7}... | collective-permute-start | bytes 294920 | tf_op jit(solution)/shard_map/ppermute | solution.py:500
  7.3 0.0 collective-permute-start
  7.3 1.9 %collective-permute-start.2 = (bf16[16,1024]{1,0:T(8,128)(2,1)}, bf16[16,1024]{1,0:T(8,128)(2,1)S(1)}, u32[]{:S(2)}, u32[]{:S(2)}) collective-permute-start(bf16[16,1024]{1,0:T(8,128)(2,1)} %get-tuple-element.16.first_ref), channel_id=1, source_target_pairs={{0,14},{2,4},{4,2},{6,8},{8,6},{10,12},{12,10},{14,0},{1,15},{3,5}... | collective-permute-start | bytes 98312 | tf_op jit(solution)/shard_map/ppermute | solution.py:501
  9.2 3.3 %shard_map.104 = (bf16[1024,1024]{1,0:T(8,128)(2,1)}, bf16[1024,1024]{1,0:T(8,128)(2,1)}) custom-call(s32[1,1024]{1,0:T(1,128)} %right_ref.1, s32[1,1024]{1,0:T(1,128)} %left_ref.1), custom_call_target="tpu_custom_call" | custom-call | flops 4194304 | bytes 4194304 | tf_op jit(solution)/shard_map/pallas_call | solution.py:502
  12.5 1.6 %collective-permute-done.2.ahead_ref = bf16[16,1024]{1,0:T(8,128)(2,1)S(1)} collective-permute-done((bf16[16,1024]{1,0:T(8,128)(2,1)}, bf16[16,1024]{1,0:T(8,128)(2,1)S(1)}, u32[]{:S(2)}, u32[]{:S(2)}) %collective-permute-start.2) | collective-permute-done | bytes 32800 | tf_op jit(solution)/shard_map/ppermute | solution.py:501
  14.1 0.0 copy-start.7
  14.1 0.0 collective-permute-done.across_ref
  14.1 0.0 copy-start
  14.1 0.0 collective-permute-done.1.pack_ref
  14.1 0.0 copy-start.2
  14.1 0.6 %copy-done.7 = bf16[16,1024]{1,0:T(8,128)(2,1)} copy-done((bf16[16,1024]{1,0:T(8,128)(2,1)}, bf16[16,1024]{1,0:T(8,128)(2,1)S(1)}, u32[]{:S(2)}) %copy-start.7) | copy-done | bytes 32792
  14.7 0.0 copy-done
  14.7 0.1 copy-done.2
  14.8 6.1 %shard_map.106 = (bf16[16,1280]{1,0:T(8,128)(2,1)}, bf16[48,1280]{1,0:T(8,128)(2,1)}) custom-call(s32[4,24]{1,0:T(4,128)} %ids_ref.5, bf16[1024,2048]{1,0:T(8,128)(2,1)} %bitcast.5, bf16[1024,1024]{1,0:T(8,128)(2,1)} %get-tuple-element.14.right_hot_ref, bf16[1024,1024]{1,0:T(8,128)(2,1)} %get-tuple-element.15.left_hot_ref, ...), custom_call_target="tpu_custom_call" | custom-call | flops 134217728 | bytes 4194304 | tf_op jit(solution)/shard_map/pallas_call | solution.py:509
  20.9 1.2 %collective-permute-start.3 = (bf16[48,1280]{1,0:T(8,128)(2,1)}, bf16[48,1280]{1,0:T(8,128)(2,1)S(1)}, u32[]{:S(2)}, u32[]{:S(2)}) collective-permute-start(bf16[48,1280]{1,0:T(8,128)(2,1)} %get-tuple-element.18.kept_ref), channel_id=1, source_target_pairs={{0,2},{2,0},{4,6},{6,4},{8,10},{10,8},{12,14},{14,12},{1,3},{3,1},... | collective-permute-start | bytes 368648 | tf_op jit(solution)/shard_map/ppermute | solution.py:517
  22.1 1.7 %collective-permute-start.5 = (bf16[16,1280]{1,0:T(8,128)(2,1)}, bf16[16,1280]{1,0:T(8,128)(2,1)S(1)}, u32[]{:S(2)}, u32[]{:S(2)}) collective-permute-start(bf16[16,1280]{1,0:T(8,128)(2,1)} %get-tuple-element.19.send_ref), channel_id=1, source_target_pairs={{0,14},{2,4},{4,2},{6,8},{8,6},{10,12},{12,10},{14,0},{1,15},{3,5}... | collective-permute-start | bytes 122888 | tf_op jit(solution)/shard_map/ppermute | solution.py:519
  23.8 0.6 %collective-permute-start.4 = (bf16[16,1280]{1,0:T(8,128)(2,1)}, bf16[16,1280]{1,0:T(8,128)(2,1)S(1)}, u32[]{:S(2)}, u32[]{:S(2)}) collective-permute-start(bf16[16,1280]{1,0:T(8,128)(2,1)} %get-tuple-element.19.send_ref), channel_id=1, source_target_pairs={{0,12},{2,6},{4,0},{6,10},{8,4},{10,14},{12,8},{14,2},{1,13},{3,7}... | collective-permute-start | bytes 122888 | tf_op jit(solution)/shard_map/ppermute | solution.py:518
  24.3 3.0 %shard_map.107.ordered_map_ref = bf16[24,1024]{1,0:T(8,128)(2,1)} custom-call(bf16[24,1024]{1,0:T(8,128)(2,1)} %bitcast.9, bf16[24,1024]{1,0:T(8,128)(2,1)} %copy-done, bf16[1024,1024]{1,0:T(8,128)(2,1)} %get-tuple-element.14.right_hot_ref), custom_call_target="tpu_custom_call" | custom-call | flops 50331648 | bytes 2097152 | tf_op jit(solution)/shard_map/pallas_call | solution.py:520
  27.3 1.7 %collective-permute-done.5.slant_ref = bf16[16,1280]{1,0:T(8,128)(2,1)S(1)} collective-permute-done((bf16[16,1280]{1,0:T(8,128)(2,1)}, bf16[16,1280]{1,0:T(8,128)(2,1)S(1)}, u32[]{:S(2)}, u32[]{:S(2)}) %collective-permute-start.5) | collective-permute-done | bytes 40992 | tf_op jit(solution)/shard_map/ppermute | solution.py:519
  29.0 0.0 copy-start.5
  29.0 0.0 collective-permute-done.4.along_ref
  29.0 0.0 copy-start.6
  29.0 0.0 collective-permute-done.3.pair_ref
  29.0 0.6 %copy-done.5 = bf16[16,1280]{1,0:T(8,128)(2,1)} copy-done((bf16[16,1280]{1,0:T(8,128)(2,1)}, bf16[16,1280]{1,0:T(8,128)(2,1)S(1)}, u32[]{:S(2)}) %copy-start.5) | copy-done | bytes 40984
  29.6 0.0 copy-done.6
  29.6 0.0 copy-start.1
  29.6 0.6 %copy-done.1 = bf16[48,1280]{1,0:T(8,128)(2,1)} copy-done((bf16[48,1280]{1,0:T(8,128)(2,1)}, bf16[48,1280]{1,0:T(8,128)(2,1)S(1)}, u32[]{:S(2)}) %copy-start.1) | copy-done | bytes 122904
  30.3 6.4 %shard_map.108 = (f32[16,1024]{1,0:T(8,128)}, f32[16,1024]{1,0:T(8,128)}, bf16[16,1408]{1,0:T(8,128)(2,1)}, f32[16,128]{1,0:T(8,128)}) custom-call(s32[4]{0:T(128)} %sizes_ref.5, s32[4,24]{1,0:T(4,128)} %ids_ref.5, f32[48,48]{1,0:T(8,128)} %inverse_ref.3, bf16[1024,2048]{1,0:T(8,128)(2,1)} %bitcast.6, bf16[1024,1024]{1,0:T(8,128)(2,1)} %get-tuple-element.14.right_hot_ref, ...), custom_call_target="tpu_custom_call" | custom-call | flops 134217728 | bytes 4194304 | tf_op jit(solution)/shard_map/pallas_call | solution.py:527
  36.7 0.0 collective-permute-start.6
  36.7 1.9 %collective-permute-start.8 = (f32[16,128]{1,0:T(8,128)}, f32[16,128]{1,0:T(8,128)S(1)}, u32[]{:S(2)}, u32[]{:S(2)}) collective-permute-start(f32[16,128]{1,0:T(8,128)} %get-tuple-element.23.own_ref), channel_id=1, source_target_pairs={{0,8},{4,12},{8,0},{12,4},{1,9},{5,13},{9,1},{13,5},{2,10},{6,14},... | collective-permute-start | bytes 24584 | tf_op jit(solution)/shard_map/ppermute | solution.py:21
  38.6 1.9 %collective-permute-start.7 = (f32[16,128]{1,0:T(8,128)}, f32[16,128]{1,0:T(8,128)S(1)}, u32[]{:S(2)}, u32[]{:S(2)}) collective-permute-start(f32[16,128]{1,0:T(8,128)} %get-tuple-element.23.own_ref), channel_id=1, source_target_pairs={{0,12},{4,0},{8,4},{12,8},{1,13},{5,1},{9,5},{13,9},{2,14},{6,2},{... | collective-permute-start | bytes 24584 | tf_op jit(solution)/shard_map/ppermute | solution.py:21
  40.5 1.0 %collective-permute-done.8.far_ref = f32[16,128]{1,0:T(8,128)S(1)} collective-permute-done((f32[16,128]{1,0:T(8,128)}, f32[16,128]{1,0:T(8,128)S(1)}, u32[]{:S(2)}, u32[]{:S(2)}) %collective-permute-start.8) | collective-permute-done | bytes 8224 | tf_op jit(solution)/shard_map/ppermute | solution.py:21
  41.5 0.0 copy-start.8
  41.5 1.4 %collective-permute-done.7.down_ref = f32[16,128]{1,0:T(8,128)S(1)} collective-permute-done((f32[16,128]{1,0:T(8,128)}, f32[16,128]{1,0:T(8,128)S(1)}, u32[]{:S(2)}, u32[]{:S(2)}) %collective-permute-start.7) | collective-permute-done | bytes 8224 | tf_op jit(solution)/shard_map/ppermute | solution.py:21
  42.9 0.0 copy-start.9
  42.9 0.0 collective-permute-done.6.up_ref
  42.9 0.0 copy-done.8
  42.9 0.6 %copy-done.9 = f32[16,128]{1,0:T(8,128)} copy-done((f32[16,128]{1,0:T(8,128)}, f32[16,128]{1,0:T(8,128)S(1)}, u32[]{:S(2)}) %copy-start.9) | copy-done | bytes 8216
  43.5 0.0 copy-start.3
  43.5 0.6 %copy-done.3 = bf16[16,1408]{1,0:T(8,128)(2,1)} copy-done((bf16[16,1408]{1,0:T(8,128)(2,1)}, bf16[16,1408]{1,0:T(8,128)(2,1)S(1)}, u32[]{:S(2)}) %copy-start.3) | copy-done | bytes 45080
  44.2 1.5 %shard_map.109.mine_ref = bf16[16,1408]{1,0:T(8,128)(2,1)} custom-call(bf16[16,1408]{1,0:T(8,128)(2,1)} %get-tuple-element.22.up_own_ref, bf16[16,1408]{1,0:T(8,128)(2,1)} %copy-done.3, f32[16,128]{1,0:T(8,128)} %copy-done.9, f32[16,128]{1,0:T(8,128)} %copy-done.8, f32[16,128]{1,0:T(8,128)} %get-tuple-element.23.own_ref), custom_call_target="tpu_custom_call" | custom-call | bytes 131072 | tf_op jit(solution)/shard_map/pallas_call | solution.py:560
  45.6 1.6 %collective-permute-start.9 = (bf16[16,1408]{1,0:T(8,128)(2,1)}, bf16[16,1408]{1,0:T(8,128)(2,1)S(1)}, u32[]{:S(2)}, u32[]{:S(2)}) collective-permute-start(bf16[16,1408]{1,0:T(8,128)(2,1)} %shard_map.109.mine_ref), channel_id=1, source_target_pairs={{0,2},{2,0},{4,6},{6,4},{8,10},{10,8},{12,14},{14,12},{1,3},{3,1},... | collective-permute-start | bytes 135176 | tf_op jit(solution)/shard_map/ppermute | solution.py:566
  47.2 2.7 %collective-permute-done.9.theirs_ref = bf16[16,1408]{1,0:T(8,128)(2,1)S(1)} collective-permute-done((bf16[16,1408]{1,0:T(8,128)(2,1)}, bf16[16,1408]{1,0:T(8,128)(2,1)S(1)}, u32[]{:S(2)}, u32[]{:S(2)}) %collective-permute-start.9) | collective-permute-done | bytes 45088 | tf_op jit(solution)/shard_map/ppermute | solution.py:566
  49.9 0.0 copy-start.4
  49.9 0.6 %copy-done.4 = bf16[16,1408]{1,0:T(8,128)(2,1)} copy-done((bf16[16,1408]{1,0:T(8,128)(2,1)}, bf16[16,1408]{1,0:T(8,128)(2,1)S(1)}, u32[]{:S(2)}) %copy-start.4) | copy-done | bytes 45080
  50.5 2.3 %shard_map.110 = (f32[16,1024]{1,0:T(8,128)}, f32[16,1024]{1,0:T(8,128)}) custom-call(s32[4]{0:T(128)} %sizes_ref.5, s32[4,24]{1,0:T(4,128)} %ids_ref.5, f32[48,48]{1,0:T(8,128)} %inverse_ref.3, f32[16,1024]{1,0:T(8,128)} %bitcast.14, f32[1,1024]{1,0:T(1,128)} %weights_ref.5, bf16[24,1024]{1,0:T(8,128)(2,1)} %bitcast.11, bf16[24,1024]{1,0:T(8,128)(2,1)} %copy-done, ...), custom_call_target="tpu_custom_call" | custom-call | bytes 393216 | tf_op jit(solution)/shard_map/pallas_call | solution.py:567
Async XLA Ops:
  2.2 11.9 %collective-permute-start.1 = (bf16[48,1024]{1,0:T(8,128)(2,1)}, bf16[48,1024]{1,0:T(8,128)(2,1)S(1)}, u32[]{:S(2)}, u32[]{:S(2)}) collective-permute-start(bf16[48,1024]{1,0:T(8,128)(2,1)} %get-tuple-element.17), channel_id=1, source_target_pairs={{0,12},{2,6},{4,0},{6,10},{8,4},{10,14},{12,8},{14,2},{1,13},{3,7}... | collective-permute-start | bytes 294920 | tf_op jit(solution)/shard_map/ppermute | solution.py:500
  7.3 6.8 %collective-permute-start = (bf16[24,1024]{1,0:T(8,128)(2,1)}, bf16[24,1024]{1,0:T(8,128)(2,1)S(1)}, u32[]{:S(2)}, u32[]{:S(2)}) collective-permute-start(bf16[24,1024]{1,0:T(8,128)(2,1)} %bitcast.8), channel_id=1, source_target_pairs={{0,2},{2,0},{4,6},{6,4},{8,10},{10,8},{12,14},{14,12},{1,3},{3,1},... | collective-permute-start | bytes 147464 | tf_op jit(solution)/shard_map/ppermute | solution.py:499
  7.3 6.8 %collective-permute-start.2 = (bf16[16,1024]{1,0:T(8,128)(2,1)}, bf16[16,1024]{1,0:T(8,128)(2,1)S(1)}, u32[]{:S(2)}, u32[]{:S(2)}) collective-permute-start(bf16[16,1024]{1,0:T(8,128)(2,1)} %get-tuple-element.16.first_ref), channel_id=1, source_target_pairs={{0,14},{2,4},{4,2},{6,8},{8,6},{10,12},{12,10},{14,0},{1,15},{3,5}... | collective-permute-start | bytes 98312 | tf_op jit(solution)/shard_map/ppermute | solution.py:501
  14.1 0.6 %copy-start.7 = (bf16[16,1024]{1,0:T(8,128)(2,1)}, bf16[16,1024]{1,0:T(8,128)(2,1)S(1)}, u32[]{:S(2)}) copy-start(bf16[16,1024]{1,0:T(8,128)(2,1)S(1)} %collective-permute-done.2.ahead_ref) | copy-start | bytes 98308
  14.1 0.6 %copy-start = (bf16[24,1024]{1,0:T(8,128)(2,1)}, bf16[24,1024]{1,0:T(8,128)(2,1)S(1)}, u32[]{:S(2)}) copy-start(bf16[24,1024]{1,0:T(8,128)(2,1)S(1)} %collective-permute-done.across_ref) | copy-start | bytes 147460
  14.1 0.7 %copy-start.2 = (bf16[48,1024]{1,0:T(8,128)(2,1)}, bf16[48,1024]{1,0:T(8,128)(2,1)S(1)}, u32[]{:S(2)}) copy-start(bf16[48,1024]{1,0:T(8,128)(2,1)S(1)} %collective-permute-done.1.pack_ref) | copy-start | bytes 294916
  20.9 8.1 %collective-permute-start.3 = (bf16[48,1280]{1,0:T(8,128)(2,1)}, bf16[48,1280]{1,0:T(8,128)(2,1)S(1)}, u32[]{:S(2)}, u32[]{:S(2)}) collective-permute-start(bf16[48,1280]{1,0:T(8,128)(2,1)} %get-tuple-element.18.kept_ref), channel_id=1, source_target_pairs={{0,2},{2,0},{4,6},{6,4},{8,10},{10,8},{12,14},{14,12},{1,3},{3,1},... | collective-permute-start | bytes 368648 | tf_op jit(solution)/shard_map/ppermute | solution.py:517
  22.1 6.9 %collective-permute-start.5 = (bf16[16,1280]{1,0:T(8,128)(2,1)}, bf16[16,1280]{1,0:T(8,128)(2,1)S(1)}, u32[]{:S(2)}, u32[]{:S(2)}) collective-permute-start(bf16[16,1280]{1,0:T(8,128)(2,1)} %get-tuple-element.19.send_ref), channel_id=1, source_target_pairs={{0,14},{2,4},{4,2},{6,8},{8,6},{10,12},{12,10},{14,0},{1,15},{3,5}... | collective-permute-start | bytes 122888 | tf_op jit(solution)/shard_map/ppermute | solution.py:519
  23.8 5.2 %collective-permute-start.4 = (bf16[16,1280]{1,0:T(8,128)(2,1)}, bf16[16,1280]{1,0:T(8,128)(2,1)S(1)}, u32[]{:S(2)}, u32[]{:S(2)}) collective-permute-start(bf16[16,1280]{1,0:T(8,128)(2,1)} %get-tuple-element.19.send_ref), channel_id=1, source_target_pairs={{0,12},{2,6},{4,0},{6,10},{8,4},{10,14},{12,8},{14,2},{1,13},{3,7}... | collective-permute-start | bytes 122888 | tf_op jit(solution)/shard_map/ppermute | solution.py:518
  29.0 0.6 %copy-start.5 = (bf16[16,1280]{1,0:T(8,128)(2,1)}, bf16[16,1280]{1,0:T(8,128)(2,1)S(1)}, u32[]{:S(2)}) copy-start(bf16[16,1280]{1,0:T(8,128)(2,1)S(1)} %collective-permute-done.5.slant_ref) | copy-start | bytes 122884
  29.0 0.6 %copy-start.6 = (bf16[16,1280]{1,0:T(8,128)(2,1)}, bf16[16,1280]{1,0:T(8,128)(2,1)S(1)}, u32[]{:S(2)}) copy-start(bf16[16,1280]{1,0:T(8,128)(2,1)S(1)} %collective-permute-done.4.along_ref) | copy-start | bytes 122884
  29.6 0.6 %copy-start.1 = (bf16[48,1280]{1,0:T(8,128)(2,1)}, bf16[48,1280]{1,0:T(8,128)(2,1)S(1)}, u32[]{:S(2)}) copy-start(bf16[48,1280]{1,0:T(8,128)(2,1)S(1)} %collective-permute-done.3.pair_ref) | copy-start | bytes 368644
  36.7 6.3 %collective-permute-start.6 = (bf16[16,1408]{1,0:T(8,128)(2,1)}, bf16[16,1408]{1,0:T(8,128)(2,1)S(1)}, u32[]{:S(2)}, u32[]{:S(2)}) collective-permute-start(bf16[16,1408]{1,0:T(8,128)(2,1)} %get-tuple-element.22.up_own_ref), channel_id=1, source_target_pairs={{0,4},{4,8},{8,12},{12,0},{1,5},{5,9},{9,13},{13,1},{2,6},{6,10},{... | collective-permute-start | bytes 135176 | tf_op jit(solution)/shard_map/ppermute | solution.py:21
  36.7 4.8 %collective-permute-start.8 = (f32[16,128]{1,0:T(8,128)}, f32[16,128]{1,0:T(8,128)S(1)}, u32[]{:S(2)}, u32[]{:S(2)}) collective-permute-start(f32[16,128]{1,0:T(8,128)} %get-tuple-element.23.own_ref), channel_id=1, source_target_pairs={{0,8},{4,12},{8,0},{12,4},{1,9},{5,13},{9,1},{13,5},{2,10},{6,14},... | collective-permute-start | bytes 24584 | tf_op jit(solution)/shard_map/ppermute | solution.py:21
  38.6 4.4 %collective-permute-start.7 = (f32[16,128]{1,0:T(8,128)}, f32[16,128]{1,0:T(8,128)S(1)}, u32[]{:S(2)}, u32[]{:S(2)}) collective-permute-start(f32[16,128]{1,0:T(8,128)} %get-tuple-element.23.own_ref), channel_id=1, source_target_pairs={{0,12},{4,0},{8,4},{12,8},{1,13},{5,1},{9,5},{13,9},{2,14},{6,2},{... | collective-permute-start | bytes 24584 | tf_op jit(solution)/shard_map/ppermute | solution.py:21
  41.5 1.4 %copy-start.8 = (f32[16,128]{1,0:T(8,128)}, f32[16,128]{1,0:T(8,128)S(1)}, u32[]{:S(2)}) copy-start(f32[16,128]{1,0:T(8,128)S(1)} %collective-permute-done.8.far_ref) | copy-start | bytes 24580
  42.9 0.6 %copy-start.9 = (f32[16,128]{1,0:T(8,128)}, f32[16,128]{1,0:T(8,128)S(1)}, u32[]{:S(2)}) copy-start(f32[16,128]{1,0:T(8,128)S(1)} %collective-permute-done.7.down_ref) | copy-start | bytes 24580
  43.5 0.6 %copy-start.3 = (bf16[16,1408]{1,0:T(8,128)(2,1)}, bf16[16,1408]{1,0:T(8,128)(2,1)S(1)}, u32[]{:S(2)}) copy-start(bf16[16,1408]{1,0:T(8,128)(2,1)S(1)} %collective-permute-done.6.up_ref) | copy-start | bytes 135172
  45.6 4.3 %collective-permute-start.9 = (bf16[16,1408]{1,0:T(8,128)(2,1)}, bf16[16,1408]{1,0:T(8,128)(2,1)S(1)}, u32[]{:S(2)}, u32[]{:S(2)}) collective-permute-start(bf16[16,1408]{1,0:T(8,128)(2,1)} %shard_map.109.mine_ref), channel_id=1, source_target_pairs={{0,2},{2,0},{4,6},{6,4},{8,10},{10,8},{12,14},{14,12},{1,3},{3,1},... | collective-permute-start | bytes 135176 | tf_op jit(solution)/shard_map/ppermute | solution.py:566
  49.9 0.6 %copy-start.4 = (bf16[16,1408]{1,0:T(8,128)(2,1)}, bf16[16,1408]{1,0:T(8,128)(2,1)S(1)}, u32[]{:S(2)}) copy-start(bf16[16,1408]{1,0:T(8,128)(2,1)S(1)} %collective-permute-done.9.theirs_ref) | copy-start | bytes 135172

commit v2 on v1

--- a/solution.py
+++ b/solution.py
@@ -13,6 +13,7 @@
 HIGH = lax.Precision.HIGHEST
 VMEM = pl.BlockSpec(memory_space=pltpu.VMEM)
 SMEM = pl.BlockSpec(memory_space=pltpu.SMEM)
+HBM = pl.BlockSpec(memory_space=pltpu.HBM)
 
 
 def shifted(value, axis, steps):
@@ -184,7 +185,7 @@
     return (names == ids).astype(F32)
 
 
-def neighbours(sub_ref):
+def neighbours():
     subdomain = lax.axis_index("sub")
     count = lax.axis_size("sub")
     return lax.rem(subdomain + count - 1, count), subdomain, lax.rem(subdomain + 1, count)
@@ -195,9 +196,37 @@
     return slots < sizes_ref[interface]
 
 
-def open_kernel(sizes_ref, loads_ref, weights_ref, maps_ref, first_ref, pack_ref):
-    before, _, _ = neighbours(None)
+def fetched(pairs, sems):
+    copies = [pltpu.make_async_copy(*pair, sems.at[at]) for at, pair in enumerate(pairs)]
+    for copy in copies:
+        copy.start()
+    return copies
+
+
+def open_kernel(
+    sizes_in,
+    loads_in,
+    weights_in,
+    maps_in,
+    first_ref,
+    pack_ref,
+    sizes_ref,
+    loads_ref,
+    weights_ref,
+    maps_ref,
+    sems,
+):
+    pairs = (
+        (sizes_in, sizes_ref),
+        (loads_in, loads_ref),
+        (weights_in, weights_ref),
+        (maps_in, maps_ref),
+    )
+    copies = fetched(pairs, sems)
+    before, _, _ = neighbours()
     half = loads_ref.shape[1]
+    for copy in copies:
+        copy.wait()
     scale = weights_ref[...]
     loaded = jnp.where(live_row(sizes_ref, before, half), loads_ref[...], 0.0)
     first = loaded * scale
@@ -208,8 +237,29 @@
     pack_ref[...] = jnp.concatenate([first, maps_ref[...].astype(F32), spare], axis=0).astype(BF16)
 
 
-def select_kernel(right_ref, left_ref, right_hot_ref, left_hot_ref):
+def select_kernel(
+    right_in,
+    left_in,
+    ids_in,
+    operator_in,
+    right_hot_ref,
+    left_hot_ref,
+    ids_ref,
+    operator_ref,
+    right_ref,
+    left_ref,
+    sems,
+):
+    pairs = (
+        (right_in, right_ref),
+        (left_in, left_ref),
+        (ids_in, ids_ref),
+        (operator_in, operator_ref),
+    )
+    copies = fetched(pairs, sems)
     half = right_ref.shape[1]
+    copies[0].wait()
+    copies[1].wait()
 
     def one(at, carry):
         start = pl.multiple_of(at * LANES, LANES)
@@ -220,6 +270,8 @@
         return carry
 
     lax.fori_loop(0, half // LANES, one, 0)
+    copies[2].wait()
+    copies[3].wait()
 
 
 def first_kernel(
@@ -228,14 +280,15 @@
     right_hot_ref,
     left_hot_ref,
     first_ref,
+    own_map_ref,
     across_ref,
     pack_ref,
     ahead_ref,
     send_ref,
     pair_ref,
-    ordered_ref,
+    ordered_map_ref,
 ):
-    before, subdomain, after = neighbours(None)
+    before, subdomain, after = neighbours()
     lower = lax.axis_index("row") == 0
     columns, half = first_ref.shape
     corners = ids_ref.shape[1]
@@ -243,12 +296,15 @@
     right = jnp.where(lower, pack_ref[:columns, :], ahead_ref[...])
     slotted = nn(right, right_hot_ref[...]).astype(BF16)
     local = nt(left, operator_ref[:, :half]) + nt(slotted, operator_ref[:, half:])
-    ordered_ref[...] = local.astype(BF16)
+    raw_map = jnp.where(lower, across_ref[...], own_map_ref[...]).astype(F32)
+    mixed = jnp.concatenate([local, raw_map], axis=0).astype(BF16)
+    ordered = nt(mixed, right_hot_ref[...])
+    ordered_map_ref[...] = ordered[columns:].astype(BF16)
+    local = jnp.where(lower, local, ordered[:columns]).astype(BF16)
     pair_ref[columns:, :half] = pack_ref[columns:, :]
 
     @pl.when(jnp.logical_not(lower))
     def _():
-        ordered_ref[...] = nt(ordered_ref[...], right_hot_ref[...]).astype(BF16)
         pair_ref[columns:, :half] = nn(pack_ref[columns:, :], left_hot_ref[...]).astype(BF16)
 
     beside = pair_ref[columns : columns + corners, :half]
@@ -258,16 +314,10 @@
         two, hot_rows(ids_ref, jnp.where(lower, after, before), LANES), HIGH
     )
     high, low = halves(coarse)
-    send = jnp.concatenate([ordered_ref[...], high, low], axis=1)
+    send = jnp.concatenate([local, high, low], axis=1)
     send_ref[...] = send
     pair_ref[:columns, :] = send
     pair_ref[columns:, half:] = jnp.zeros((pair_ref.shape[0] - columns, 2 * LANES), BF16)
-
-
-def order_kernel(own_ref, across_ref, right_hot_ref, out_ref):
-    lower = lax.axis_index("row") == 0
-    raw = jnp.where(lower, across_ref[...], own_ref[...])
-    out_ref[...] = nt(raw, right_hot_ref[...]).astype(BF16)
 
 
 def second_kernel(
@@ -293,7 +343,7 @@
     small_ref,
     ordered_ref,
 ):
-    before, subdomain, after = neighbours(None)
+    before, subdomain, after = neighbours()
     lower = lax.axis_index("row") == 0
     columns, half = loads_ref.shape
     corners = ids_ref.shape[1]
@@ -399,7 +449,7 @@
     solution_ref,
     residual_ref,
 ):
-    before, subdomain, _ = neighbours(None)
+    before, subdomain, _ = neighbours()
     lower = lax.axis_index("row") == 0
     columns, half = loads_ref.shape
     corners = ids_ref.shape[1]
@@ -479,51 +529,77 @@
     along = pairs(lambda at, side: (at - 1, 0) if side == 0 else (at + 1, 1))
     slant = pairs(lambda at, side: (at - 1, 1) if side == 0 else (at + 1, 0))
 
-    def call(kernel, specs, outs, scratch=(), flops=0, moved=0):
-        return pl.pallas_call(
+    def call(kernel, specs, outs, scratch=(), flops=0, moved=0, room=4):
+        made = pl.pallas_call(
             kernel,
             in_specs=specs,
             out_specs=[VMEM] * len(outs),
             out_shape=outs,
             scratch_shapes=scratch,
             cost_estimate=cost(flops, moved),
+            compiler_params=pltpu.CompilerParams(vmem_limit_bytes=room << 20),
         )
+
+        def run(*operands):
+            pairs = zip(operands, specs, strict=True)
+            placed = [
+                pltpu.with_memory_space_constraint(operand, pltpu.HBM) if spec is HBM else operand
+                for operand, spec in pairs
+            ]
+            return made(*placed)
+
+        return run
 
     rows = columns + corners + 8
     first, pack = call(
         open_kernel,
-        [SMEM, VMEM, VMEM, VMEM],
+        [HBM] * 4,
         [shape((columns, half), BF16), shape((rows, half), BF16)],
+        scratch=[
+            pltpu.SMEM(iface_sizes.shape, jnp.int32),
+            pltpu.VMEM(loaded.shape, F32),
+            pltpu.VMEM(weights.shape, F32),
+            pltpu.VMEM(own_map.shape, BF16),
+            pltpu.SemaphoreType.DMA((4,)),
+        ],
         moved=4 * rows * half,
     )(iface_sizes, loaded, weights, own_map)
     other_map = lax.ppermute(own_map, grid, across)
     pack_in = lax.ppermute(pack, grid, along)
     ahead = lax.ppermute(first, grid, slant)
-    right_hot, left_hot = call(
+    right_hot, left_hot, ids, held = call(
         select_kernel,
-        [VMEM, VMEM],
-        [shape((half, half), BF16), shape((half, half), BF16)],
+        [HBM] * 4,
+        [
+            shape((half, half), BF16),
+            shape((half, half), BF16),
+            shape(corner_ids.shape, jnp.int32),
+            shape(operator.shape, BF16),
+        ],
+        scratch=[
+            pltpu.VMEM(right_partner.shape, jnp.int32),
+            pltpu.VMEM(left_partner.shape, jnp.int32),
+            pltpu.SemaphoreType.DMA((4,)),
+        ],
         flops=4 * half * half,
         moved=4 * half * half,
-    )(right_partner, left_partner)
-    send, kept = call(
+        room=12,
+    )(right_partner, left_partner, corner_ids, operator)
+    send, kept, ordered_map = call(
         first_kernel,
-        [VMEM] * 8,
-        [shape((columns, half + 2 * LANES), BF16), shape((rows, half + 2 * LANES), BF16)],
-        scratch=[pltpu.VMEM((columns, block), BF16)],
+        [VMEM] * 9,
+        [
+            shape((columns, half + 2 * LANES), BF16),
+            shape((rows, half + 2 * LANES), BF16),
+            shape((corners, half), BF16),
+        ],
         flops=2 * big,
         moved=4 * block * half,
-    )(corner_ids, operator, right_hot, left_hot, first, other_map, pack_in, ahead)
+        room=16,
+    )(ids, held, right_hot, left_hot, first, own_map, other_map, pack_in, ahead)
     pair_in = lax.ppermute(kept, grid, across)
     along_in = lax.ppermute(send, grid, along)
     slant_in = lax.ppermute(send, grid, slant)
-    (ordered_map,) = call(
-        order_kernel,
-        [VMEM] * 3,
-        [shape((corners, half), BF16)],
-        flops=2 * corners * half * half,
-        moved=2 * half * half,
-    )(own_map, other_map, right_hot)
     image, following, up, small = call(
         second_kernel,
         [SMEM] + [VMEM] * 15,
@@ -536,11 +612,12 @@
         scratch=[pltpu.VMEM((columns, block), BF16)],
         flops=2 * big,
         moved=4 * block * half,
+        room=16,
     )(
         iface_sizes,
-        corner_ids,
+        ids,
         coarse_inverse,
-        operator,
+        held,
         right_hot,
         loaded,
         weights,
@@ -571,7 +648,7 @@
         moved=24 * columns * half,
     )(
         iface_sizes,
-        corner_ids,
+        ids,
         coarse_inverse,
         loaded,
         weights,

time: 53 us -> 38.7 us (0.73)
  Pallas kernels: 24.1 us -> 10.7 us
  local copies, waits for them, and re-layouts: 3.74 us -> 0.03 us
  waiting for transfers between devices: 8.37 us -> 11.3 us
    pallas_call x7 -> x6, Pallas kernels: 24.1 us -> 10.7 us  [run(): return made(*placed)]
    unnamed x20 -> x10, local copies, waits for them, and re-layouts: 3.74 us -> 0.03 us
    ppermute x1, waiting for transfers between devices: 1.66 us -> 4.21 us  [ring(): slant_in = lax.ppermute(send, grid, slant)]
    ppermute x1, waiting for transfers between devices: 1.57 us -> 2.42 us  [ring(): ahead = lax.ppermute(first, grid, slant)]
  transfers between devices with their start and end apart: 10 -> 10, of which waited for: 5 -> 5; matrix products, arithmetic and copies ran while one was open for 0% -> 0% of each run, Pallas kernels for 12% -> 6%
where the time goes in v2:
time: 38.7 us; the launch traced here: 38.5 us
  starting transfers between devices  15.7 us (41%)
  waiting for transfers between devices  11.3 us (29%)
  Pallas kernels  10.7 us (28%)
  between operations  0.73 us (2%)
    pallas_call x6, Pallas kernels, run(): return made(*placed)  10.7 us
    ppermute x1, starting transfers between devices, ring(): pack_in = lax.ppermute(pack, grid, along)  5.13 us
    ppermute x1, waiting for transfers between devices, ring(): slant_in = lax.ppermute(send, grid, slant)  4.21 us
    ppermute x3, starting transfers between devices, shifted(): return lax.ppermute(value, axis, pairs)  3.88 us
    ppermute x1, waiting for transfers between devices, ring(): theirs = lax.ppermute(mine, grid, across)  2.48 us
    ppermute x1, waiting for transfers between devices, ring(): ahead = lax.ppermute(first, grid, slant)  2.42 us
    ppermute x3, waiting for transfers between devices, shifted(): return lax.ppermute(value, axis, pairs)  2.19 us
    ppermute x1, starting transfers between devices, ring(): ahead = lax.ppermute(first, grid, slant)  1.91 us
  transfers between devices with their start and end apart: 10, of which 5 were waited for; matrix products, arithmetic and copies ran while one was open for 0% of the time, Pallas kernels for 6%

profile of v2, /device:TPU:0, one launch (start us, length us, event | category | flops | bytes accessed | tf_op | source)
XLA Modules:
  0.0 38.5 jit_solution(13978702532566684327)
XLA Ops:
  0.6 0.0 copy-start
  0.6 0.9 %shard_map.105 = (bf16[16,1024]{1,0:T(8,128)(2,1)S(1)}, bf16[48,1024]{1,0:T(8,128)(2,1)S(1)}) custom-call(s32[4]{0:T(128)} %sizes_ref.3, f32[16,1024]{1,0:T(8,128)} %bitcast.10, f32[1,1024]{1,0:T(1,128)} %weights_ref.3, bf16[24,1024]{1,0:T(8,128)(2,1)} %bitcast.5), custom_call_target="tpu_custom_call" | custom-call | bytes 196608 | tf_op jit(solution)/shard_map/pallas_call | solution.py:549
  1.6 5.1 %collective-permute-start.1 = (bf16[48,1024]{1,0:T(8,128)(2,1)S(1)}, bf16[48,1024]{1,0:T(8,128)(2,1)S(1)}, u32[]{:S(2)}, u32[]{:S(2)}) collective-permute-start(bf16[48,1024]{1,0:T(8,128)(2,1)S(1)} %get-tuple-element.22), channel_id=1, source_target_pairs={{0,12},{2,6},{4,0},{6,10},{8,4},{10,14},{12,8},{14,2},{1,13},{3,7}... | collective-permute-start | bytes 294920 | tf_op jit(solution)/shard_map/ppermute | solution.py:568
  6.7 0.0 collective-permute-start
  6.7 1.9 %collective-permute-start.2 = (bf16[16,1024]{1,0:T(8,128)(2,1)S(1)}, bf16[16,1024]{1,0:T(8,128)(2,1)S(1)}, u32[]{:S(2)}, u32[]{:S(2)}) collective-permute-start(bf16[16,1024]{1,0:T(8,128)(2,1)S(1)} %get-tuple-element.21.first_ref), channel_id=1, source_target_pairs={{0,14},{2,4},{4,2},{6,8},{8,6},{10,12},{12,10},{14,0},{1,15},{3,5}... | collective-permute-start | bytes 98312 | tf_op jit(solution)/shard_map/ppermute | solution.py:569
  8.6 2.3 %shard_map.104 = (bf16[1024,1024]{1,0:T(8,128)(2,1)S(1)}, bf16[1024,1024]{1,0:T(8,128)(2,1)S(1)}, s32[4,24]{1,0:T(4,128)S(1)}, bf16[1024,2048]{1,0:T(8,128)(2,1)S(1)}) custom-call(s32[1,1024]{1,0:T(1,128)} %right_in.1, s32[1,1024]{1,0:T(1,128)} %left_in.1, s32[4,24]{1,0:T(4,128)} %ids_in.1, bf16[1024,2048]{1,0:T(8,128)(2,1)} %bitcast.13), custom_call_target="tpu_custom_call" | custom-call | flops 4194304 | bytes 4194304 | tf_op jit(solution)/shard_map/pallas_call | solution.py:549
  10.9 2.4 %collective-permute-done.2.ahead_ref = bf16[16,1024]{1,0:T(8,128)(2,1)S(1)} collective-permute-done((bf16[16,1024]{1,0:T(8,128)(2,1)S(1)}, bf16[16,1024]{1,0:T(8,128)(2,1)S(1)}, u32[]{:S(2)}, u32[]{:S(2)}) %collective-permute-start.2) | collective-permute-done | bytes 32800 | tf_op jit(solution)/shard_map/ppermute | solution.py:569
  13.3 0.0 collective-permute-done.across_ref
  13.3 0.0 collective-permute-done.1.pack_ref
  13.3 0.0 copy-done
  13.3 0.0 copy-start.1
  13.3 0.0 copy-start.2
  13.4 0.0 copy-start.3
  13.4 0.0 copy-start.4
  13.4 2.5 %shard_map.106 = (bf16[16,1280]{1,0:T(8,128)(2,1)S(1)}, bf16[48,1280]{1,0:T(8,128)(2,1)S(1)}, bf16[24,1024]{1,0:T(8,128)(2,1)S(1)}) custom-call(s32[4,24]{1,0:T(4,128)S(1)} %get-tuple-element.17.ids_ref, bf16[1024,2048]{1,0:T(8,128)(2,1)S(1)} %get-tuple-element.18.operator_ref, bf16[1024,1024]{1,0:T(8,128)(2,1)S(1)} %get-tuple-element.19.right_hot_ref, ...), custom_call_target="tpu_custom_call" | custom-call | flops 134217728 | bytes 4194304 | tf_op jit(solution)/shard_map/pallas_call | solution.py:549
  15.9 0.7 %collective-permute-start.3 = (bf16[48,1280]{1,0:T(8,128)(2,1)S(1)}, bf16[48,1280]{1,0:T(8,128)(2,1)S(1)}, u32[]{:S(2)}, u32[]{:S(2)}) collective-permute-start(bf16[48,1280]{1,0:T(8,128)(2,1)S(1)} %get-tuple-element.23.kept_ref), channel_id=1, source_target_pairs={{0,2},{2,0},{4,6},{6,4},{8,10},{10,8},{12,14},{14,12},{1,3},{3,1},... | collective-permute-start | bytes 368648 | tf_op jit(solution)/shard_map/ppermute | solution.py:600
  16.6 1.7 %collective-permute-start.5 = (bf16[16,1280]{1,0:T(8,128)(2,1)S(1)}, bf16[16,1280]{1,0:T(8,128)(2,1)S(1)}, u32[]{:S(2)}, u32[]{:S(2)}) collective-permute-start(bf16[16,1280]{1,0:T(8,128)(2,1)S(1)} %get-tuple-element.25.send_ref), channel_id=1, source_target_pairs={{0,14},{2,4},{4,2},{6,8},{8,6},{10,12},{12,10},{14,0},{1,15},{3,5}... | collective-permute-start | bytes 122888 | tf_op jit(solution)/shard_map/ppermute | solution.py:602
  18.3 0.8 %collective-permute-start.4 = (bf16[16,1280]{1,0:T(8,128)(2,1)S(1)}, bf16[16,1280]{1,0:T(8,128)(2,1)S(1)}, u32[]{:S(2)}, u32[]{:S(2)}) collective-permute-start(bf16[16,1280]{1,0:T(8,128)(2,1)S(1)} %get-tuple-element.25.send_ref), channel_id=1, source_target_pairs={{0,12},{2,6},{4,0},{6,10},{8,4},{10,14},{12,8},{14,2},{1,13},{3,7}... | collective-permute-start | bytes 122888 | tf_op jit(solution)/shard_map/ppermute | solution.py:601
  19.1 4.2 %collective-permute-done.5.slant_ref = bf16[16,1280]{1,0:T(8,128)(2,1)S(1)} collective-permute-done((bf16[16,1280]{1,0:T(8,128)(2,1)S(1)}, bf16[16,1280]{1,0:T(8,128)(2,1)S(1)}, u32[]{:S(2)}, u32[]{:S(2)}) %collective-permute-start.5) | collective-permute-done | bytes 40992 | tf_op jit(solution)/shard_map/ppermute | solution.py:602
  23.3 0.0 collective-permute-done.4.along_ref
  23.3 0.0 collective-permute-done.3.pair_ref
  23.3 0.0 copy-done.1
  23.3 0.0 copy-done.2
  23.3 0.0 copy-done.3
  23.3 0.0 copy-done.4
  23.4 3.3 %shard_map.107 = (f32[16,1024]{1,0:T(8,128)S(1)}, f32[16,1024]{1,0:T(8,128)S(1)}, bf16[16,1408]{1,0:T(8,128)(2,1)S(1)}, f32[16,128]{1,0:T(8,128)S(1)}) custom-call(s32[4]{0:T(128)S(1)} %copy-done.4, s32[4,24]{1,0:T(4,128)S(1)} %get-tuple-element.17.ids_ref, f32[48,48]{1,0:T(8,128)S(1)} %copy-done.2, bf16[1024,2048]{1,0:T(8,128)(2,1)S(1)} %get-tuple-element.18.operator_ref, ...), custom_call_target="tpu_custom_call" | custom-call | flops 134217728 | bytes 4194304 | tf_op jit(solution)/shard_map/pallas_call | solution.py:549
  26.7 0.1 collective-permute-start.6
  26.8 2.1 %collective-permute-start.8 = (f32[16,128]{1,0:T(8,128)S(1)}, f32[16,128]{1,0:T(8,128)S(1)}, u32[]{:S(2)}, u32[]{:S(2)}) collective-permute-start(f32[16,128]{1,0:T(8,128)S(1)} %get-tuple-element.29.own_ref), channel_id=1, source_target_pairs={{0,8},{4,12},{8,0},{12,4},{1,9},{5,13},{9,1},{13,5},{2,10},{6,14},... | collective-permute-start | bytes 24584 | tf_op jit(solution)/shard_map/ppermute | solution.py:22
  28.9 1.7 %collective-permute-start.7 = (f32[16,128]{1,0:T(8,128)S(1)}, f32[16,128]{1,0:T(8,128)S(1)}, u32[]{:S(2)}, u32[]{:S(2)}) collective-permute-start(f32[16,128]{1,0:T(8,128)S(1)} %get-tuple-element.29.own_ref), channel_id=1, source_target_pairs={{0,12},{4,0},{8,4},{12,8},{1,13},{5,1},{9,5},{13,9},{2,14},{6,2},{... | collective-permute-start | bytes 24584 | tf_op jit(solution)/shard_map/ppermute | solution.py:22
  30.5 0.8 %collective-permute-done.8.far_ref = f32[16,128]{1,0:T(8,128)S(1)} collective-permute-done((f32[16,128]{1,0:T(8,128)S(1)}, f32[16,128]{1,0:T(8,128)S(1)}, u32[]{:S(2)}, u32[]{:S(2)}) %collective-permute-start.8) | collective-permute-done | bytes 8224 | tf_op jit(solution)/shard_map/ppermute | solution.py:22
  31.4 1.4 %collective-permute-done.7.down_ref = f32[16,128]{1,0:T(8,128)S(1)} collective-permute-done((f32[16,128]{1,0:T(8,128)S(1)}, f32[16,128]{1,0:T(8,128)S(1)}, u32[]{:S(2)}, u32[]{:S(2)}) %collective-permute-start.7) | collective-permute-done | bytes 8224 | tf_op jit(solution)/shard_map/ppermute | solution.py:22
  32.7 0.0 collective-permute-done.6.up_ref
  32.8 1.6 %collective-permute-start.9 = (bf16[16,1408]{1,0:T(8,128)(2,1)S(1)}, bf16[16,1408]{1,0:T(8,128)(2,1)S(1)}, u32[]{:S(2)}, u32[]{:S(2)}) collective-permute-start(bf16[16,1408]{1,0:T(8,128)(2,1)S(1)} %shard_map.108.mine_ref), channel_id=1, source_target_pairs={{0,2},{2,0},{4,6},{6,4},{8,10},{10,8},{12,14},{14,12},{1,3},{3,1},... | collective-permute-start | bytes 135176 | tf_op jit(solution)/shard_map/ppermute | solution.py:643
  34.4 2.5 %collective-permute-done.9.theirs_ref = bf16[16,1408]{1,0:T(8,128)(2,1)S(1)} collective-permute-done((bf16[16,1408]{1,0:T(8,128)(2,1)S(1)}, bf16[16,1408]{1,0:T(8,128)(2,1)S(1)}, u32[]{:S(2)}, u32[]{:S(2)}) %collective-permute-start.9) | collective-permute-done | bytes 45088 | tf_op jit(solution)/shard_map/ppermute | solution.py:643
  36.9 1.6 %shard_map.109 = (f32[16,1024]{1,0:T(8,128)}, f32[16,1024]{1,0:T(8,128)}) custom-call(s32[4]{0:T(128)S(1)} %copy-done.4, s32[4,24]{1,0:T(4,128)S(1)} %get-tuple-element.17.ids_ref, f32[48,48]{1,0:T(8,128)S(1)} %copy-done.2, f32[16,1024]{1,0:T(8,128)S(1)} %bitcast.12, f32[1,1024]{1,0:T(1,128)S(1)} %copy-done.3, bf16[24,1024]{1,0:T(8,128)(2,1)S(1)} %bitcast.9, ...), custom_call_target="tpu_custom_call" | custom-call | bytes 393216 | tf_op jit(solution)/shard_map/pallas_call | solution.py:549
  (1 shorter events, 0.0 us)
Async XLA Ops:
  0.6 12.7 %copy-start = (bf16[1,24,1024]{2,1,0:T(8,128)(2,1)S(1)}, bf16[1,24,1024]{2,1,0:T(8,128)(2,1)}, u32[]{:S(2)}) copy-start(bf16[1,24,1024]{2,1,0:T(8,128)(2,1)} %param.12) | copy-start | bytes 147460
  1.6 11.8 %collective-permute-start.1 = (bf16[48,1024]{1,0:T(8,128)(2,1)S(1)}, bf16[48,1024]{1,0:T(8,128)(2,1)S(1)}, u32[]{:S(2)}, u32[]{:S(2)}) collective-permute-start(bf16[48,1024]{1,0:T(8,128)(2,1)S(1)} %get-tuple-element.22), channel_id=1, source_target_pairs={{0,12},{2,6},{4,0},{6,10},{8,4},{10,14},{12,8},{14,2},{1,13},{3,7}... | collective-permute-start | bytes 294920 | tf_op jit(solution)/shard_map/ppermute | solution.py:568
  6.7 6.6 %collective-permute-start = (bf16[24,1024]{1,0:T(8,128)(2,1)}, bf16[24,1024]{1,0:T(8,128)(2,1)S(1)}, u32[]{:S(2)}, u32[]{:S(2)}) collective-permute-start(bf16[24,1024]{1,0:T(8,128)(2,1)} %bitcast.6), channel_id=1, source_target_pairs={{0,2},{2,0},{4,6},{6,4},{8,10},{10,8},{12,14},{14,12},{1,3},{3,1},... | collective-permute-start | bytes 147464 | tf_op jit(solution)/shard_map/ppermute | solution.py:567
  6.7 6.6 %collective-permute-start.2 = (bf16[16,1024]{1,0:T(8,128)(2,1)S(1)}, bf16[16,1024]{1,0:T(8,128)(2,1)S(1)}, u32[]{:S(2)}, u32[]{:S(2)}) collective-permute-start(bf16[16,1024]{1,0:T(8,128)(2,1)S(1)} %get-tuple-element.21.first_ref), channel_id=1, source_target_pairs={{0,14},{2,4},{4,2},{6,8},{8,6},{10,12},{12,10},{14,0},{1,15},{3,5}... | collective-permute-start | bytes 98312 | tf_op jit(solution)/shard_map/ppermute | solution.py:569
  13.3 10.0 %copy-start.1 = (f32[1,16,1024]{2,1,0:T(8,128)S(1)}, f32[1,16,1024]{2,1,0:T(8,128)}, u32[]{:S(2)}) copy-start(f32[1,16,1024]{2,1,0:T(8,128)} %param.9) | copy-start | bytes 196612
  13.3 10.0 %copy-start.2 = (f32[48,48]{1,0:T(8,128)S(1)}, f32[48,48]{1,0:T(8,128)}, u32[]{:S(2)}) copy-start(f32[48,48]{1,0:T(8,128)} %inverse_ref.3) | copy-start | bytes 27652
  13.4 10.0 %copy-start.3 = (f32[1,1024]{1,0:T(1,128)S(1)}, f32[1,1024]{1,0:T(1,128)}, u32[]{:S(2)}) copy-start(f32[1,1024]{1,0:T(1,128)} %weights_ref.3) | copy-start | bytes 12292
  13.4 10.0 %copy-start.4 = (s32[4]{0:T(128)S(1)}, s32[4]{0:T(128)}, u32[]{:S(2)}) copy-start(s32[4]{0:T(128)} %sizes_ref.3) | copy-start | bytes 52
  15.9 7.4 %collective-permute-start.3 = (bf16[48,1280]{1,0:T(8,128)(2,1)S(1)}, bf16[48,1280]{1,0:T(8,128)(2,1)S(1)}, u32[]{:S(2)}, u32[]{:S(2)}) collective-permute-start(bf16[48,1280]{1,0:T(8,128)(2,1)S(1)} %get-tuple-element.23.kept_ref), channel_id=1, source_target_pairs={{0,2},{2,0},{4,6},{6,4},{8,10},{10,8},{12,14},{14,12},{1,3},{3,1},... | collective-permute-start | bytes 368648 | tf_op jit(solution)/shard_map/ppermute | solution.py:600
  16.6 6.7 %collective-permute-start.5 = (bf16[16,1280]{1,0:T(8,128)(2,1)S(1)}, bf16[16,1280]{1,0:T(8,128)(2,1)S(1)}, u32[]{:S(2)}, u32[]{:S(2)}) collective-permute-start(bf16[16,1280]{1,0:T(8,128)(2,1)S(1)} %get-tuple-element.25.send_ref), channel_id=1, source_target_pairs={{0,14},{2,4},{4,2},{6,8},{8,6},{10,12},{12,10},{14,0},{1,15},{3,5}... | collective-permute-start | bytes 122888 | tf_op jit(solution)/shard_map/ppermute | solution.py:602
  18.3 5.0 %collective-permute-start.4 = (bf16[16,1280]{1,0:T(8,128)(2,1)S(1)}, bf16[16,1280]{1,0:T(8,128)(2,1)S(1)}, u32[]{:S(2)}, u32[]{:S(2)}) collective-permute-start(bf16[16,1280]{1,0:T(8,128)(2,1)S(1)} %get-tuple-element.25.send_ref), channel_id=1, source_target_pairs={{0,12},{2,6},{4,0},{6,10},{8,4},{10,14},{12,8},{14,2},{1,13},{3,7}... | collective-permute-start | bytes 122888 | tf_op jit(solution)/shard_map/ppermute | solution.py:601
  26.7 6.1 %collective-permute-start.6 = (bf16[16,1408]{1,0:T(8,128)(2,1)S(1)}, bf16[16,1408]{1,0:T(8,128)(2,1)S(1)}, u32[]{:S(2)}, u32[]{:S(2)}) collective-permute-start(bf16[16,1408]{1,0:T(8,128)(2,1)S(1)} %get-tuple-element.28.up_own_ref), channel_id=1, source_target_pairs={{0,4},{4,8},{8,12},{12,0},{1,5},{5,9},{9,13},{13,1},{2,6},{6,10},{... | collective-permute-start | bytes 135176 | tf_op jit(solution)/shard_map/ppermute | solution.py:22
  26.8 4.5 %collective-permute-start.8 = (f32[16,128]{1,0:T(8,128)S(1)}, f32[16,128]{1,0:T(8,128)S(1)}, u32[]{:S(2)}, u32[]{:S(2)}) collective-permute-start(f32[16,128]{1,0:T(8,128)S(1)} %get-tuple-element.29.own_ref), channel_id=1, source_target_pairs={{0,8},{4,12},{8,0},{12,4},{1,9},{5,13},{9,1},{13,5},{2,10},{6,14},... | collective-permute-start | bytes 24584 | tf_op jit(solution)/shard_map/ppermute | solution.py:22
  28.9 3.9 %collective-permute-start.7 = (f32[16,128]{1,0:T(8,128)S(1)}, f32[16,128]{1,0:T(8,128)S(1)}, u32[]{:S(2)}, u32[]{:S(2)}) collective-permute-start(f32[16,128]{1,0:T(8,128)S(1)} %get-tuple-element.29.own_ref), channel_id=1, source_target_pairs={{0,12},{4,0},{8,4},{12,8},{1,13},{5,1},{9,5},{13,9},{2,14},{6,2},{... | collective-permute-start | bytes 24584 | tf_op jit(solution)/shard_map/ppermute | solution.py:22
  32.8 4.1 %collective-permute-start.9 = (bf16[16,1408]{1,0:T(8,128)(2,1)S(1)}, bf16[16,1408]{1,0:T(8,128)(2,1)S(1)}, u32[]{:S(2)}, u32[]{:S(2)}) collective-permute-start(bf16[16,1408]{1,0:T(8,128)(2,1)S(1)} %shard_map.108.mine_ref), channel_id=1, source_target_pairs={{0,2},{2,0},{4,6},{6,4},{8,10},{10,8},{12,14},{14,12},{1,3},{3,1},... | collective-permute-start | bytes 135176 | tf_op jit(solution)/shard_map/ppermute | solution.py:643

commit v3 on v0

--- a/solution.py
+++ b/solution.py
@@ -1,10 +1,18 @@
 import jax
 import jax.numpy as jnp
 from jax import lax
+from jax.experimental import pallas as pl
+from jax.experimental.pallas import tpu as pltpu
 from jax.sharding import PartitionSpec as P
 
 TILE = 128
+LANES = 128
 ITERS = 2
+F32 = jnp.float32
+BF16 = jnp.bfloat16
+HIGH = lax.Precision.HIGHEST
+VMEM = pl.BlockSpec(memory_space=pltpu.VMEM)
+HBM = pl.BlockSpec(memory_space=pltpu.HBM)
 
 
 def shifted(value, axis, steps):
@@ -40,7 +48,7 @@
     return (live_cols + TILE - 1) // TILE
 
 
-def per_device(
+def general(
     loads,
     weights,
     dual_ops,
@@ -127,6 +135,584 @@
     return (solution[:, :half][None], residual[:, :half][None])
 
 
+def cost(flops, moved):
+    return pl.CostEstimate(flops=flops, bytes_accessed=moved, transcendentals=0)
+
+
+def nt(first, second, precision=None):
+    return lax.dot_general(
+        first, second, (((1,), (1,)), ((), ())), preferred_element_type=F32, precision=precision
+    )
+
+
+def nn(first, second, precision=None):
+    return jnp.dot(first, second, preferred_element_type=F32, precision=precision)
+
+
+def halves(value):
+    high = value.astype(BF16)
+    return high, (value - high.astype(F32)).astype(BF16)
+
+
+def stacked(value):
+    return jnp.concatenate(halves(value), axis=0)
+
+
+def folded(value):
+    rows = value.shape[0] // 2
+    return value[:rows] + value[rows:]
+
+
+def thirds(value):
+    high = value.astype(BF16)
+    rest = value - high.astype(F32)
+    middle = rest.astype(BF16)
+    return high, middle, (rest - middle.astype(F32)).astype(BF16)
+
+
+def pieces_sum(ref, half, count):
+    total = ref[:, half : half + LANES].astype(F32)
+    for piece in range(1, count):
+        at = half + piece * LANES
+        total = total + ref[:, at : at + LANES].astype(F32)
+    return total
+
+
+def neighbours():
+    subdomain = lax.axis_index("sub")
+    count = lax.axis_size("sub")
+    return lax.rem(subdomain + count - 1, count), subdomain, lax.rem(subdomain + 1, count)
+
+
+def hot_rows(ids_ref, subdomain, extent):
+    ids = ids_ref[pl.ds(subdomain, 1), :]
+    names = lax.broadcasted_iota(jnp.int32, (extent, ids.shape[1]), 0)
+    return (names == ids).astype(F32)
+
+
+def hot_names(ids_ref):
+    spare = jnp.zeros((LANES, LANES - 3 * ids_ref.shape[1]), F32)
+    hots = [hot_rows(ids_ref, each, LANES) for each in neighbours()]
+    return jnp.concatenate([*hots, spare], axis=1)
+
+
+def selected(values, names):
+    high, middle, low = thirds(values)
+    rows = values.shape[0]
+    parts = nt(jnp.concatenate([high, middle, low], axis=0), names)
+    return parts[:rows] + parts[rows : 2 * rows] + parts[2 * rows :]
+
+
+def solved_backs(coarse, solver):
+    rows = coarse.shape[0]
+    parts = nn(stacked(coarse), solver)
+    width = solver.shape[1] // 2
+    return parts[:rows, :width] + (parts[:rows, width:] + parts[rows:, :width])
+
+
+def open_kernel(
+    sizes_in,
+    loads_in,
+    maps_in,
+    weights_in,
+    ids_in,
+    inverse_in,
+    right_in,
+    left_in,
+    pack_ref,
+    loaded_ref,
+    live_ref,
+    weights_ref,
+    ids_ref,
+    inverse_ref,
+    right_ref,
+    left_ref,
+    sizes_ref,
+    loads_ref,
+    maps_ref,
+    sems,
+):
+    pairs = (
+        (sizes_in, sizes_ref),
+        (loads_in, loads_ref),
+        (weights_in, weights_ref),
+        (maps_in, maps_ref),
+        (ids_in, ids_ref),
+        (inverse_in, inverse_ref),
+        (right_in, right_ref),
+        (left_in, left_ref),
+    )
+    copies = [pltpu.make_async_copy(*pair, sems.at[at]) for at, pair in enumerate(pairs)]
+    for copy in copies:
+        copy.start()
+    before, subdomain, _ = neighbours()
+    for copy in copies:
+        copy.wait()
+    slots = lax.broadcasted_iota(jnp.int32, live_ref.shape, 1)
+    which = lax.broadcasted_iota(jnp.int32, live_ref.shape, 0)
+    bound = jnp.where(which == 0, sizes_ref[before], sizes_ref[subdomain])
+    live = (slots < bound).astype(F32)
+    live_ref[...] = live
+    scale = weights_ref[...]
+    loaded = jnp.where(live[0:1] > 0.0, loads_ref[...], 0.0)
+    loaded_ref[...] = loaded
+    first = loaded * scale
+    high = scale.astype(BF16).astype(F32)
+    spare = jnp.where(which == 0, high, jnp.where(which == 1, scale - high, 0.0))
+    pack_ref[...] = jnp.concatenate([first, maps_ref[...].astype(F32), spare], axis=0).astype(BF16)
+
+
+def side_columns(ref, side, half):
+    return ref.at[:, pl.ds(pl.multiple_of(side * half, half), half)]
+
+
+def select_kernel(
+    right_ref,
+    left_ref,
+    pack_ref,
+    operator_in,
+    right_hot_ref,
+    order_ref,
+    left_hot_ref,
+    square_ref,
+    cross_ref,
+    local_ref,
+    turned_ref,
+    sems,
+):
+    half = right_ref.shape[1]
+    columns = local_ref.shape[0]
+    side = lax.axis_index("row")
+    lower = side == 0
+    square = pltpu.make_async_copy(side_columns(operator_in, side, half), square_ref, sems.at[0])
+    cross = pltpu.make_async_copy(side_columns(operator_in, 1 - side, half), cross_ref, sems.at[1])
+
+    @pl.when(lower)
+    def _():
+        square.start()
+        cross.start()
+
+    @pl.when(jnp.logical_not(lower))
+    def _():
+        cross.start()
+        square.start()
+
+    right = right_ref[...]
+    tall = jnp.transpose(jnp.broadcast_to(right, (8, half)).astype(F32))[:, 0:1].astype(jnp.int32)
+    names = lax.broadcasted_iota(jnp.int32, (LANES, half), 1)
+    for at in range(half // LANES):
+        rows = slice(at * LANES, (at + 1) * LANES)
+        order_ref[rows, :] = (names == tall[rows]).astype(F32).astype(BF16)
+
+    def one(at, carry):
+        start = pl.multiple_of(at * LANES, LANES)
+        slots = lax.broadcasted_iota(jnp.int32, (LANES, half), 0) + start
+        rows = pl.ds(start, LANES)
+        right_hot_ref[rows, :] = (slots == right).astype(F32).astype(BF16)
+        left_hot_ref[rows, :] = (slots == left_ref[...]).astype(F32).astype(BF16)
+        return carry
+
+    lax.fori_loop(0, half // LANES, one, 0)
+    left = pack_ref[:columns, :]
+
+    @pl.when(lower)
+    def _():
+        turned_ref[...] = left
+        square.wait()
+        local_ref[...] = nn(left, square_ref[...])
+        cross.wait()
+
+    @pl.when(jnp.logical_not(lower))
+    def _():
+        turned_ref[...] = nt(left, left_hot_ref[...]).astype(BF16)
+        cross.wait()
+        local_ref[...] = nt(left, cross_ref[...])
+        square.wait()
+
+
+def first_kernel(
+    ids_ref,
+    square_ref,
+    cross_ref,
+    right_hot_ref,
+    order_ref,
+    local_ref,
+    turned_ref,
+    own_pack_ref,
+    across_ref,
+    along_ref,
+    slant_ref,
+    send_ref,
+):
+    columns, half = local_ref.shape
+    corners = ids_ref.shape[1]
+    before, subdomain, after = neighbours()
+    lower = lax.axis_index("row") == 0
+    left = own_pack_ref[:columns, :]
+    right = jnp.where(lower, along_ref[:columns, :], slant_ref[:columns, :])
+    slotted = nn(right, right_hot_ref[...]).astype(BF16)
+
+    @pl.when(lower)
+    def _():
+        send_ref[:, :half] = (local_ref[...] + nt(slotted, cross_ref[...])).astype(BF16)
+
+    @pl.when(jnp.logical_not(lower))
+    def _():
+        local = (local_ref[...] + nn(slotted, square_ref[...])).astype(BF16)
+        send_ref[:, :half] = nn(local, order_ref[...]).astype(BF16)
+
+    one = nt(jnp.where(lower, slotted, left), across_ref[...])
+    beside = along_ref[columns:, :]
+    two = nt(jnp.where(lower, right, turned_ref[...]), beside)[:, :corners]
+    hot_own = hot_rows(ids_ref, subdomain, LANES)
+    hot_other = hot_rows(ids_ref, jnp.where(lower, after, before), LANES)
+    high, low = halves(selected(one, hot_own) + selected(two, hot_other))
+    send_ref[:, half:] = jnp.concatenate([high, low], axis=1)
+
+
+def order_kernel(
+    ids_ref,
+    inverse_ref,
+    order_ref,
+    left_hot_ref,
+    own_pack_ref,
+    across_ref,
+    along_ref,
+    slant_ref,
+    maps_ref,
+    solver_ref,
+    scale_ref,
+    names_ref,
+):
+    half = order_ref.shape[1]
+    corners = ids_ref.shape[1]
+    width = inverse_ref.shape[0]
+    columns = own_pack_ref.shape[0] - corners - 8
+    lower = lax.axis_index("row") == 0
+    own, across = own_pack_ref[columns:, :].astype(F32)[:corners], across_ref[...].astype(F32)
+    along, slant = along_ref[columns:, :].astype(F32), slant_ref[columns:, :].astype(F32)
+    ahead, behind = jnp.where(lower, along, slant), jnp.where(lower, slant, along)
+    scale_ref[...] = ahead[corners : corners + 1] + ahead[corners + 1 : corners + 2]
+    raw = jnp.where(lower, across, own).astype(BF16)
+    ordered = nn(raw, order_ref[...])
+    turned = nn(behind[:corners].astype(BF16), left_hot_ref[...])
+    spare = jnp.zeros((LANES - 3 * corners, half), F32)
+    blank = jnp.zeros((corners, half), F32)
+    mine = jnp.where(lower, own, across)
+    maps_ref[:, :half] = jnp.concatenate([turned, mine, blank, spare], axis=0).astype(BF16)
+    maps_ref[:, half:] = jnp.concatenate([blank, ordered, ahead[:corners], spare], axis=0).astype(BF16)
+    names = hot_names(ids_ref)
+    names_ref[...] = names.astype(BF16)
+    backs = nn(inverse_ref[...], names[:width], HIGH)
+    low_rows = jnp.zeros((LANES - width, LANES), F32)
+    side = jnp.concatenate([inverse_ref[...], jnp.zeros((width, LANES - width), F32)], axis=1)
+    pieces = []
+    for piece in (backs, side):
+        tall = jnp.concatenate([piece, low_rows], axis=0)
+        pieces.extend(halves(tall))
+    solver_ref[...] = jnp.concatenate(pieces, axis=1)
+
+
+def second_kernel(
+    names_ref,
+    solver_ref,
+    maps_ref,
+    right_hot_ref,
+    order_ref,
+    square_ref,
+    cross_ref,
+    live_ref,
+    loaded_ref,
+    weights_ref,
+    scale_ref,
+    own_ref,
+    across_ref,
+    along_ref,
+    slant_ref,
+    image_ref,
+    next_ref,
+    up_ref,
+    small_ref,
+):
+    lower = lax.axis_index("row") == 0
+    columns, half = loaded_ref.shape
+    own, across = own_ref[:, :half].astype(F32), across_ref[:, :half].astype(F32)
+    along, slant = along_ref[:, :half].astype(F32), slant_ref[:, :half].astype(F32)
+    mine = pieces_sum(own_ref, half, 2) + pieces_sum(across_ref, half, 2)
+    coarse = mine + (pieces_sum(along_ref, half, 2) + pieces_sum(slant_ref, half, 2))
+    backs = solved_backs(coarse, solver_ref[:, : 2 * LANES]).astype(BF16)
+    fix = nn(backs, maps_ref[...])
+    image = jnp.where(lower, own, across) + jnp.where(lower, slant, along) + fix[:, :half]
+    image = jnp.where(live_ref[0:1] > 0.0, image, 0.0)
+    image_right = jnp.where(lower, across, own) + jnp.where(lower, along, slant) + fix[:, half:]
+    image_right = jnp.where(live_ref[1:2] > 0.0, image_right, 0.0)
+    left = weights_ref[...] * image
+    right = scale_ref[...] * image_right
+    image_ref[...] = image
+    next_ref[...] = left
+    left_2, right_2 = stacked(left), stacked(right)
+    slotted_2 = nn(right_2, right_hot_ref[...]).astype(BF16)
+    near, far = jnp.where(lower, left_2, slotted_2), jnp.where(lower, slotted_2, left_2)
+    local = folded(nn(near, square_ref[...]) + nt(far, cross_ref[...]))
+    rounded = local.astype(BF16)
+    up_ref[:, :half] = rounded
+
+    @pl.when(jnp.logical_not(lower))
+    def _():
+        up_ref[:, :half] = nn(rounded, order_ref[...]).astype(BF16)
+
+    block = folded(near.astype(F32))
+    energy = jnp.sum(block * local, axis=1, keepdims=True)
+    sided = jnp.where(lower, maps_ref[:, half:], maps_ref[:, :half])
+    corner = folded(nt(jnp.where(lower, right_2, left_2), sided))
+    loaded = loaded_ref[...]
+    first = loaded * weights_ref[...]
+    sums = (
+        jnp.sum(loaded * first, axis=1, keepdims=True),
+        jnp.sum(first * image, axis=1, keepdims=True),
+        jnp.sum(image * left, axis=1, keepdims=True),
+        energy,
+    )
+    lane = lax.broadcasted_iota(jnp.int32, (columns, LANES), 1)
+    small = selected(corner, names_ref[...])
+    for at, value in enumerate(sums):
+        small = jnp.where(lane == LANES - len(sums) + at, value, small)
+    small_ref[...] = small
+    up_ref[:, half:] = jnp.concatenate(thirds(small), axis=1)
+
+
+def relay_kernel(up_own_ref, up_ref, down_ref, far_ref, own_ref, out_ref):
+    lower = lax.axis_index("row") == 0
+    half = up_ref.shape[1] - 3 * LANES
+    total = own_ref[...] + pieces_sum(up_ref, half, 3)
+    total = total + down_ref[...] + far_ref[...]
+    out_ref[:, :half] = jnp.where(lower, up_own_ref[:, :half], up_ref[:, :half])
+    out_ref[:, half:] = jnp.concatenate(thirds(total), axis=1)
+
+
+def close_kernel(
+    solver_ref,
+    maps_ref,
+    live_ref,
+    loaded_ref,
+    weights_ref,
+    image_ref,
+    next_ref,
+    mine_ref,
+    theirs_ref,
+    solution_ref,
+    residual_ref,
+):
+    lower = lax.axis_index("row") == 0
+    columns, half = loaded_ref.shape
+    mine, theirs = pieces_sum(mine_ref, half, 3), pieces_sum(theirs_ref, half, 3)
+    total = jnp.where(lower, mine, theirs)
+    lane = lax.broadcasted_iota(jnp.int32, (columns, LANES), 1)
+    coarse = jnp.where(lane < LANES - 4, total, 0.0)
+    backs = solved_backs(coarse, solver_ref[:, : 2 * LANES]).astype(BF16)
+    solved = solved_backs(coarse, solver_ref[:, 2 * LANES :])
+    fix = nn(backs, maps_ref[:, :half])
+    image_next = mine_ref[:, :half].astype(F32) + theirs_ref[:, :half].astype(F32) + fix
+    image_next = jnp.where(live_ref[0:1] > 0.0, image_next, 0.0)
+
+    def column(values, at):
+        return jnp.sum(jnp.where(lane == LANES - 4 + at, values, 0.0), axis=1, keepdims=True)
+
+    gamma = column(total, 0)
+    delta = column(total, 1)
+    cross = column(total, 2)
+    energy = column(mine + theirs, 3) + jnp.sum(coarse * solved, axis=1, keepdims=True)
+    alpha = gamma / delta
+    gamma_next = gamma - 2.0 * alpha * delta + alpha * alpha * cross
+    ratio = gamma_next / gamma
+    grown = 1.0 + ratio
+    curvature = grown * grown * delta - 2.0 * grown * alpha * cross + alpha * alpha * energy
+    alpha_next = gamma_next / curvature
+    loaded = loaded_ref[...]
+    first = loaded * weights_ref[...]
+    direction = grown * first - alpha * next_ref[...]
+    along = grown * image_ref[...] - alpha * image_next
+    solution_ref[...] = alpha * first + alpha_next * direction
+    residual_ref[...] = loaded - alpha * image_ref[...] - alpha_next * along
+
+
+def ring(
+    loads,
+    weights,
+    dual_ops,
+    corner_maps,
+    coarse_inverse,
+    corner_ids,
+    iface_sizes,
+    left_partner,
+    right_partner,
+):
+    count = lax.axis_size("sub")
+    sides = lax.axis_size("row")
+    columns, half = loads.shape[1:]
+    corners = corner_maps.shape[1]
+    operator = dual_ops[0]
+    own_map = corner_maps[0]
+    loaded = loads[0]
+    block = operator.shape[0]
+    shape = jax.ShapeDtypeStruct
+    grid = ("sub", "row")
+    big = 2 * columns * block * 2 * half
+
+    def pairs(target):
+        listed = []
+        for at in range(count):
+            for side in range(sides):
+                to_at, to_side = target(at, side)
+                listed.append((at * sides + side, (to_at % count) * sides + to_side))
+        return listed
+
+    across = pairs(lambda at, side: (at, 1 - side))
+    along = pairs(lambda at, side: (at - 1, 0) if side == 0 else (at + 1, 1))
+    slant = pairs(lambda at, side: (at - 1, 1) if side == 0 else (at + 1, 0))
+
+    def call(kernel, operands, outs, scratch=(), flops=0, moved=0, room=4):
+        specs, placed = [], []
+        for operand in operands:
+            held = isinstance(operand, tuple)
+            specs.append(HBM if held else VMEM)
+            placed.append(
+                pltpu.with_memory_space_constraint(operand[0], pltpu.HBM) if held else operand
+            )
+        return pl.pallas_call(
+            kernel,
+            in_specs=specs,
+            out_specs=[VMEM] * len(outs),
+            out_shape=[shape(*out) for out in outs],
+            scratch_shapes=scratch,
+            cost_estimate=cost(flops, moved),
+            compiler_params=pltpu.CompilerParams(vmem_limit_bytes=room << 20),
+        )(*placed)
+
+    rows = columns + corners + 8
+    arguments = (weights, corner_ids, coarse_inverse, right_partner, left_partner)
+    pack, load, live, scale, ids, inverse, right_map, left_map = call(
+        open_kernel,
+        [(array,) for array in (iface_sizes, loaded, own_map, *arguments)],
+        [((rows, half), BF16), ((columns, half), F32), ((8, half), F32)]
+        + [(array.shape, array.dtype) for array in arguments],
+        scratch=[
+            pltpu.SMEM(iface_sizes.shape, jnp.int32),
+            pltpu.VMEM(loaded.shape, F32),
+            pltpu.VMEM(own_map.shape, BF16),
+            pltpu.SemaphoreType.DMA((8,)),
+        ],
+        moved=4 * rows * half,
+    )
+    pack_slant = lax.ppermute(pack, grid, slant)
+    pack_along = lax.ppermute(pack, grid, along)
+    map_across = lax.ppermute(own_map, grid, across)
+    right_hot, order, left_hot, square, cross, local_left, turned = call(
+        select_kernel,
+        [right_map, left_map, pack, (operator,)],
+        [((half, half), BF16)] * 3
+        + [((block, half), BF16)] * 2
+        + [((columns, block), F32), ((columns, half), BF16)],
+        scratch=[pltpu.SemaphoreType.DMA((2,))],
+        flops=big,
+        moved=4 * half * half,
+        room=14,
+    )
+    (send,) = call(
+        first_kernel,
+        [
+            ids,
+            square,
+            cross,
+            right_hot,
+            order,
+            local_left,
+            turned,
+            pack,
+            map_across,
+            pack_along,
+            pack_slant,
+        ],
+        [((columns, half + 2 * LANES), BF16)],
+        flops=2 * big,
+        moved=4 * block * half,
+        room=14,
+    )
+    send_slant = lax.ppermute(send, grid, slant)
+    send_along = lax.ppermute(send, grid, along)
+    send_across = lax.ppermute(send, grid, across)
+    maps, solver, scale_right, names = call(
+        order_kernel,
+        [ids, inverse, order, left_hot, pack, map_across, pack_along, pack_slant],
+        [
+            ((LANES, 2 * half), BF16),
+            ((LANES, 4 * LANES), BF16),
+            ((1, half), F32),
+            ((LANES, LANES), BF16),
+        ],
+        flops=4 * corners * half * half,
+        moved=4 * half * half,
+        room=8,
+    )
+    image, following, up, small = call(
+        second_kernel,
+        [
+            names,
+            solver,
+            maps,
+            right_hot,
+            order,
+            square,
+            cross,
+            live,
+            load,
+            scale,
+            scale_right,
+            send,
+            send_across,
+            send_along,
+            send_slant,
+        ],
+        [
+            ((columns, half), F32),
+            ((columns, half), F32),
+            ((columns, half + 3 * LANES), BF16),
+            ((columns, LANES), F32),
+        ],
+        flops=2 * big,
+        moved=4 * block * half,
+        room=14,
+    )
+    far_in = shifted(small, "sub", 2)
+    down_in = shifted(small, "sub", -1)
+    up_in = shifted(up, "sub", 1)
+    (mine,) = call(
+        relay_kernel,
+        [up, up_in, down_in, far_in, small],
+        [((columns, half + 3 * LANES), BF16)],
+        moved=8 * columns * half,
+    )
+    theirs = lax.ppermute(mine, grid, across)
+    solution, residual = call(
+        close_kernel,
+        [solver, maps, live, load, scale, image, following, mine, theirs],
+        [((columns, half), F32), ((columns, half), F32)],
+        moved=24 * columns * half,
+    )
+    return solution[None], residual[None]
+
+
+def per_device(*arrays):
+    loads, _, dual_ops, corner_maps, coarse_inverse = arrays[:5]
+    half = loads.shape[2]
+    neighbourly = lax.axis_size("sub") == 4 and lax.axis_size("row") == 2
+    sided = dual_ops.shape[1] == half and half % LANES == 0
+    narrow = coarse_inverse.shape[0] + 4 <= LANES and 3 * corner_maps.shape[1] <= LANES
+    if neighbourly and sided and narrow and ITERS == 2:
+        return ring(*arrays)
+    return general(*arrays)
+
+
 def solution(mesh):
     placed = (
         P(("parts", "sub"), "col", None),

time: 137 us -> 35.2 us (0.26)
  blocking collectives: 65.9 us -> 0 us
  matrix products: 22.3 us -> 0 us
  local copies, waits for them, and re-layouts: 22.1 us -> 0 us
  other arithmetic: 8.41 us -> 0 us
  Pallas kernels: 0 us -> 8.38 us
  waiting for transfers between devices: 3.74 us -> 9.61 us
  starting transfers between devices: 11.4 us -> 16.4 us
  between operations: 2.25 us -> 0.67 us
    psum x4 -> x0, blocking collectives: 56.7 us -> none  [the longest x2 37.5 us: apply_operator(): coarse = lax.psum(scattered, ('sub', 'row'))]
    dot_general x26 -> x0, matrix products: 22.3 us -> none  [the longest x16 20.7 us: one_tile(): lax.dot_general(vector, piece, (((1,), (1,)), ((), ())), preferred_elemen...]
    gather x11 -> x0, local copies, waits for them, and re-layouts: 19.4 us -> none  [the longest x4 5.95 us: apply_operator(): jnp.take(arrived_right, right_map, axis=1)]
    ppermute x0 -> x7, starting transfers between devices: none -> 12 us  [the longest x1 6.07 us: ring(): pack_slant = lax.ppermute(pack, grid, slant)]
    all_gather x2 -> x0, blocking collectives: 9.15 us -> none  [apply_operator(): lax.all_gather(united.astype(jnp.bfloat16), 'row', axis=1, tiled=True)]
    pallas_call x0 -> x7, Pallas kernels: none -> 8.38 us  [call(): pl.pallas_call(kernel, in_specs=specs, out_specs=[VMEM] * len(outs), out_...]
    ppermute x0 -> x7, waiting for transfers between devices: none -> 7.48 us  [the longest x1 2.33 us: ring(): theirs = lax.ppermute(mine, grid, across)]
    ppermute x6 -> x3, starting transfers between devices: 11.4 us -> 4.32 us  [shifted(): return lax.ppermute(value, axis, pairs)]
  transfers between devices with their start and end apart: 6 -> 10, of which waited for: 2 -> 6; matrix products, arithmetic and copies ran while one was open for 14% -> 0% of each run, Pallas kernels for 0% -> 9%
where the time goes in v3:
time: 35.2 us; the launch traced here: 35 us
  starting transfers between devices  16.4 us (47%)
  waiting for transfers between devices  9.61 us (27%)
  Pallas kernels  8.38 us (24%)
  between operations  0.67 us (2%)
    pallas_call x7, Pallas kernels, call(): pl.pallas_call(kernel, in_specs=specs, out_specs=[VMEM] * len(outs), out_...  8.38 us
    ppermute x1, starting transfers between devices, ring(): pack_slant = lax.ppermute(pack, grid, slant)  6.07 us
    ppermute x3, starting transfers between devices, shifted(): return lax.ppermute(value, axis, pairs)  4.32 us
    ppermute x1, starting transfers between devices, ring(): send_slant = lax.ppermute(send, grid, slant)  3.58 us
    ppermute x1, waiting for transfers between devices, ring(): theirs = lax.ppermute(mine, grid, across)  2.33 us
    ppermute x3, waiting for transfers between devices, shifted(): return lax.ppermute(value, axis, pairs)  2.12 us
    ppermute x1, waiting for transfers between devices, ring(): send_slant = lax.ppermute(send, grid, slant)  2.08 us
    ppermute x1, waiting for transfers between devices, ring(): map_across = lax.ppermute(own_map, grid, across)  2.05 us
  transfers between devices with their start and end apart: 10, of which 6 were waited for; matrix products, arithmetic and copies ran while one was open for 0% of the time, Pallas kernels for 9%

profile of v3, /device:TPU:0, one launch (start us, length us, event | category | flops | bytes accessed | tf_op | source)
XLA Modules:
  0.0 35.0 jit_solution(2051673647433419619)
XLA Ops:
  0.6 1.0 %shard_map.104 = (bf16[48,1024]{1,0:T(8,128)(2,1)S(1)}, f32[16,1024]{1,0:T(8,128)S(1)}, f32[8,1024]{1,0:T(8,128)S(1)}, f32[1,1024]{1,0:T(1,128)S(1)}, s32[4,24]{...) custom-call(s32[4]{0:T(128)} %sizes_in.1, f32[16,1024]{1,0:T(8,128)} %bitcast.6, ...), custom_call_target="tpu_custom_call" | custom-call | bytes 196608 | tf_op jit(solution)/shard_map/pallas_call | solution.py:582
  1.6 6.1 %collective-permute-start.2 = (bf16[48,1024]{1,0:T(8,128)(2,1)S(1)}, bf16[48,1024]{1,0:T(8,128)(2,1)S(1)}, u32[]{:S(2)}, u32[]{:S(2)}) collective-permute-start(bf16[48,1024]{1,0:T(8,128)(2,1)S(1)} %get-tuple-element.31.pack_ref.own_pack_ref), channel_id=1, source_target_pairs={{0,14},{2,4},{4,2},{6,8},{8,6},{10,12},{12,10},{14,0},{1,15},{3,5}... | collective-permute-start | bytes 294920 | tf_op jit(solution)/shard_map/ppermute | solution.py:607
  7.7 0.4 %collective-permute-start.1 = (bf16[48,1024]{1,0:T(8,128)(2,1)S(1)}, bf16[48,1024]{1,0:T(8,128)(2,1)S(1)}, u32[]{:S(2)}, u32[]{:S(2)}) collective-permute-start(bf16[48,1024]{1,0:T(8,128)(2,1)S(1)} %get-tuple-element.31.pack_ref.own_pack_ref), channel_id=1, source_target_pairs={{0,12},{2,6},{4,0},{6,10},{8,4},{10,14},{12,8},{14,2},{1,13},{3,7}... | collective-permute-start | bytes 294920 | tf_op jit(solution)/shard_map/ppermute | solution.py:608
  8.1 0.0 collective-permute-start
  8.1 2.2 %shard_map.105 = (bf16[1024,1024]{1,0:T(8,128)(2,1)S(1)}, bf16[1024,1024]{1,0:T(8,128)(2,1)S(1)}, bf16[1024,1024]{1,0:T(8,128)(2,1)S(1)}, bf16[1024,1024]{1,0:T(...) custom-call(s32[1,1024]{1,0:T(1,128)S(1)} %get-tuple-element.29.right_ref, ...), custom_call_target="tpu_custom_call" | custom-call | flops 67108864 | bytes 4194304 | tf_op jit(solution)/shard_map/pallas_call | solution.py:582
  10.4 2.0 %collective-permute-done.across_ref = bf16[24,1024]{1,0:T(8,128)(2,1)S(1)} collective-permute-done((bf16[24,1024]{1,0:T(8,128)(2,1)}, bf16[24,1024]{1,0:T(8,128)(2,1)S(1)}, u32[]{:S(2)}, u32[]{:S(2)}) %collective-permute-start) | collective-permute-done | bytes 49184 | tf_op jit(solution)/shard_map/ppermute | solution.py:609
  12.4 0.0 collective-permute-done.2.slant_ref
  12.4 0.0 collective-permute-done.1.along_ref
  12.4 1.3 %shard_map.107.own_ref = bf16[16,1280]{1,0:T(8,128)(2,1)S(1)} custom-call(s32[4,24]{1,0:T(4,128)S(1)} %get-tuple-element.27.ids_ref, bf16[1024,1024]{1,0:T(8,128)(2,1)S(1)} %get-tuple-element.41.square_ref, bf16[1024,1024]{1,0:T(8,128)(2,1)S(1)} %get-tuple-element.42.cross_ref, bf16[1024,1024]{1,0:T(8,128)(2,1)S(1)} %get-tuple-element.40.right_hot_ref, ...), custom_call_target="tpu_custom_call" | custom-call | flops 134217728 | bytes 4194304 | tf_op jit(solution)/shard_map/pallas_call | solution.py:582
  13.7 3.6 %collective-permute-start.5 = (bf16[16,1280]{1,0:T(8,128)(2,1)S(1)}, bf16[16,1280]{1,0:T(8,128)(2,1)S(1)}, u32[]{:S(2)}, u32[]{:S(2)}) collective-permute-start(bf16[16,1280]{1,0:T(8,128)(2,1)S(1)} %shard_map.107.own_ref), channel_id=1, source_target_pairs={{0,14},{2,4},{4,2},{6,8},{8,6},{10,12},{12,10},{14,0},{1,15},{3,5}... | collective-permute-start | bytes 122888 | tf_op jit(solution)/shard_map/ppermute | solution.py:641
  17.3 0.2 collective-permute-start.4
  17.5 0.0 collective-permute-start.3
  17.5 0.9 %shard_map.106 = (bf16[128,2048]{1,0:T(8,128)(2,1)S(1)}, bf16[128,512]{1,0:T(8,128)(2,1)S(1)}, f32[1,1024]{1,0:T(1,128)S(1)}, bf16[128,128]{1,0:T(8,128)(2,1)S(1)}) custom-call(s32[4,24]{1,0:T(4,128)S(1)} %get-tuple-element.27.ids_ref, f32[48,48]{1,0:T(8,128)S(1)} %get-tuple-element.28.inverse_ref, bf16[1024,1024]{1,0:T(8,128)(2,1)S(1)} %get-tuple-element.32.order_ref, ...), custom_call_target="tpu_custom_call" | custom-call | flops 100663296 | bytes 4194304 | tf_op jit(solution)/shard_map/pallas_call | solution.py:582
  18.4 2.1 %collective-permute-done.5.slant_ref = bf16[16,1280]{1,0:T(8,128)(2,1)S(1)} collective-permute-done((bf16[16,1280]{1,0:T(8,128)(2,1)S(1)}, bf16[16,1280]{1,0:T(8,128)(2,1)S(1)}, u32[]{:S(2)}, u32[]{:S(2)}) %collective-permute-start.5) | collective-permute-done | bytes 40992 | tf_op jit(solution)/shard_map/ppermute | solution.py:641
  20.5 0.9 %collective-permute-done.4.along_ref = bf16[16,1280]{1,0:T(8,128)(2,1)S(1)} collective-permute-done((bf16[16,1280]{1,0:T(8,128)(2,1)S(1)}, bf16[16,1280]{1,0:T(8,128)(2,1)S(1)}, u32[]{:S(2)}, u32[]{:S(2)}) %collective-permute-start.4) | collective-permute-done | bytes 40992 | tf_op jit(solution)/shard_map/ppermute | solution.py:642
  21.3 0.2 collective-permute-done.3.across_ref
  21.5 2.0 %shard_map.108 = (f32[16,1024]{1,0:T(8,128)S(1)}, f32[16,1024]{1,0:T(8,128)S(1)}, bf16[16,1408]{1,0:T(8,128)(2,1)S(1)}, f32[16,128]{1,0:T(8,128)S(1)}) custom-call(bf16[128,128]{1,0:T(8,128)(2,1)S(1)} %get-tuple-element.39.names_ref, bf16[128,512]{1,0:T(8,128)(2,1)S(1)} %get-tuple-element.34.solver_ref, bf16[128,2048]{1,0:T(8,128)(2,1)S(1)} %get-tuple-element.35.maps_ref, ...), custom_call_target="tpu_custom_call" | custom-call | flops 134217728 | bytes 4194304 | tf_op jit(solution)/shard_map/pallas_call | solution.py:582
  23.5 1.9 %collective-permute-start.6 = (bf16[16,1408]{1,0:T(8,128)(2,1)S(1)}, bf16[16,1408]{1,0:T(8,128)(2,1)S(1)}, u32[]{:S(2)}, u32[]{:S(2)}) collective-permute-start(bf16[16,1408]{1,0:T(8,128)(2,1)S(1)} %get-tuple-element.48.up_own_ref), channel_id=1, source_target_pairs={{0,4},{4,8},{8,12},{12,0},{1,5},{5,9},{9,13},{13,1},{2,6},{6,10},{... | collective-permute-start | bytes 135176 | tf_op jit(solution)/shard_map/ppermute | solution.py:21
  25.4 0.8 %collective-permute-start.8 = (f32[16,128]{1,0:T(8,128)S(1)}, f32[16,128]{1,0:T(8,128)S(1)}, u32[]{:S(2)}, u32[]{:S(2)}) collective-permute-start(f32[16,128]{1,0:T(8,128)S(1)} %get-tuple-element.49.own_ref), channel_id=1, source_target_pairs={{0,8},{4,12},{8,0},{12,4},{1,9},{5,13},{9,1},{13,5},{2,10},{6,14},... | collective-permute-start | bytes 24584 | tf_op jit(solution)/shard_map/ppermute | solution.py:21
  26.2 1.7 %collective-permute-start.7 = (f32[16,128]{1,0:T(8,128)S(1)}, f32[16,128]{1,0:T(8,128)S(1)}, u32[]{:S(2)}, u32[]{:S(2)}) collective-permute-start(f32[16,128]{1,0:T(8,128)S(1)} %get-tuple-element.49.own_ref), channel_id=1, source_target_pairs={{0,12},{4,0},{8,4},{12,8},{1,13},{5,1},{9,5},{13,9},{2,14},{6,2},{... | collective-permute-start | bytes 24584 | tf_op jit(solution)/shard_map/ppermute | solution.py:21
  27.8 2.1 %collective-permute-done.8.far_ref = f32[16,128]{1,0:T(8,128)S(1)} collective-permute-done((f32[16,128]{1,0:T(8,128)S(1)}, f32[16,128]{1,0:T(8,128)S(1)}, u32[]{:S(2)}, u32[]{:S(2)}) %collective-permute-start.8) | collective-permute-done | bytes 8224 | tf_op jit(solution)/shard_map/ppermute | solution.py:21
  30.0 0.0 collective-permute-done.7.down_ref
  30.0 0.0 collective-permute-done.6.up_ref
  30.0 1.8 %collective-permute-start.9 = (bf16[16,1408]{1,0:T(8,128)(2,1)S(1)}, bf16[16,1408]{1,0:T(8,128)(2,1)S(1)}, u32[]{:S(2)}, u32[]{:S(2)}) collective-permute-start(bf16[16,1408]{1,0:T(8,128)(2,1)S(1)} %shard_map.109.mine_ref), channel_id=1, source_target_pairs={{0,2},{2,0},{4,6},{6,4},{8,10},{10,8},{12,14},{14,12},{1,3},{3,1},... | collective-permute-start | bytes 135176 | tf_op jit(solution)/shard_map/ppermute | solution.py:695
  31.8 2.3 %collective-permute-done.9.theirs_ref = bf16[16,1408]{1,0:T(8,128)(2,1)S(1)} collective-permute-done((bf16[16,1408]{1,0:T(8,128)(2,1)S(1)}, bf16[16,1408]{1,0:T(8,128)(2,1)S(1)}, u32[]{:S(2)}, u32[]{:S(2)}) %collective-permute-start.9) | collective-permute-done | bytes 45088 | tf_op jit(solution)/shard_map/ppermute | solution.py:695
  34.1 0.9 %shard_map.110 = (f32[16,1024]{1,0:T(8,128)}, f32[16,1024]{1,0:T(8,128)}) custom-call(bf16[128,512]{1,0:T(8,128)(2,1)S(1)} %get-tuple-element.34.solver_ref, bf16[128,2048]{1,0:T(8,128)(2,1)S(1)} %get-tuple-element.35.maps_ref, f32[8,1024]{1,0:T(8,128)S(1)} %get-tuple-element.36.live_ref, f32[16,1024]{1,0:T(8,128)S(1)} %get-tuple-element.37.loaded_ref, ...), custom_call_target="tpu_custom_call" | custom-call | bytes 393216 | tf_op jit(solution)/shard_map/pallas_call | solution.py:582
  (1 shorter events, 0.0 us)
Async XLA Ops:
  1.6 10.8 %collective-permute-start.2 = (bf16[48,1024]{1,0:T(8,128)(2,1)S(1)}, bf16[48,1024]{1,0:T(8,128)(2,1)S(1)}, u32[]{:S(2)}, u32[]{:S(2)}) collective-permute-start(bf16[48,1024]{1,0:T(8,128)(2,1)S(1)} %get-tuple-element.31.pack_ref.own_pack_ref), channel_id=1, source_target_pairs={{0,14},{2,4},{4,2},{6,8},{8,6},{10,12},{12,10},{14,0},{1,15},{3,5}... | collective-permute-start | bytes 294920 | tf_op jit(solution)/shard_map/ppermute | solution.py:607
  7.7 4.8 %collective-permute-start.1 = (bf16[48,1024]{1,0:T(8,128)(2,1)S(1)}, bf16[48,1024]{1,0:T(8,128)(2,1)S(1)}, u32[]{:S(2)}, u32[]{:S(2)}) collective-permute-start(bf16[48,1024]{1,0:T(8,128)(2,1)S(1)} %get-tuple-element.31.pack_ref.own_pack_ref), channel_id=1, source_target_pairs={{0,12},{2,6},{4,0},{6,10},{8,4},{10,14},{12,8},{14,2},{1,13},{3,7}... | collective-permute-start | bytes 294920 | tf_op jit(solution)/shard_map/ppermute | solution.py:608
  8.1 4.3 %collective-permute-start = (bf16[24,1024]{1,0:T(8,128)(2,1)}, bf16[24,1024]{1,0:T(8,128)(2,1)S(1)}, u32[]{:S(2)}, u32[]{:S(2)}) collective-permute-start(bf16[24,1024]{1,0:T(8,128)(2,1)} %bitcast.8), channel_id=1, source_target_pairs={{0,2},{2,0},{4,6},{6,4},{8,10},{10,8},{12,14},{14,12},{1,3},{3,1},... | collective-permute-start | bytes 147464 | tf_op jit(solution)/shard_map/ppermute | solution.py:609
  13.7 6.7 %collective-permute-start.5 = (bf16[16,1280]{1,0:T(8,128)(2,1)S(1)}, bf16[16,1280]{1,0:T(8,128)(2,1)S(1)}, u32[]{:S(2)}, u32[]{:S(2)}) collective-permute-start(bf16[16,1280]{1,0:T(8,128)(2,1)S(1)} %shard_map.107.own_ref), channel_id=1, source_target_pairs={{0,14},{2,4},{4,2},{6,8},{8,6},{10,12},{12,10},{14,0},{1,15},{3,5}... | collective-permute-start | bytes 122888 | tf_op jit(solution)/shard_map/ppermute | solution.py:641
  17.3 4.0 %collective-permute-start.4 = (bf16[16,1280]{1,0:T(8,128)(2,1)S(1)}, bf16[16,1280]{1,0:T(8,128)(2,1)S(1)}, u32[]{:S(2)}, u32[]{:S(2)}) collective-permute-start(bf16[16,1280]{1,0:T(8,128)(2,1)S(1)} %shard_map.107.own_ref), channel_id=1, source_target_pairs={{0,12},{2,6},{4,0},{6,10},{8,4},{10,14},{12,8},{14,2},{1,13},{3,7}... | collective-permute-start | bytes 122888 | tf_op jit(solution)/shard_map/ppermute | solution.py:642
  17.5 4.0 %collective-permute-start.3 = (bf16[16,1280]{1,0:T(8,128)(2,1)S(1)}, bf16[16,1280]{1,0:T(8,128)(2,1)S(1)}, u32[]{:S(2)}, u32[]{:S(2)}) collective-permute-start(bf16[16,1280]{1,0:T(8,128)(2,1)S(1)} %shard_map.107.own_ref), channel_id=1, source_target_pairs={{0,2},{2,0},{4,6},{6,4},{8,10},{10,8},{12,14},{14,12},{1,3},{3,1},... | collective-permute-start | bytes 122888 | tf_op jit(solution)/shard_map/ppermute | solution.py:643
  23.5 6.4 %collective-permute-start.6 = (bf16[16,1408]{1,0:T(8,128)(2,1)S(1)}, bf16[16,1408]{1,0:T(8,128)(2,1)S(1)}, u32[]{:S(2)}, u32[]{:S(2)}) collective-permute-start(bf16[16,1408]{1,0:T(8,128)(2,1)S(1)} %get-tuple-element.48.up_own_ref), channel_id=1, source_target_pairs={{0,4},{4,8},{8,12},{12,0},{1,5},{5,9},{9,13},{13,1},{2,6},{6,10},{... | collective-permute-start | bytes 135176 | tf_op jit(solution)/shard_map/ppermute | solution.py:21
  25.4 4.5 %collective-permute-start.8 = (f32[16,128]{1,0:T(8,128)S(1)}, f32[16,128]{1,0:T(8,128)S(1)}, u32[]{:S(2)}, u32[]{:S(2)}) collective-permute-start(f32[16,128]{1,0:T(8,128)S(1)} %get-tuple-element.49.own_ref), channel_id=1, source_target_pairs={{0,8},{4,12},{8,0},{12,4},{1,9},{5,13},{9,1},{13,5},{2,10},{6,14},... | collective-permute-start | bytes 24584 | tf_op jit(solution)/shard_map/ppermute | solution.py:21
  26.2 3.8 %collective-permute-start.7 = (f32[16,128]{1,0:T(8,128)S(1)}, f32[16,128]{1,0:T(8,128)S(1)}, u32[]{:S(2)}, u32[]{:S(2)}) collective-permute-start(f32[16,128]{1,0:T(8,128)S(1)} %get-tuple-element.49.own_ref), channel_id=1, source_target_pairs={{0,12},{4,0},{8,4},{12,8},{1,13},{5,1},{9,5},{13,9},{2,14},{6,2},{... | collective-permute-start | bytes 24584 | tf_op jit(solution)/shard_map/ppermute | solution.py:21
  30.0 4.1 %collective-permute-start.9 = (bf16[16,1408]{1,0:T(8,128)(2,1)S(1)}, bf16[16,1408]{1,0:T(8,128)(2,1)S(1)}, u32[]{:S(2)}, u32[]{:S(2)}) collective-permute-start(bf16[16,1408]{1,0:T(8,128)(2,1)S(1)} %shard_map.109.mine_ref), channel_id=1, source_target_pairs={{0,2},{2,0},{4,6},{6,4},{8,10},{10,8},{12,14},{14,12},{1,3},{3,1},... | collective-permute-start | bytes 135176 | tf_op jit(solution)/shard_map/ppermute | solution.py:695

commit v4 on v3

--- a/solution.py
+++ b/solution.py
@@ -266,6 +266,12 @@
     return ref.at[:, pl.ds(pl.multiple_of(side * half, half), half)]
 
 
+def turn(source_ref, target_ref):
+    for at in range(0, source_ref.shape[1], LANES):
+        block = slice(at, at + LANES)
+        target_ref[block, :] = jnp.transpose(source_ref[:, block])
+
+
 def select_kernel(
     right_ref,
     left_ref,
@@ -276,6 +282,7 @@
     left_hot_ref,
     square_ref,
     cross_ref,
+    early_ref,
     local_ref,
     turned_ref,
     sems,
@@ -297,19 +304,29 @@
         cross.start()
         square.start()
 
+    short = jnp.int16
     right = right_ref[...]
     tall = jnp.transpose(jnp.broadcast_to(right, (8, half)).astype(F32))[:, 0:1].astype(jnp.int32)
-    names = lax.broadcasted_iota(jnp.int32, (LANES, half), 1)
+    tall = jnp.broadcast_to(tall, (half, LANES)).astype(short)
+    names = lax.broadcasted_iota(jnp.int32, (LANES, LANES), 1)
+    full, none = jnp.ones((LANES, half), BF16), jnp.zeros((LANES, half), BF16)
+    narrow_full, narrow_none = jnp.ones((LANES, LANES), BF16), jnp.zeros((LANES, LANES), BF16)
     for at in range(half // LANES):
         rows = slice(at * LANES, (at + 1) * LANES)
-        order_ref[rows, :] = (names == tall[rows]).astype(F32).astype(BF16)
+        for block in range(half // LANES):
+            own = (names + block * LANES).astype(short)
+            hit = own == tall[rows]
+            columns_at = slice(block * LANES, (block + 1) * LANES)
+            order_ref[rows, columns_at] = jnp.where(hit, narrow_full, narrow_none)
+    wide_right = jnp.broadcast_to(right, (LANES, half)).astype(short)
+    wide_left = jnp.broadcast_to(left_ref[...], (LANES, half)).astype(short)
 
     def one(at, carry):
         start = pl.multiple_of(at * LANES, LANES)
-        slots = lax.broadcasted_iota(jnp.int32, (LANES, half), 0) + start
+        slots = (lax.broadcasted_iota(jnp.int32, (LANES, half), 0) + start).astype(short)
         rows = pl.ds(start, LANES)
-        right_hot_ref[rows, :] = (slots == right).astype(F32).astype(BF16)
-        left_hot_ref[rows, :] = (slots == left_ref[...]).astype(F32).astype(BF16)
+        right_hot_ref[rows, :] = jnp.where(slots == wide_right, full, none)
+        left_hot_ref[rows, :] = jnp.where(slots == wide_left, full, none)
         return carry
 
     lax.fori_loop(0, half // LANES, one, 0)
@@ -321,6 +338,7 @@
         square.wait()
         local_ref[...] = nn(left, square_ref[...])
         cross.wait()
+        turn(cross_ref, early_ref)
 
     @pl.when(jnp.logical_not(lower))
     def _():
@@ -333,7 +351,7 @@
 def first_kernel(
     ids_ref,
     square_ref,
-    cross_ref,
+    early_ref,
     right_hot_ref,
     order_ref,
     local_ref,
@@ -348,26 +366,27 @@
     corners = ids_ref.shape[1]
     before, subdomain, after = neighbours()
     lower = lax.axis_index("row") == 0
-    left = own_pack_ref[:columns, :]
-    right = jnp.where(lower, along_ref[:columns, :], slant_ref[:columns, :])
-    slotted = nn(right, right_hot_ref[...]).astype(BF16)
+    def coarse_part(own_side, other_side, other):
+        one = nt(own_side, across_ref[...])
+        two = nt(other_side, along_ref[columns:, :])[:, :corners]
+        hot_own = hot_rows(ids_ref, subdomain, LANES)
+        hot_other = hot_rows(ids_ref, other, LANES)
+        high, low = halves(selected(one, hot_own) + selected(two, hot_other))
+        send_ref[:, half:] = jnp.concatenate([high, low], axis=1)
 
     @pl.when(lower)
     def _():
-        send_ref[:, :half] = (local_ref[...] + nt(slotted, cross_ref[...])).astype(BF16)
+        right = along_ref[:columns, :]
+        slotted = nn(right, right_hot_ref[...]).astype(BF16)
+        coarse_part(slotted, right, after)
+        send_ref[:, :half] = (local_ref[...] + nn(slotted, early_ref[...])).astype(BF16)
 
     @pl.when(jnp.logical_not(lower))
     def _():
+        slotted = nn(slant_ref[:columns, :], right_hot_ref[...]).astype(BF16)
+        coarse_part(own_pack_ref[:columns, :], turned_ref[...], before)
         local = (local_ref[...] + nn(slotted, square_ref[...])).astype(BF16)
         send_ref[:, :half] = nn(local, order_ref[...]).astype(BF16)
-
-    one = nt(jnp.where(lower, slotted, left), across_ref[...])
-    beside = along_ref[columns:, :]
-    two = nt(jnp.where(lower, right, turned_ref[...]), beside)[:, :corners]
-    hot_own = hot_rows(ids_ref, subdomain, LANES)
-    hot_other = hot_rows(ids_ref, jnp.where(lower, after, before), LANES)
-    high, low = halves(selected(one, hot_own) + selected(two, hot_other))
-    send_ref[:, half:] = jnp.concatenate([high, low], axis=1)
 
 
 def order_kernel(
@@ -375,6 +394,7 @@
     inverse_ref,
     order_ref,
     left_hot_ref,
+    cross_ref,
     own_pack_ref,
     across_ref,
     along_ref,
@@ -383,6 +403,7 @@
     solver_ref,
     scale_ref,
     names_ref,
+    late_ref,
 ):
     half = order_ref.shape[1]
     corners = ids_ref.shape[1]
@@ -412,6 +433,10 @@
         pieces.extend(halves(tall))
     solver_ref[...] = jnp.concatenate(pieces, axis=1)
 
+    @pl.when(jnp.logical_not(lower))
+    def _():
+        turn(cross_ref, late_ref)
+
 
 def second_kernel(
     names_ref,
@@ -420,7 +445,8 @@
     right_hot_ref,
     order_ref,
     square_ref,
-    cross_ref,
+    early_ref,
+    late_ref,
     live_ref,
     loaded_ref,
     weights_ref,
@@ -451,34 +477,40 @@
     image_ref[...] = image
     next_ref[...] = left
     left_2, right_2 = stacked(left), stacked(right)
-    slotted_2 = nn(right_2, right_hot_ref[...]).astype(BF16)
-    near, far = jnp.where(lower, left_2, slotted_2), jnp.where(lower, slotted_2, left_2)
-    local = folded(nn(near, square_ref[...]) + nt(far, cross_ref[...]))
-    rounded = local.astype(BF16)
-    up_ref[:, :half] = rounded
-
-    @pl.when(jnp.logical_not(lower))
-    def _():
-        up_ref[:, :half] = nn(rounded, order_ref[...]).astype(BF16)
-
-    block = folded(near.astype(F32))
-    energy = jnp.sum(block * local, axis=1, keepdims=True)
-    sided = jnp.where(lower, maps_ref[:, half:], maps_ref[:, :half])
-    corner = folded(nt(jnp.where(lower, right_2, left_2), sided))
     loaded = loaded_ref[...]
     first = loaded * weights_ref[...]
-    sums = (
+    sums = [
         jnp.sum(loaded * first, axis=1, keepdims=True),
         jnp.sum(first * image, axis=1, keepdims=True),
         jnp.sum(image * left, axis=1, keepdims=True),
-        energy,
-    )
+    ]
     lane = lax.broadcasted_iota(jnp.int32, (columns, LANES), 1)
-    small = selected(corner, names_ref[...])
-    for at, value in enumerate(sums):
-        small = jnp.where(lane == LANES - len(sums) + at, value, small)
-    small_ref[...] = small
-    up_ref[:, half:] = jnp.concatenate(thirds(small), axis=1)
+
+    def totals(block, local, corner):
+        energy = jnp.sum(block * local, axis=1, keepdims=True)
+        small = selected(folded(corner), names_ref[...])
+        for at, value in enumerate([*sums, energy]):
+            small = jnp.where(lane == LANES - len(sums) - 1 + at, value, small)
+        small_ref[...] = small
+        up_ref[:, half:] = jnp.concatenate(thirds(small), axis=1)
+
+    @pl.when(lower)
+    def _():
+        local = nn(left_2, square_ref[...])
+        slotted_2 = nn(right_2, right_hot_ref[...]).astype(BF16)
+        corner = nt(right_2, maps_ref[:, half:])
+        local = folded(local + nn(slotted_2, early_ref[...]))
+        up_ref[:, :half] = local.astype(BF16)
+        totals(folded(left_2.astype(F32)), local, corner)
+
+    @pl.when(jnp.logical_not(lower))
+    def _():
+        slotted_2 = nn(right_2, right_hot_ref[...]).astype(BF16)
+        local = nn(left_2, late_ref[...])
+        corner = nt(left_2, maps_ref[:, :half])
+        local = folded(local + nn(slotted_2, square_ref[...]))
+        up_ref[:, :half] = nn(local.astype(BF16), order_ref[...]).astype(BF16)
+        totals(folded(slotted_2.astype(F32)), local, corner)
 
 
 def relay_kernel(up_own_ref, up_ref, down_ref, far_ref, own_ref, out_ref):
@@ -607,23 +639,23 @@
     pack_slant = lax.ppermute(pack, grid, slant)
     pack_along = lax.ppermute(pack, grid, along)
     map_across = lax.ppermute(own_map, grid, across)
-    right_hot, order, left_hot, square, cross, local_left, turned = call(
+    right_hot, order, left_hot, square, cross, early, local_left, turned = call(
         select_kernel,
         [right_map, left_map, pack, (operator,)],
         [((half, half), BF16)] * 3
-        + [((block, half), BF16)] * 2
+        + [((block, half), BF16)] * 3
         + [((columns, block), F32), ((columns, half), BF16)],
         scratch=[pltpu.SemaphoreType.DMA((2,))],
         flops=big,
         moved=4 * half * half,
-        room=14,
+        room=16,
     )
     (send,) = call(
         first_kernel,
         [
             ids,
             square,
-            cross,
+            early,
             right_hot,
             order,
             local_left,
@@ -636,23 +668,24 @@
         [((columns, half + 2 * LANES), BF16)],
         flops=2 * big,
         moved=4 * block * half,
-        room=14,
+        room=16,
     )
     send_slant = lax.ppermute(send, grid, slant)
     send_along = lax.ppermute(send, grid, along)
     send_across = lax.ppermute(send, grid, across)
-    maps, solver, scale_right, names = call(
+    maps, solver, scale_right, names, late = call(
         order_kernel,
-        [ids, inverse, order, left_hot, pack, map_across, pack_along, pack_slant],
+        [ids, inverse, order, left_hot, cross, pack, map_across, pack_along, pack_slant],
         [
             ((LANES, 2 * half), BF16),
             ((LANES, 4 * LANES), BF16),
             ((1, half), F32),
             ((LANES, LANES), BF16),
+            ((half, block), BF16),
         ],
         flops=4 * corners * half * half,
         moved=4 * half * half,
-        room=8,
+        room=12,
     )
     image, following, up, small = call(
         second_kernel,
@@ -663,7 +696,8 @@
             right_hot,
             order,
             square,
-            cross,
+            early,
+            late,
             live,
             load,
             scale,
@@ -681,7 +715,7 @@
         ],
         flops=2 * big,
         moved=4 * block * half,
-        room=14,
+        room=16,
     )
     far_in = shifted(small, "sub", 2)
     down_in = shifted(small, "sub", -1)

time: 35.2 us -> 34.5 us (0.980)
  waiting for transfers between devices: 9.61 us -> 9.19 us
    ppermute x1, waiting for transfers between devices: 2.05 us -> 1.45 us  [ring(): map_across = lax.ppermute(own_map, grid, across)]
  transfers between devices with their start and end apart: 10 -> 10, of which waited for: 6 -> 5; matrix products, arithmetic and copies ran while one was open for 0% -> 0% of each run, Pallas kernels for 9% -> 11%
where the time goes in v4:
time: 34.5 us; the launch traced here: 34.4 us
  starting transfers between devices  16.3 us (47%)
  waiting for transfers between devices  9.19 us (27%)
  Pallas kernels  8.2 us (24%)
  between operations  0.67 us (2%)
    pallas_call x7, Pallas kernels, call(): pl.pallas_call(kernel, in_specs=specs, out_specs=[VMEM] * len(outs), out_...  8.2 us
    ppermute x1, starting transfers between devices, ring(): pack_slant = lax.ppermute(pack, grid, slant)  6.07 us
    ppermute x3, starting transfers between devices, shifted(): return lax.ppermute(value, axis, pairs)  4.45 us
    ppermute x1, starting transfers between devices, ring(): send_slant = lax.ppermute(send, grid, slant)  3.7 us
    ppermute x1, waiting for transfers between devices, ring(): theirs = lax.ppermute(mine, grid, across)  2.5 us
    ppermute x3, waiting for transfers between devices, shifted(): return lax.ppermute(value, axis, pairs)  2.13 us
    ppermute x1, waiting for transfers between devices, ring(): send_slant = lax.ppermute(send, grid, slant)  2.1 us
    ppermute x1, starting transfers between devices, ring(): theirs = lax.ppermute(mine, grid, across)  1.61 us
  transfers between devices with their start and end apart: 10, of which 5 were waited for; matrix products, arithmetic and copies ran while one was open for 0% of the time, Pallas kernels for 11%

profile of v4, /device:TPU:0, one launch (start us, length us, event | category | flops | bytes accessed | tf_op | source)
XLA Modules:
  0.0 34.4 jit_solution(9920589932459129888)
XLA Ops:
  0.6 1.0 %shard_map.104 = (bf16[48,1024]{1,0:T(8,128)(2,1)S(1)}, f32[16,1024]{1,0:T(8,128)S(1)}, f32[8,1024]{1,0:T(8,128)S(1)}, f32[1,1024]{1,0:T(1,128)S(1)}, s32[4,24]{...) custom-call(s32[4]{0:T(128)} %sizes_in.1, f32[16,1024]{1,0:T(8,128)} %bitcast.6, ...), custom_call_target="tpu_custom_call" | custom-call | bytes 196608 | tf_op jit(solution)/shard_map/pallas_call | solution.py:614
  1.6 6.1 %collective-permute-start.2 = (bf16[48,1024]{1,0:T(8,128)(2,1)S(1)}, bf16[48,1024]{1,0:T(8,128)(2,1)S(1)}, u32[]{:S(2)}, u32[]{:S(2)}) collective-permute-start(bf16[48,1024]{1,0:T(8,128)(2,1)S(1)} %get-tuple-element.33.pack_ref.own_pack_ref), channel_id=1, source_target_pairs={{0,14},{2,4},{4,2},{6,8},{8,6},{10,12},{12,10},{14,0},{1,15},{3,5}... | collective-permute-start | bytes 294920 | tf_op jit(solution)/shard_map/ppermute | solution.py:639
  7.7 0.4 %collective-permute-start.1 = (bf16[48,1024]{1,0:T(8,128)(2,1)S(1)}, bf16[48,1024]{1,0:T(8,128)(2,1)S(1)}, u32[]{:S(2)}, u32[]{:S(2)}) collective-permute-start(bf16[48,1024]{1,0:T(8,128)(2,1)S(1)} %get-tuple-element.33.pack_ref.own_pack_ref), channel_id=1, source_target_pairs={{0,12},{2,6},{4,0},{6,10},{8,4},{10,14},{12,8},{14,2},{1,13},{3,7}... | collective-permute-start | bytes 294920 | tf_op jit(solution)/shard_map/ppermute | solution.py:640
  8.1 0.0 collective-permute-start
  8.1 2.8 %shard_map.105 = (bf16[1024,1024]{1,0:T(8,128)(2,1)S(1)}, bf16[1024,1024]{1,0:T(8,128)(2,1)S(1)}, bf16[1024,1024]{1,0:T(8,128)(2,1)S(1)}, bf16[1024,1024]{1,0:T(...) custom-call(s32[1,1024]{1,0:T(1,128)S(1)} %get-tuple-element.31.righ, ...), custom_call_target="tpu_custom_call" | custom-call | flops 67108864 | bytes 4194304 | tf_op jit(solution)/shard_map/pallas_call | solution.py:614
  11.0 1.5 %collective-permute-done.across_ref = bf16[24,1024]{1,0:T(8,128)(2,1)S(1)} collective-permute-done((bf16[24,1024]{1,0:T(8,128)(2,1)}, bf16[24,1024]{1,0:T(8,128)(2,1)S(1)}, u32[]{:S(2)}, u32[]{:S(2)}) %collective-permute-start) | collective-permute-done | bytes 49184 | tf_op jit(solution)/shard_map/ppermute | solution.py:641
  12.4 0.0 collective-permute-done.2.slant_ref
  12.4 0.0 collective-permute-done.1.along_ref
  12.4 1.0 %shard_map.107.own_ref = bf16[16,1280]{1,0:T(8,128)(2,1)S(1)} custom-call(s32[4,24]{1,0:T(4,128)S(1)} %get-tuple-element.29.ids_ref, bf16[1024,1024]{1,0:T(8,128)(2,1)S(1)} %get-tuple-element.44.square_ref, bf16[1024,1024]{1,0:T(8,128)(2,1)S(1)} %get-tuple-element.45.early_ref, bf16[1024,1024]{1,0:T(8,128)(2,1)S(1)} %get-tuple-element.43.right_hot_ref, ...), custom_call_target="tpu_custom_call" | custom-call | flops 134217728 | bytes 4194304 | tf_op jit(solution)/shard_map/pallas_call | solution.py:614
  13.4 3.7 %collective-permute-start.5 = (bf16[16,1280]{1,0:T(8,128)(2,1)S(1)}, bf16[16,1280]{1,0:T(8,128)(2,1)S(1)}, u32[]{:S(2)}, u32[]{:S(2)}) collective-permute-start(bf16[16,1280]{1,0:T(8,128)(2,1)S(1)} %shard_map.107.own_ref), channel_id=1, source_target_pairs={{0,14},{2,4},{4,2},{6,8},{8,6},{10,12},{12,10},{14,0},{1,15},{3,5}... | collective-permute-start | bytes 122888 | tf_op jit(solution)/shard_map/ppermute | solution.py:673
  17.1 0.0 collective-permute-start.4
  17.1 0.0 collective-permute-start.3
  17.1 0.9 %shard_map.106 = (bf16[128,2048]{1,0:T(8,128)(2,1)S(1)}, bf16[128,512]{1,0:T(8,128)(2,1)S(1)}, f32[1,1024]{1,0:T(1,128)S(1)}, bf16[128,128]{1,0:T(8,128)(2,1)S(1)}, bf16[1024,1024]{1,0:T(8,128)(2,1)S(1)}) custom-call(s32[4,24]{1,0:T(4,128)S(1)} %get-tuple-element.29.ids_ref, f32[48,48]{1,0:T(8,128)S(1)} %get-tuple-element.30.inverse_ref, ...), custom_call_target="tpu_custom_call" | custom-call | flops 100663296 | bytes 4194304 | tf_op jit(solution)/shard_map/pallas_call | solution.py:614
  18.0 2.1 %collective-permute-done.5.slant_ref = bf16[16,1280]{1,0:T(8,128)(2,1)S(1)} collective-permute-done((bf16[16,1280]{1,0:T(8,128)(2,1)S(1)}, bf16[16,1280]{1,0:T(8,128)(2,1)S(1)}, u32[]{:S(2)}, u32[]{:S(2)}) %collective-permute-start.5) | collective-permute-done | bytes 40992 | tf_op jit(solution)/shard_map/ppermute | solution.py:673
  20.1 1.0 %collective-permute-done.4.along_ref = bf16[16,1280]{1,0:T(8,128)(2,1)S(1)} collective-permute-done((bf16[16,1280]{1,0:T(8,128)(2,1)S(1)}, bf16[16,1280]{1,0:T(8,128)(2,1)S(1)}, u32[]{:S(2)}, u32[]{:S(2)}) %collective-permute-start.4) | collective-permute-done | bytes 40992 | tf_op jit(solution)/shard_map/ppermute | solution.py:674
  21.1 0.0 collective-permute-done.3.across_ref
  21.1 1.6 %shard_map.108 = (f32[16,1024]{1,0:T(8,128)S(1)}, f32[16,1024]{1,0:T(8,128)S(1)}, bf16[16,1408]{1,0:T(8,128)(2,1)S(1)}, f32[16,128]{1,0:T(8,128)S(1)}) custom-call(bf16[128,128]{1,0:T(8,128)(2,1)S(1)} %get-tuple-element.42.names_ref, bf16[128,512]{1,0:T(8,128)(2,1)S(1)} %get-tuple-element.37.solver_ref, bf16[128,2048]{1,0:T(8,128)(2,1)S(1)} %get-tuple-element.38.maps_ref, ...), custom_call_target="tpu_custom_call" | custom-call | flops 134217728 | bytes 4194304 | tf_op jit(solution)/shard_map/pallas_call | solution.py:614
  22.7 2.0 %collective-permute-start.6 = (bf16[16,1408]{1,0:T(8,128)(2,1)S(1)}, bf16[16,1408]{1,0:T(8,128)(2,1)S(1)}, u32[]{:S(2)}, u32[]{:S(2)}) collective-permute-start(bf16[16,1408]{1,0:T(8,128)(2,1)S(1)} %get-tuple-element.52.up_own_ref), channel_id=1, source_target_pairs={{0,4},{4,8},{8,12},{12,0},{1,5},{5,9},{9,13},{13,1},{2,6},{6,10},{... | collective-permute-start | bytes 135176 | tf_op jit(solution)/shard_map/ppermute | solution.py:21
  24.8 0.8 %collective-permute-start.8 = (f32[16,128]{1,0:T(8,128)S(1)}, f32[16,128]{1,0:T(8,128)S(1)}, u32[]{:S(2)}, u32[]{:S(2)}) collective-permute-start(f32[16,128]{1,0:T(8,128)S(1)} %get-tuple-element.53.own_ref), channel_id=1, source_target_pairs={{0,8},{4,12},{8,0},{12,4},{1,9},{5,13},{9,1},{13,5},{2,10},{6,14},... | collective-permute-start | bytes 24584 | tf_op jit(solution)/shard_map/ppermute | solution.py:21
  25.5 1.6 %collective-permute-start.7 = (f32[16,128]{1,0:T(8,128)S(1)}, f32[16,128]{1,0:T(8,128)S(1)}, u32[]{:S(2)}, u32[]{:S(2)}) collective-permute-start(f32[16,128]{1,0:T(8,128)S(1)} %get-tuple-element.53.own_ref), channel_id=1, source_target_pairs={{0,12},{4,0},{8,4},{12,8},{1,13},{5,1},{9,5},{13,9},{2,14},{6,2},{... | collective-permute-start | bytes 24584 | tf_op jit(solution)/shard_map/ppermute | solution.py:21
  27.2 2.1 %collective-permute-done.8.far_ref = f32[16,128]{1,0:T(8,128)S(1)} collective-permute-done((f32[16,128]{1,0:T(8,128)S(1)}, f32[16,128]{1,0:T(8,128)S(1)}, u32[]{:S(2)}, u32[]{:S(2)}) %collective-permute-start.8) | collective-permute-done | bytes 8224 | tf_op jit(solution)/shard_map/ppermute | solution.py:21
  29.3 0.0 collective-permute-done.7.down_ref
  29.3 0.0 collective-permute-done.6.up_ref
  29.3 1.6 %collective-permute-start.9 = (bf16[16,1408]{1,0:T(8,128)(2,1)S(1)}, bf16[16,1408]{1,0:T(8,128)(2,1)S(1)}, u32[]{:S(2)}, u32[]{:S(2)}) collective-permute-start(bf16[16,1408]{1,0:T(8,128)(2,1)S(1)} %shard_map.109.mine_ref), channel_id=1, source_target_pairs={{0,2},{2,0},{4,6},{6,4},{8,10},{10,8},{12,14},{14,12},{1,3},{3,1},... | collective-permute-start | bytes 135176 | tf_op jit(solution)/shard_map/ppermute | solution.py:729
  31.0 2.5 %collective-permute-done.9.theirs_ref = bf16[16,1408]{1,0:T(8,128)(2,1)S(1)} collective-permute-done((bf16[16,1408]{1,0:T(8,128)(2,1)S(1)}, bf16[16,1408]{1,0:T(8,128)(2,1)S(1)}, u32[]{:S(2)}, u32[]{:S(2)}) %collective-permute-start.9) | collective-permute-done | bytes 45088 | tf_op jit(solution)/shard_map/ppermute | solution.py:729
  33.5 0.9 %shard_map.110 = (f32[16,1024]{1,0:T(8,128)}, f32[16,1024]{1,0:T(8,128)}) custom-call(bf16[128,512]{1,0:T(8,128)(2,1)S(1)} %get-tuple-element.37.solver_ref, bf16[128,2048]{1,0:T(8,128)(2,1)S(1)} %get-tuple-element.38.maps_ref, f32[8,1024]{1,0:T(8,128)S(1)} %get-tuple-element.39.live_ref, f32[16,1024]{1,0:T(8,128)S(1)} %get-tuple-element.40.loaded_ref, ...), custom_call_target="tpu_custom_call" | custom-call | bytes 393216 | tf_op jit(solution)/shard_map/pallas_call | solution.py:614
  (1 shorter events, 0.0 us)
Async XLA Ops:
  1.6 10.8 %collective-permute-start.2 = (bf16[48,1024]{1,0:T(8,128)(2,1)S(1)}, bf16[48,1024]{1,0:T(8,128)(2,1)S(1)}, u32[]{:S(2)}, u32[]{:S(2)}) collective-permute-start(bf16[48,1024]{1,0:T(8,128)(2,1)S(1)} %get-tuple-element.33.pack_ref.own_pack_ref), channel_id=1, source_target_pairs={{0,14},{2,4},{4,2},{6,8},{8,6},{10,12},{12,10},{14,0},{1,15},{3,5}... | collective-permute-start | bytes 294920 | tf_op jit(solution)/shard_map/ppermute | solution.py:639
  7.7 4.8 %collective-permute-start.1 = (bf16[48,1024]{1,0:T(8,128)(2,1)S(1)}, bf16[48,1024]{1,0:T(8,128)(2,1)S(1)}, u32[]{:S(2)}, u32[]{:S(2)}) collective-permute-start(bf16[48,1024]{1,0:T(8,128)(2,1)S(1)} %get-tuple-element.33.pack_ref.own_pack_ref), channel_id=1, source_target_pairs={{0,12},{2,6},{4,0},{6,10},{8,4},{10,14},{12,8},{14,2},{1,13},{3,7}... | collective-permute-start | bytes 294920 | tf_op jit(solution)/shard_map/ppermute | solution.py:640
  8.1 4.3 %collective-permute-start = (bf16[24,1024]{1,0:T(8,128)(2,1)}, bf16[24,1024]{1,0:T(8,128)(2,1)S(1)}, u32[]{:S(2)}, u32[]{:S(2)}) collective-permute-start(bf16[24,1024]{1,0:T(8,128)(2,1)} %bitcast.8), channel_id=1, source_target_pairs={{0,2},{2,0},{4,6},{6,4},{8,10},{10,8},{12,14},{14,12},{1,3},{3,1},... | collective-permute-start | bytes 147464 | tf_op jit(solution)/shard_map/ppermute | solution.py:641
  13.4 6.7 %collective-permute-start.5 = (bf16[16,1280]{1,0:T(8,128)(2,1)S(1)}, bf16[16,1280]{1,0:T(8,128)(2,1)S(1)}, u32[]{:S(2)}, u32[]{:S(2)}) collective-permute-start(bf16[16,1280]{1,0:T(8,128)(2,1)S(1)} %shard_map.107.own_ref), channel_id=1, source_target_pairs={{0,14},{2,4},{4,2},{6,8},{8,6},{10,12},{12,10},{14,0},{1,15},{3,5}... | collective-permute-start | bytes 122888 | tf_op jit(solution)/shard_map/ppermute | solution.py:673
  17.1 4.0 %collective-permute-start.4 = (bf16[16,1280]{1,0:T(8,128)(2,1)S(1)}, bf16[16,1280]{1,0:T(8,128)(2,1)S(1)}, u32[]{:S(2)}, u32[]{:S(2)}) collective-permute-start(bf16[16,1280]{1,0:T(8,128)(2,1)S(1)} %shard_map.107.own_ref), channel_id=1, source_target_pairs={{0,12},{2,6},{4,0},{6,10},{8,4},{10,14},{12,8},{14,2},{1,13},{3,7}... | collective-permute-start | bytes 122888 | tf_op jit(solution)/shard_map/ppermute | solution.py:674
  17.1 4.0 %collective-permute-start.3 = (bf16[16,1280]{1,0:T(8,128)(2,1)S(1)}, bf16[16,1280]{1,0:T(8,128)(2,1)S(1)}, u32[]{:S(2)}, u32[]{:S(2)}) collective-permute-start(bf16[16,1280]{1,0:T(8,128)(2,1)S(1)} %shard_map.107.own_ref), channel_id=1, source_target_pairs={{0,2},{2,0},{4,6},{6,4},{8,10},{10,8},{12,14},{14,12},{1,3},{3,1},... | collective-permute-start | bytes 122888 | tf_op jit(solution)/shard_map/ppermute | solution.py:675
  22.7 6.6 %collective-permute-start.6 = (bf16[16,1408]{1,0:T(8,128)(2,1)S(1)}, bf16[16,1408]{1,0:T(8,128)(2,1)S(1)}, u32[]{:S(2)}, u32[]{:S(2)}) collective-permute-start(bf16[16,1408]{1,0:T(8,128)(2,1)S(1)} %get-tuple-element.52.up_own_ref), channel_id=1, source_target_pairs={{0,4},{4,8},{8,12},{12,0},{1,5},{5,9},{9,13},{13,1},{2,6},{6,10},{... | collective-permute-start | bytes 135176 | tf_op jit(solution)/shard_map/ppermute | solution.py:21
  24.8 4.5 %collective-permute-start.8 = (f32[16,128]{1,0:T(8,128)S(1)}, f32[16,128]{1,0:T(8,128)S(1)}, u32[]{:S(2)}, u32[]{:S(2)}) collective-permute-start(f32[16,128]{1,0:T(8,128)S(1)} %get-tuple-element.53.own_ref), channel_id=1, source_target_pairs={{0,8},{4,12},{8,0},{12,4},{1,9},{5,13},{9,1},{13,5},{2,10},{6,14},... | collective-permute-start | bytes 24584 | tf_op jit(solution)/shard_map/ppermute | solution.py:21
  25.5 3.8 %collective-permute-start.7 = (f32[16,128]{1,0:T(8,128)S(1)}, f32[16,128]{1,0:T(8,128)S(1)}, u32[]{:S(2)}, u32[]{:S(2)}) collective-permute-start(f32[16,128]{1,0:T(8,128)S(1)} %get-tuple-element.53.own_ref), channel_id=1, source_target_pairs={{0,12},{4,0},{8,4},{12,8},{1,13},{5,1},{9,5},{13,9},{2,14},{6,2},{... | collective-permute-start | bytes 24584 | tf_op jit(solution)/shard_map/ppermute | solution.py:21
  29.3 4.1 %collective-permute-start.9 = (bf16[16,1408]{1,0:T(8,128)(2,1)S(1)}, bf16[16,1408]{1,0:T(8,128)(2,1)S(1)}, u32[]{:S(2)}, u32[]{:S(2)}) collective-permute-start(bf16[16,1408]{1,0:T(8,128)(2,1)S(1)} %shard_map.109.mine_ref), channel_id=1, source_target_pairs={{0,2},{2,0},{4,6},{6,4},{8,10},{10,8},{12,14},{14,12},{1,3},{3,1},... | collective-permute-start | bytes 135176 | tf_op jit(solution)/shard_map/ppermute | solution.py:729

commit v5 on v4

--- a/solution.py
+++ b/solution.py
@@ -220,6 +220,7 @@
     right_in,
     left_in,
     pack_ref,
+    skew_ref,
     loaded_ref,
     live_ref,
     weights_ref,
@@ -259,7 +260,10 @@
     first = loaded * scale
     high = scale.astype(BF16).astype(F32)
     spare = jnp.where(which == 0, high, jnp.where(which == 1, scale - high, 0.0))
-    pack_ref[...] = jnp.concatenate([first, maps_ref[...].astype(F32), spare], axis=0).astype(BF16)
+    maps = maps_ref[...].astype(F32)
+    pack_ref[...] = jnp.concatenate([first, maps, spare], axis=0).astype(BF16)
+    short = jnp.concatenate([first, spare], axis=0)
+    skew_ref[...] = jnp.where(lax.axis_index("row") == 0, short, maps).astype(BF16)
 
 
 def side_columns(ref, side, half):
@@ -361,11 +365,13 @@
     along_ref,
     slant_ref,
     send_ref,
+    pair_ref,
 ):
     columns, half = local_ref.shape
     corners = ids_ref.shape[1]
     before, subdomain, after = neighbours()
     lower = lax.axis_index("row") == 0
+
     def coarse_part(own_side, other_side, other):
         one = nt(own_side, across_ref[...])
         two = nt(other_side, along_ref[columns:, :])[:, :corners]
@@ -387,6 +393,13 @@
         coarse_part(own_pack_ref[:columns, :], turned_ref[...], before)
         local = (local_ref[...] + nn(slotted, square_ref[...])).astype(BF16)
         send_ref[:, :half] = nn(local, order_ref[...]).astype(BF16)
+
+    wide = send_ref.shape[1]
+    relayed = along_ref[columns : columns + corners, :].astype(F32)
+    tail = relayed[columns:]
+    tail = jnp.concatenate([tail[:, : half // 2], tail[:, half // 2 :]], axis=0)
+    pair_ref[:, :wide] = send_ref[...]
+    pair_ref[:, wide:] = jnp.concatenate([relayed[:columns], tail], axis=1).astype(BF16)
 
 
 def order_kernel(
@@ -411,17 +424,19 @@
     columns = own_pack_ref.shape[0] - corners - 8
     lower = lax.axis_index("row") == 0
     own, across = own_pack_ref[columns:, :].astype(F32)[:corners], across_ref[...].astype(F32)
-    along, slant = along_ref[columns:, :].astype(F32), slant_ref[columns:, :].astype(F32)
-    ahead, behind = jnp.where(lower, along, slant), jnp.where(lower, slant, along)
-    scale_ref[...] = ahead[corners : corners + 1] + ahead[corners + 1 : corners + 2]
+    along, slant = along_ref[columns:, :].astype(F32), slant_ref[...].astype(F32)
+    behind = jnp.where(lower, slant, along[:corners])
+    ahead = jnp.where(lower, along[:corners], 0.0)
+    scales = jnp.where(lower, along[corners:], slant[columns:])
+    scale_ref[...] = scales[0:1] + scales[1:2]
     raw = jnp.where(lower, across, own).astype(BF16)
     ordered = nn(raw, order_ref[...])
-    turned = nn(behind[:corners].astype(BF16), left_hot_ref[...])
+    turned = nn(behind.astype(BF16), left_hot_ref[...])
     spare = jnp.zeros((LANES - 3 * corners, half), F32)
     blank = jnp.zeros((corners, half), F32)
     mine = jnp.where(lower, own, across)
     maps_ref[:, :half] = jnp.concatenate([turned, mine, blank, spare], axis=0).astype(BF16)
-    maps_ref[:, half:] = jnp.concatenate([blank, ordered, ahead[:corners], spare], axis=0).astype(BF16)
+    maps_ref[:, half:] = jnp.concatenate([blank, ordered, ahead, spare], axis=0).astype(BF16)
     names = hot_names(ids_ref)
     names_ref[...] = names.astype(BF16)
     backs = nn(inverse_ref[...], names[:width], HIGH)
@@ -470,7 +485,15 @@
     fix = nn(backs, maps_ref[...])
     image = jnp.where(lower, own, across) + jnp.where(lower, slant, along) + fix[:, :half]
     image = jnp.where(live_ref[0:1] > 0.0, image, 0.0)
-    image_right = jnp.where(lower, across, own) + jnp.where(lower, along, slant) + fix[:, half:]
+    wide = own_ref.shape[1]
+    half_rows = columns // 2
+    tail = across_ref[:, wide + half :].astype(F32)
+    tail = jnp.concatenate([tail[:half_rows], tail[half_rows:]], axis=1)
+    relayed = jnp.concatenate([across_ref[:, wide : wide + half].astype(F32), tail], axis=0)
+    count = relayed.shape[0]
+    more = nn(backs[:, 2 * count : 3 * count], relayed.astype(BF16))
+    fix_right = fix[:, half:] + jnp.where(lower, 0.0, more)
+    image_right = jnp.where(lower, across, own) + jnp.where(lower, along, slant) + fix_right
     image_right = jnp.where(live_ref[1:2] > 0.0, image_right, 0.0)
     left = weights_ref[...] * image
     right = scale_ref[...] * image_right
@@ -623,10 +646,11 @@
 
     rows = columns + corners + 8
     arguments = (weights, corner_ids, coarse_inverse, right_partner, left_partner)
-    pack, load, live, scale, ids, inverse, right_map, left_map = call(
+    pack, skew, load, live, scale, ids, inverse, right_map, left_map = call(
         open_kernel,
         [(array,) for array in (iface_sizes, loaded, own_map, *arguments)],
-        [((rows, half), BF16), ((columns, half), F32), ((8, half), F32)]
+        [((rows, half), BF16), ((columns + 8, half), BF16)]
+        + [((columns, half), F32), ((8, half), F32)]
         + [(array.shape, array.dtype) for array in arguments],
         scratch=[
             pltpu.SMEM(iface_sizes.shape, jnp.int32),
@@ -636,7 +660,7 @@
         ],
         moved=4 * rows * half,
     )
-    pack_slant = lax.ppermute(pack, grid, slant)
+    pack_slant = lax.ppermute(skew, grid, slant)
     pack_along = lax.ppermute(pack, grid, along)
     map_across = lax.ppermute(own_map, grid, across)
     right_hot, order, left_hot, square, cross, early, local_left, turned = call(
@@ -650,7 +674,8 @@
         moved=4 * half * half,
         room=16,
     )
-    (send,) = call(
+    wide = half + 2 * LANES
+    send, pair = call(
         first_kernel,
         [
             ids,
@@ -665,14 +690,14 @@
             pack_along,
             pack_slant,
         ],
-        [((columns, half + 2 * LANES), BF16)],
+        [((columns, wide), BF16), ((columns, wide + half + half // 2), BF16)],
         flops=2 * big,
         moved=4 * block * half,
         room=16,
     )
     send_slant = lax.ppermute(send, grid, slant)
     send_along = lax.ppermute(send, grid, along)
-    send_across = lax.ppermute(send, grid, across)
+    send_across = lax.ppermute(pair, grid, across)
     maps, solver, scale_right, names, late = call(
         order_kernel,
         [ids, inverse, order, left_hot, cross, pack, map_across, pack_along, pack_slant],
@@ -741,8 +766,10 @@
     half = loads.shape[2]
     neighbourly = lax.axis_size("sub") == 4 and lax.axis_size("row") == 2
     sided = dual_ops.shape[1] == half and half % LANES == 0
+    columns, corners = loads.shape[1], corner_maps.shape[1]
+    fitting = columns % 16 == 0 and corners == columns + columns // 2 and corners == columns + 8
     narrow = coarse_inverse.shape[0] + 4 <= LANES and 3 * corner_maps.shape[1] <= LANES
-    if neighbourly and sided and narrow and ITERS == 2:
+    if neighbourly and sided and fitting and narrow and ITERS == 2:
         return ring(*arrays)
     return general(*arrays)
 

time: 34.5 us -> 34.7 us (level)
  waiting for transfers between devices: 9.19 us -> 10.2 us
  starting transfers between devices: 16.3 us -> 15.4 us
    ppermute x1, starting transfers between devices: 0.45 us -> 5.13 us  [ring(): pack_along = lax.ppermute(pack, grid, along)]
    ppermute x2, starting transfers between devices: 6.07 us -> 2.35 us  [the longest x1 1.91 us: ring(): pack_slant = lax.ppermute(skew, grid, slant)]
    ppermute x2, waiting for transfers between devices: 0.02 us -> 2.02 us  [the longest x1 2.02 us: ring(): pack_slant = lax.ppermute(skew, grid, slant)]
    ppermute x1, starting transfers between devices: 3.7 us -> 1.76 us  [ring(): send_slant = lax.ppermute(send, grid, slant)]
    ppermute x1, waiting for transfers between devices: 1.45 us -> 0.01 us  [ring(): map_across = lax.ppermute(own_map, grid, across)]
    ppermute x1, starting transfers between devices: 0.01 us -> 1.04 us  [ring(): send_along = lax.ppermute(send, grid, along)]
    ppermute x1, waiting for transfers between devices: 0.99 us -> 0.01 us  [ring(): send_along = lax.ppermute(send, grid, along)]
    ppermute x1, waiting for transfers between devices: 2.1 us -> 2.99 us  [ring(): send_slant = lax.ppermute(send, grid, slant)]
where the time goes in v5:
time: 34.7 us; the launch traced here: 34.5 us
  starting transfers between devices  15.4 us (44%)
  waiting for transfers between devices  10.2 us (29%)
  Pallas kernels  8.25 us (24%)
  between operations  0.68 us (2%)
    pallas_call x7, Pallas kernels, call(): pl.pallas_call(kernel, in_specs=specs, out_specs=[VMEM] * len(outs), out_...  8.25 us
    ppermute x1, starting transfers between devices, ring(): pack_along = lax.ppermute(pack, grid, along)  5.13 us
    ppermute x3, starting transfers between devices, shifted(): return lax.ppermute(value, axis, pairs)  3.84 us
    ppermute x1, waiting for transfers between devices, ring(): send_slant = lax.ppermute(send, grid, slant)  2.99 us
    ppermute x1, waiting for transfers between devices, ring(): theirs = lax.ppermute(mine, grid, across)  2.88 us
    ppermute x3, waiting for transfers between devices, shifted(): return lax.ppermute(value, axis, pairs)  2.29 us
    ppermute x1, waiting for transfers between devices, ring(): pack_slant = lax.ppermute(skew, grid, slant)  2.02 us
    ppermute x1, starting transfers between devices, ring(): pack_slant = lax.ppermute(skew, grid, slant)  1.91 us
  transfers between devices with their start and end apart: 10, of which 5 were waited for; matrix products, arithmetic and copies ran while one was open for 0% of the time, Pallas kernels for 11%

profile of v5, /device:TPU:0, one launch (start us, length us, event | category | flops | bytes accessed | tf_op | source)
XLA Modules:
  0.0 34.5 jit_solution(14553074775615017390)
XLA Ops:
  0.6 1.0 %shard_map.104 = (bf16[48,1024]{1,0:T(8,128)(2,1)S(1)}, bf16[24,1024]{1,0:T(8,128)(2,1)S(1)}, f32[16,1024]{1,0:T(8,128)S(1)}, f32[8,1024]{1,0:T(8,128)S(1)}, f32...) custom-call(s32[4]{0:T(128)} %sizes_in.1, ...), custom_call_target="tpu_custom_call" | custom-call | bytes 196608 | tf_op jit(solution)/shard_map/pallas_call | solution.py:637
  1.6 5.1 %collective-permute-start.1 = (bf16[48,1024]{1,0:T(8,128)(2,1)S(1)}, bf16[48,1024]{1,0:T(8,128)(2,1)S(1)}, u32[]{:S(2)}, u32[]{:S(2)}) collective-permute-start(bf16[48,1024]{1,0:T(8,128)(2,1)S(1)} %get-tuple-element.36.pack_ref.own_pack_ref), channel_id=1, source_target_pairs={{0,12},{2,6},{4,0},{6,10},{8,4},{10,14},{12,8},{14,2},{1,13},{3,7}... | collective-permute-start | bytes 294920 | tf_op jit(solution)/shard_map/ppermute | solution.py:664
  6.7 0.0 collective-permute-start
  6.7 1.9 %collective-permute-start.2 = (bf16[24,1024]{1,0:T(8,128)(2,1)S(1)}, bf16[24,1024]{1,0:T(8,128)(2,1)S(1)}, u32[]{:S(2)}, u32[]{:S(2)}) collective-permute-start(bf16[24,1024]{1,0:T(8,128)(2,1)S(1)} %get-tuple-element.40), channel_id=1, source_target_pairs={{0,14},{2,4},{4,2},{6,8},{8,6},{10,12},{12,10},{14,0},{1,15},{3,5}... | collective-permute-start | bytes 147464 | tf_op jit(solution)/shard_map/ppermute | solution.py:663
  8.6 2.8 %shard_map.105 = (bf16[1024,1024]{1,0:T(8,128)(2,1)S(1)}, bf16[1024,1024]{1,0:T(8,128)(2,1)S(1)}, bf16[1024,1024]{1,0:T(8,128)(2,1)S(1)}, bf16[1024,1024]{1,0:T(...) custom-call(s32[1,1024]{1,0:T(1,128)S(1)} %get-tuple-element.34.righ, ...), custom_call_target="tpu_custom_call" | custom-call | flops 67108864 | bytes 4194304 | tf_op jit(solution)/shard_map/pallas_call | solution.py:637
  11.5 0.0 collective-permute-done.across_ref
  11.5 2.0 %collective-permute-done.2.slant_ref = bf16[24,1024]{1,0:T(8,128)(2,1)S(1)} collective-permute-done((bf16[24,1024]{1,0:T(8,128)(2,1)S(1)}, bf16[24,1024]{1,0:T(8,128)(2,1)S(1)}, u32[]{:S(2)}, u32[]{:S(2)}) %collective-permute-start.2) | collective-permute-done | bytes 49184 | tf_op jit(solution)/shard_map/ppermute | solution.py:663
  13.5 0.0 collective-permute-done.1.along_ref
  13.5 1.0 %shard_map.107 = (bf16[16,1280]{1,0:T(8,128)(2,1)S(1)}, bf16[16,2816]{1,0:T(8,128)(2,1)S(1)}) custom-call(s32[4,24]{1,0:T(4,128)S(1)} %get-tuple-element.32.ids_ref, bf16[1024,1024]{1,0:T(8,128)(2,1)S(1)} %get-tuple-element.48.square_ref, bf16[1024,1024]{1,0:T(8,128)(2,1)S(1)} %get-tuple-element.49.early_ref, ...), custom_call_target="tpu_custom_call" | custom-call | flops 134217728 | bytes 4194304 | tf_op jit(solution)/shard_map/pallas_call | solution.py:637
  14.5 0.4 %collective-permute-start.3 = (bf16[16,2816]{1,0:T(8,128)(2,1)S(1)}, bf16[16,2816]{1,0:T(8,128)(2,1)S(1)}, u32[]{:S(2)}, u32[]{:S(2)}) collective-permute-start(bf16[16,2816]{1,0:T(8,128)(2,1)S(1)} %get-tuple-element.55), channel_id=1, source_target_pairs={{0,2},{2,0},{4,6},{6,4},{8,10},{10,8},{12,14},{14,12},{1,3},{3,1},... | collective-permute-start | bytes 270344 | tf_op jit(solution)/shard_map/ppermute | solution.py:700
  14.9 1.8 %collective-permute-start.5 = (bf16[16,1280]{1,0:T(8,128)(2,1)S(1)}, bf16[16,1280]{1,0:T(8,128)(2,1)S(1)}, u32[]{:S(2)}, u32[]{:S(2)}) collective-permute-start(bf16[16,1280]{1,0:T(8,128)(2,1)S(1)} %get-tuple-element.54.own_ref), channel_id=1, source_target_pairs={{0,14},{2,4},{4,2},{6,8},{8,6},{10,12},{12,10},{14,0},{1,15},{3,5}... | collective-permute-start | bytes 122888 | tf_op jit(solution)/shard_map/ppermute | solution.py:698
  16.7 1.0 %collective-permute-start.4 = (bf16[16,1280]{1,0:T(8,128)(2,1)S(1)}, bf16[16,1280]{1,0:T(8,128)(2,1)S(1)}, u32[]{:S(2)}, u32[]{:S(2)}) collective-permute-start(bf16[16,1280]{1,0:T(8,128)(2,1)S(1)} %get-tuple-element.54.own_ref), channel_id=1, source_target_pairs={{0,12},{2,6},{4,0},{6,10},{8,4},{10,14},{12,8},{14,2},{1,13},{3,7}... | collective-permute-start | bytes 122888 | tf_op jit(solution)/shard_map/ppermute | solution.py:699
  17.8 0.9 %shard_map.106 = (bf16[128,2048]{1,0:T(8,128)(2,1)S(1)}, bf16[128,512]{1,0:T(8,128)(2,1)S(1)}, f32[1,1024]{1,0:T(1,128)S(1)}, bf16[128,128]{1,0:T(8,128)(2,1)S(1)}, bf16[1024,1024]{1,0:T(8,128)(2,1)S(1)}) custom-call(s32[4,24]{1,0:T(4,128)S(1)} %get-tuple-element.32.ids_ref, f32[48,48]{1,0:T(8,128)S(1)} %get-tuple-element.33.inverse_ref, ...), custom_call_target="tpu_custom_call" | custom-call | flops 100663296 | bytes 4194304 | tf_op jit(solution)/shard_map/pallas_call | solution.py:637
  18.6 3.0 %collective-permute-done.5.slant_ref = bf16[16,1280]{1,0:T(8,128)(2,1)S(1)} collective-permute-done((bf16[16,1280]{1,0:T(8,128)(2,1)S(1)}, bf16[16,1280]{1,0:T(8,128)(2,1)S(1)}, u32[]{:S(2)}, u32[]{:S(2)}) %collective-permute-start.5) | collective-permute-done | bytes 40992 | tf_op jit(solution)/shard_map/ppermute | solution.py:698
  21.6 0.0 collective-permute-done.4.along_ref
  21.6 0.0 collective-permute-done.3.across_ref
  21.7 1.7 %shard_map.108 = (f32[16,1024]{1,0:T(8,128)S(1)}, f32[16,1024]{1,0:T(8,128)S(1)}, bf16[16,1408]{1,0:T(8,128)(2,1)S(1)}, f32[16,128]{1,0:T(8,128)S(1)}) custom-call(bf16[128,128]{1,0:T(8,128)(2,1)S(1)} %get-tuple-element.46.names_ref, bf16[128,512]{1,0:T(8,128)(2,1)S(1)} %get-tuple-element.41.solver_ref, bf16[128,2048]{1,0:T(8,128)(2,1)S(1)} %get-tuple-element.42.maps_ref, ...), custom_call_target="tpu_custom_call" | custom-call | flops 134217728 | bytes 4194304 | tf_op jit(solution)/shard_map/pallas_call | solution.py:637
  23.3 0.4 %collective-permute-start.6 = (bf16[16,1408]{1,0:T(8,128)(2,1)S(1)}, bf16[16,1408]{1,0:T(8,128)(2,1)S(1)}, u32[]{:S(2)}, u32[]{:S(2)}) collective-permute-start(bf16[16,1408]{1,0:T(8,128)(2,1)S(1)} %get-tuple-element.58.up_own_ref), channel_id=1, source_target_pairs={{0,4},{4,8},{8,12},{12,0},{1,5},{5,9},{9,13},{13,1},{2,6},{6,10},{... | collective-permute-start | bytes 135176 | tf_op jit(solution)/shard_map/ppermute | solution.py:21
  23.7 2.1 %collective-permute-start.8 = (f32[16,128]{1,0:T(8,128)S(1)}, f32[16,128]{1,0:T(8,128)S(1)}, u32[]{:S(2)}, u32[]{:S(2)}) collective-permute-start(f32[16,128]{1,0:T(8,128)S(1)} %get-tuple-element.59.own_ref), channel_id=1, source_target_pairs={{0,8},{4,12},{8,0},{12,4},{1,9},{5,13},{9,1},{13,5},{2,10},{6,14},... | collective-permute-start | bytes 24584 | tf_op jit(solution)/shard_map/ppermute | solution.py:21
  25.8 1.4 %collective-permute-start.7 = (f32[16,128]{1,0:T(8,128)S(1)}, f32[16,128]{1,0:T(8,128)S(1)}, u32[]{:S(2)}, u32[]{:S(2)}) collective-permute-start(f32[16,128]{1,0:T(8,128)S(1)} %get-tuple-element.59.own_ref), channel_id=1, source_target_pairs={{0,12},{4,0},{8,4},{12,8},{1,13},{5,1},{9,5},{13,9},{2,14},{6,2},{... | collective-permute-start | bytes 24584 | tf_op jit(solution)/shard_map/ppermute | solution.py:21
  27.2 1.1 %collective-permute-done.8.far_ref = f32[16,128]{1,0:T(8,128)S(1)} collective-permute-done((f32[16,128]{1,0:T(8,128)S(1)}, f32[16,128]{1,0:T(8,128)S(1)}, u32[]{:S(2)}, u32[]{:S(2)}) %collective-permute-start.8) | collective-permute-done | bytes 8224 | tf_op jit(solution)/shard_map/ppermute | solution.py:21
  28.3 1.2 %collective-permute-done.7.down_ref = f32[16,128]{1,0:T(8,128)S(1)} collective-permute-done((f32[16,128]{1,0:T(8,128)S(1)}, f32[16,128]{1,0:T(8,128)S(1)}, u32[]{:S(2)}, u32[]{:S(2)}) %collective-permute-start.7) | collective-permute-done | bytes 8224 | tf_op jit(solution)/shard_map/ppermute | solution.py:21
  29.5 0.0 collective-permute-done.6.up_ref
  29.5 1.2 %collective-permute-start.9 = (bf16[16,1408]{1,0:T(8,128)(2,1)S(1)}, bf16[16,1408]{1,0:T(8,128)(2,1)S(1)}, u32[]{:S(2)}, u32[]{:S(2)}) collective-permute-start(bf16[16,1408]{1,0:T(8,128)(2,1)S(1)} %shard_map.109.mine_ref), channel_id=1, source_target_pairs={{0,2},{2,0},{4,6},{6,4},{8,10},{10,8},{12,14},{14,12},{1,3},{3,1},... | collective-permute-start | bytes 135176 | tf_op jit(solution)/shard_map/ppermute | solution.py:754
  30.7 2.9 %collective-permute-done.9.theirs_ref = bf16[16,1408]{1,0:T(8,128)(2,1)S(1)} collective-permute-done((bf16[16,1408]{1,0:T(8,128)(2,1)S(1)}, bf16[16,1408]{1,0:T(8,128)(2,1)S(1)}, u32[]{:S(2)}, u32[]{:S(2)}) %collective-permute-start.9) | collective-permute-done | bytes 45088 | tf_op jit(solution)/shard_map/ppermute | solution.py:754
  33.6 0.9 %shard_map.110 = (f32[16,1024]{1,0:T(8,128)}, f32[16,1024]{1,0:T(8,128)}) custom-call(bf16[128,512]{1,0:T(8,128)(2,1)S(1)} %get-tuple-element.41.solver_ref, bf16[128,2048]{1,0:T(8,128)(2,1)S(1)} %get-tuple-element.42.maps_ref, f32[8,1024]{1,0:T(8,128)S(1)} %get-tuple-element.43.live_ref, f32[16,1024]{1,0:T(8,128)S(1)} %get-tuple-element.44.loaded_ref, ...), custom_call_target="tpu_custom_call" | custom-call | bytes 393216 | tf_op jit(solution)/shard_map/pallas_call | solution.py:637
  (1 shorter events, 0.0 us)
Async XLA Ops:
  1.6 11.9 %collective-permute-start.1 = (bf16[48,1024]{1,0:T(8,128)(2,1)S(1)}, bf16[48,1024]{1,0:T(8,128)(2,1)S(1)}, u32[]{:S(2)}, u32[]{:S(2)}) collective-permute-start(bf16[48,1024]{1,0:T(8,128)(2,1)S(1)} %get-tuple-element.36.pack_ref.own_pack_ref), channel_id=1, source_target_pairs={{0,12},{2,6},{4,0},{6,10},{8,4},{10,14},{12,8},{14,2},{1,13},{3,7}... | collective-permute-start | bytes 294920 | tf_op jit(solution)/shard_map/ppermute | solution.py:664
  6.7 4.8 %collective-permute-start = (bf16[24,1024]{1,0:T(8,128)(2,1)}, bf16[24,1024]{1,0:T(8,128)(2,1)S(1)}, u32[]{:S(2)}, u32[]{:S(2)}) collective-permute-start(bf16[24,1024]{1,0:T(8,128)(2,1)} %bitcast.8), channel_id=1, source_target_pairs={{0,2},{2,0},{4,6},{6,4},{8,10},{10,8},{12,14},{14,12},{1,3},{3,1},... | collective-permute-start | bytes 147464 | tf_op jit(solution)/shard_map/ppermute | solution.py:665
  6.7 6.8 %collective-permute-start.2 = (bf16[24,1024]{1,0:T(8,128)(2,1)S(1)}, bf16[24,1024]{1,0:T(8,128)(2,1)S(1)}, u32[]{:S(2)}, u32[]{:S(2)}) collective-permute-start(bf16[24,1024]{1,0:T(8,128)(2,1)S(1)} %get-tuple-element.40), channel_id=1, source_target_pairs={{0,14},{2,4},{4,2},{6,8},{8,6},{10,12},{12,10},{14,0},{1,15},{3,5}... | collective-permute-start | bytes 147464 | tf_op jit(solution)/shard_map/ppermute | solution.py:663
  14.5 7.1 %collective-permute-start.3 = (bf16[16,2816]{1,0:T(8,128)(2,1)S(1)}, bf16[16,2816]{1,0:T(8,128)(2,1)S(1)}, u32[]{:S(2)}, u32[]{:S(2)}) collective-permute-start(bf16[16,2816]{1,0:T(8,128)(2,1)S(1)} %get-tuple-element.55), channel_id=1, source_target_pairs={{0,2},{2,0},{4,6},{6,4},{8,10},{10,8},{12,14},{14,12},{1,3},{3,1},... | collective-permute-start | bytes 270344 | tf_op jit(solution)/shard_map/ppermute | solution.py:700
  14.9 6.7 %collective-permute-start.5 = (bf16[16,1280]{1,0:T(8,128)(2,1)S(1)}, bf16[16,1280]{1,0:T(8,128)(2,1)S(1)}, u32[]{:S(2)}, u32[]{:S(2)}) collective-permute-start(bf16[16,1280]{1,0:T(8,128)(2,1)S(1)} %get-tuple-element.54.own_ref), channel_id=1, source_target_pairs={{0,14},{2,4},{4,2},{6,8},{8,6},{10,12},{12,10},{14,0},{1,15},{3,5}... | collective-permute-start | bytes 122888 | tf_op jit(solution)/shard_map/ppermute | solution.py:698
  16.7 4.9 %collective-permute-start.4 = (bf16[16,1280]{1,0:T(8,128)(2,1)S(1)}, bf16[16,1280]{1,0:T(8,128)(2,1)S(1)}, u32[]{:S(2)}, u32[]{:S(2)}) collective-permute-start(bf16[16,1280]{1,0:T(8,128)(2,1)S(1)} %get-tuple-element.54.own_ref), channel_id=1, source_target_pairs={{0,12},{2,6},{4,0},{6,10},{8,4},{10,14},{12,8},{14,2},{1,13},{3,7}... | collective-permute-start | bytes 122888 | tf_op jit(solution)/shard_map/ppermute | solution.py:699
  23.3 6.1 %collective-permute-start.6 = (bf16[16,1408]{1,0:T(8,128)(2,1)S(1)}, bf16[16,1408]{1,0:T(8,128)(2,1)S(1)}, u32[]{:S(2)}, u32[]{:S(2)}) collective-permute-start(bf16[16,1408]{1,0:T(8,128)(2,1)S(1)} %get-tuple-element.58.up_own_ref), channel_id=1, source_target_pairs={{0,4},{4,8},{8,12},{12,0},{1,5},{5,9},{9,13},{13,1},{2,6},{6,10},{... | collective-permute-start | bytes 135176 | tf_op jit(solution)/shard_map/ppermute | solution.py:21
  23.7 4.5 %collective-permute-start.8 = (f32[16,128]{1,0:T(8,128)S(1)}, f32[16,128]{1,0:T(8,128)S(1)}, u32[]{:S(2)}, u32[]{:S(2)}) collective-permute-start(f32[16,128]{1,0:T(8,128)S(1)} %get-tuple-element.59.own_ref), channel_id=1, source_target_pairs={{0,8},{4,12},{8,0},{12,4},{1,9},{5,13},{9,1},{13,5},{2,10},{6,14},... | collective-permute-start | bytes 24584 | tf_op jit(solution)/shard_map/ppermute | solution.py:21
  25.8 3.7 %collective-permute-start.7 = (f32[16,128]{1,0:T(8,128)S(1)}, f32[16,128]{1,0:T(8,128)S(1)}, u32[]{:S(2)}, u32[]{:S(2)}) collective-permute-start(f32[16,128]{1,0:T(8,128)S(1)} %get-tuple-element.59.own_ref), channel_id=1, source_target_pairs={{0,12},{4,0},{8,4},{12,8},{1,13},{5,1},{9,5},{13,9},{2,14},{6,2},{... | collective-permute-start | bytes 24584 | tf_op jit(solution)/shard_map/ppermute | solution.py:21
  29.5 4.1 %collective-permute-start.9 = (bf16[16,1408]{1,0:T(8,128)(2,1)S(1)}, bf16[16,1408]{1,0:T(8,128)(2,1)S(1)}, u32[]{:S(2)}, u32[]{:S(2)}) collective-permute-start(bf16[16,1408]{1,0:T(8,128)(2,1)S(1)} %shard_map.109.mine_ref), channel_id=1, source_target_pairs={{0,2},{2,0},{4,6},{6,4},{8,10},{10,8},{12,14},{14,12},{1,3},{3,1},... | collective-permute-start | bytes 135176 | tf_op jit(solution)/shard_map/ppermute | solution.py:754

commit v6 on v5

--- a/solution.py
+++ b/solution.py
@@ -156,11 +156,6 @@
 
 def stacked(value):
     return jnp.concatenate(halves(value), axis=0)
-
-
-def folded(value):
-    rows = value.shape[0] // 2
-    return value[:rows] + value[rows:]
 
 
 def thirds(value):
@@ -499,7 +494,7 @@
     right = scale_ref[...] * image_right
     image_ref[...] = image
     next_ref[...] = left
-    left_2, right_2 = stacked(left), stacked(right)
+    left_2, right_2 = left.astype(BF16), right.astype(BF16)
     loaded = loaded_ref[...]
     first = loaded * weights_ref[...]
     sums = [
@@ -511,7 +506,7 @@
 
     def totals(block, local, corner):
         energy = jnp.sum(block * local, axis=1, keepdims=True)
-        small = selected(folded(corner), names_ref[...])
+        small = selected(corner, names_ref[...])
         for at, value in enumerate([*sums, energy]):
             small = jnp.where(lane == LANES - len(sums) - 1 + at, value, small)
         small_ref[...] = small
@@ -522,18 +517,18 @@
         local = nn(left_2, square_ref[...])
         slotted_2 = nn(right_2, right_hot_ref[...]).astype(BF16)
         corner = nt(right_2, maps_ref[:, half:])
-        local = folded(local + nn(slotted_2, early_ref[...]))
+        local = local + nn(slotted_2, early_ref[...])
         up_ref[:, :half] = local.astype(BF16)
-        totals(folded(left_2.astype(F32)), local, corner)
+        totals(left_2.astype(F32), local, corner)
 
     @pl.when(jnp.logical_not(lower))
     def _():
         slotted_2 = nn(right_2, right_hot_ref[...]).astype(BF16)
         local = nn(left_2, late_ref[...])
         corner = nt(left_2, maps_ref[:, :half])
-        local = folded(local + nn(slotted_2, square_ref[...]))
+        local = local + nn(slotted_2, square_ref[...])
         up_ref[:, :half] = nn(local.astype(BF16), order_ref[...]).astype(BF16)
-        totals(folded(slotted_2.astype(F32)), local, corner)
+        totals(slotted_2.astype(F32), local, corner)
 
 
 def relay_kernel(up_own_ref, up_ref, down_ref, far_ref, own_ref, out_ref):

time: 34.7 us -> 34.5 us (level)
  no operation moved by 1% of the time
where the time goes in v6:
time: 34.5 us; the launch traced here: 34.3 us
  starting transfers between devices  15.4 us (45%)
  waiting for transfers between devices  10.2 us (30%)
  Pallas kernels  8.04 us (23%)
  between operations  0.68 us (2%)
    pallas_call x7, Pallas kernels, call(): pl.pallas_call(kernel, in_specs=specs, out_specs=[VMEM] * len(outs), out_...  8.04 us
    ppermute x1, starting transfers between devices, ring(): pack_along = lax.ppermute(pack, grid, along)  5.13 us
    ppermute x3, starting transfers between devices, shifted(): return lax.ppermute(value, axis, pairs)  3.84 us
    ppermute x1, waiting for transfers between devices, ring(): send_slant = lax.ppermute(send, grid, slant)  2.99 us
    ppermute x1, waiting for transfers between devices, ring(): theirs = lax.ppermute(mine, grid, across)  2.87 us
    ppermute x3, waiting for transfers between devices, shifted(): return lax.ppermute(value, axis, pairs)  2.29 us
    ppermute x1, waiting for transfers between devices, ring(): pack_slant = lax.ppermute(skew, grid, slant)  2.02 us
    ppermute x1, starting transfers between devices, ring(): pack_slant = lax.ppermute(skew, grid, slant)  1.91 us
  transfers between devices with their start and end apart: 10, of which 5 were waited for; matrix products, arithmetic and copies ran while one was open for 0% of the time, Pallas kernels for 11%

profile of v6, /device:TPU:0, one launch (start us, length us, event | category | flops | bytes accessed | tf_op | source)
XLA Modules:
  0.0 34.3 jit_solution(3368867136030560656)
XLA Ops:
  0.6 1.0 %shard_map.104 = (bf16[48,1024]{1,0:T(8,128)(2,1)S(1)}, bf16[24,1024]{1,0:T(8,128)(2,1)S(1)}, f32[16,1024]{1,0:T(8,128)S(1)}, f32[8,1024]{1,0:T(8,128)S(1)}, f32...) custom-call(s32[4]{0:T(128)} %sizes_in.1, ...), custom_call_target="tpu_custom_call" | custom-call | bytes 196608 | tf_op jit(solution)/shard_map/pallas_call | solution.py:632
  1.6 5.1 %collective-permute-start.1 = (bf16[48,1024]{1,0:T(8,128)(2,1)S(1)}, bf16[48,1024]{1,0:T(8,128)(2,1)S(1)}, u32[]{:S(2)}, u32[]{:S(2)}) collective-permute-start(bf16[48,1024]{1,0:T(8,128)(2,1)S(1)} %get-tuple-element.36.pack_ref.own_pack_ref), channel_id=1, source_target_pairs={{0,12},{2,6},{4,0},{6,10},{8,4},{10,14},{12,8},{14,2},{1,13},{3,7}... | collective-permute-start | bytes 294920 | tf_op jit(solution)/shard_map/ppermute | solution.py:659
  6.7 0.0 collective-permute-start
  6.7 1.9 %collective-permute-start.2 = (bf16[24,1024]{1,0:T(8,128)(2,1)S(1)}, bf16[24,1024]{1,0:T(8,128)(2,1)S(1)}, u32[]{:S(2)}, u32[]{:S(2)}) collective-permute-start(bf16[24,1024]{1,0:T(8,128)(2,1)S(1)} %get-tuple-element.40), channel_id=1, source_target_pairs={{0,14},{2,4},{4,2},{6,8},{8,6},{10,12},{12,10},{14,0},{1,15},{3,5}... | collective-permute-start | bytes 147464 | tf_op jit(solution)/shard_map/ppermute | solution.py:658
  8.6 2.8 %shard_map.105 = (bf16[1024,1024]{1,0:T(8,128)(2,1)S(1)}, bf16[1024,1024]{1,0:T(8,128)(2,1)S(1)}, bf16[1024,1024]{1,0:T(8,128)(2,1)S(1)}, bf16[1024,1024]{1,0:T(...) custom-call(s32[1,1024]{1,0:T(1,128)S(1)} %get-tuple-element.34.righ, ...), custom_call_target="tpu_custom_call" | custom-call | flops 67108864 | bytes 4194304 | tf_op jit(solution)/shard_map/pallas_call | solution.py:632
  11.5 0.0 collective-permute-done.across_ref
  11.5 2.0 %collective-permute-done.2.slant_ref = bf16[24,1024]{1,0:T(8,128)(2,1)S(1)} collective-permute-done((bf16[24,1024]{1,0:T(8,128)(2,1)S(1)}, bf16[24,1024]{1,0:T(8,128)(2,1)S(1)}, u32[]{:S(2)}, u32[]{:S(2)}) %collective-permute-start.2) | collective-permute-done | bytes 49184 | tf_op jit(solution)/shard_map/ppermute | solution.py:658
  13.5 0.0 collective-permute-done.1.along_ref
  13.5 1.0 %shard_map.107 = (bf16[16,1280]{1,0:T(8,128)(2,1)S(1)}, bf16[16,2816]{1,0:T(8,128)(2,1)S(1)}) custom-call(s32[4,24]{1,0:T(4,128)S(1)} %get-tuple-element.32.ids_ref, bf16[1024,1024]{1,0:T(8,128)(2,1)S(1)} %get-tuple-element.48.square_ref, bf16[1024,1024]{1,0:T(8,128)(2,1)S(1)} %get-tuple-element.49.early_ref, ...), custom_call_target="tpu_custom_call" | custom-call | flops 134217728 | bytes 4194304 | tf_op jit(solution)/shard_map/pallas_call | solution.py:632
  14.5 0.4 %collective-permute-start.3 = (bf16[16,2816]{1,0:T(8,128)(2,1)S(1)}, bf16[16,2816]{1,0:T(8,128)(2,1)S(1)}, u32[]{:S(2)}, u32[]{:S(2)}) collective-permute-start(bf16[16,2816]{1,0:T(8,128)(2,1)S(1)} %get-tuple-element.55), channel_id=1, source_target_pairs={{0,2},{2,0},{4,6},{6,4},{8,10},{10,8},{12,14},{14,12},{1,3},{3,1},... | collective-permute-start | bytes 270344 | tf_op jit(solution)/shard_map/ppermute | solution.py:695
  14.9 1.8 %collective-permute-start.5 = (bf16[16,1280]{1,0:T(8,128)(2,1)S(1)}, bf16[16,1280]{1,0:T(8,128)(2,1)S(1)}, u32[]{:S(2)}, u32[]{:S(2)}) collective-permute-start(bf16[16,1280]{1,0:T(8,128)(2,1)S(1)} %get-tuple-element.54.own_ref), channel_id=1, source_target_pairs={{0,14},{2,4},{4,2},{6,8},{8,6},{10,12},{12,10},{14,0},{1,15},{3,5}... | collective-permute-start | bytes 122888 | tf_op jit(solution)/shard_map/ppermute | solution.py:693
  16.7 1.0 %collective-permute-start.4 = (bf16[16,1280]{1,0:T(8,128)(2,1)S(1)}, bf16[16,1280]{1,0:T(8,128)(2,1)S(1)}, u32[]{:S(2)}, u32[]{:S(2)}) collective-permute-start(bf16[16,1280]{1,0:T(8,128)(2,1)S(1)} %get-tuple-element.54.own_ref), channel_id=1, source_target_pairs={{0,12},{2,6},{4,0},{6,10},{8,4},{10,14},{12,8},{14,2},{1,13},{3,7}... | collective-permute-start | bytes 122888 | tf_op jit(solution)/shard_map/ppermute | solution.py:694
  17.8 0.9 %shard_map.106 = (bf16[128,2048]{1,0:T(8,128)(2,1)S(1)}, bf16[128,512]{1,0:T(8,128)(2,1)S(1)}, f32[1,1024]{1,0:T(1,128)S(1)}, bf16[128,128]{1,0:T(8,128)(2,1)S(1)}, bf16[1024,1024]{1,0:T(8,128)(2,1)S(1)}) custom-call(s32[4,24]{1,0:T(4,128)S(1)} %get-tuple-element.32.ids_ref, f32[48,48]{1,0:T(8,128)S(1)} %get-tuple-element.33.inverse_ref, ...), custom_call_target="tpu_custom_call" | custom-call | flops 100663296 | bytes 4194304 | tf_op jit(solution)/shard_map/pallas_call | solution.py:632
  18.6 3.0 %collective-permute-done.5.slant_ref = bf16[16,1280]{1,0:T(8,128)(2,1)S(1)} collective-permute-done((bf16[16,1280]{1,0:T(8,128)(2,1)S(1)}, bf16[16,1280]{1,0:T(8,128)(2,1)S(1)}, u32[]{:S(2)}, u32[]{:S(2)}) %collective-permute-start.5) | collective-permute-done | bytes 40992 | tf_op jit(solution)/shard_map/ppermute | solution.py:693
  21.6 0.0 collective-permute-done.4.along_ref
  21.6 0.0 collective-permute-done.3.across_ref
  21.7 1.5 %shard_map.108 = (f32[16,1024]{1,0:T(8,128)S(1)}, f32[16,1024]{1,0:T(8,128)S(1)}, bf16[16,1408]{1,0:T(8,128)(2,1)S(1)}, f32[16,128]{1,0:T(8,128)S(1)}) custom-call(bf16[128,128]{1,0:T(8,128)(2,1)S(1)} %get-tuple-element.46.names_ref, bf16[128,512]{1,0:T(8,128)(2,1)S(1)} %get-tuple-element.41.solver_ref, bf16[128,2048]{1,0:T(8,128)(2,1)S(1)} %get-tuple-element.42.maps_ref, ...), custom_call_target="tpu_custom_call" | custom-call | flops 134217728 | bytes 4194304 | tf_op jit(solution)/shard_map/pallas_call | solution.py:632
  23.1 0.4 %collective-permute-start.6 = (bf16[16,1408]{1,0:T(8,128)(2,1)S(1)}, bf16[16,1408]{1,0:T(8,128)(2,1)S(1)}, u32[]{:S(2)}, u32[]{:S(2)}) collective-permute-start(bf16[16,1408]{1,0:T(8,128)(2,1)S(1)} %get-tuple-element.58.up_own_ref), channel_id=1, source_target_pairs={{0,4},{4,8},{8,12},{12,0},{1,5},{5,9},{9,13},{13,1},{2,6},{6,10},{... | collective-permute-start | bytes 135176 | tf_op jit(solution)/shard_map/ppermute | solution.py:21
  23.5 2.1 %collective-permute-start.8 = (f32[16,128]{1,0:T(8,128)S(1)}, f32[16,128]{1,0:T(8,128)S(1)}, u32[]{:S(2)}, u32[]{:S(2)}) collective-permute-start(f32[16,128]{1,0:T(8,128)S(1)} %get-tuple-element.59.own_ref), channel_id=1, source_target_pairs={{0,8},{4,12},{8,0},{12,4},{1,9},{5,13},{9,1},{13,5},{2,10},{6,14},... | collective-permute-start | bytes 24584 | tf_op jit(solution)/shard_map/ppermute | solution.py:21
  25.6 1.4 %collective-permute-start.7 = (f32[16,128]{1,0:T(8,128)S(1)}, f32[16,128]{1,0:T(8,128)S(1)}, u32[]{:S(2)}, u32[]{:S(2)}) collective-permute-start(f32[16,128]{1,0:T(8,128)S(1)} %get-tuple-element.59.own_ref), channel_id=1, source_target_pairs={{0,12},{4,0},{8,4},{12,8},{1,13},{5,1},{9,5},{13,9},{2,14},{6,2},{... | collective-permute-start | bytes 24584 | tf_op jit(solution)/shard_map/ppermute | solution.py:21
  26.9 1.1 %collective-permute-done.8.far_ref = f32[16,128]{1,0:T(8,128)S(1)} collective-permute-done((f32[16,128]{1,0:T(8,128)S(1)}, f32[16,128]{1,0:T(8,128)S(1)}, u32[]{:S(2)}, u32[]{:S(2)}) %collective-permute-start.8) | collective-permute-done | bytes 8224 | tf_op jit(solution)/shard_map/ppermute | solution.py:21
  28.1 1.2 %collective-permute-done.7.down_ref = f32[16,128]{1,0:T(8,128)S(1)} collective-permute-done((f32[16,128]{1,0:T(8,128)S(1)}, f32[16,128]{1,0:T(8,128)S(1)}, u32[]{:S(2)}, u32[]{:S(2)}) %collective-permute-start.7) | collective-permute-done | bytes 8224 | tf_op jit(solution)/shard_map/ppermute | solution.py:21
  29.2 0.0 collective-permute-done.6.up_ref
  29.3 1.2 %collective-permute-start.9 = (bf16[16,1408]{1,0:T(8,128)(2,1)S(1)}, bf16[16,1408]{1,0:T(8,128)(2,1)S(1)}, u32[]{:S(2)}, u32[]{:S(2)}) collective-permute-start(bf16[16,1408]{1,0:T(8,128)(2,1)S(1)} %shard_map.109.mine_ref), channel_id=1, source_target_pairs={{0,2},{2,0},{4,6},{6,4},{8,10},{10,8},{12,14},{14,12},{1,3},{3,1},... | collective-permute-start | bytes 135176 | tf_op jit(solution)/shard_map/ppermute | solution.py:749
  30.5 2.9 %collective-permute-done.9.theirs_ref = bf16[16,1408]{1,0:T(8,128)(2,1)S(1)} collective-permute-done((bf16[16,1408]{1,0:T(8,128)(2,1)S(1)}, bf16[16,1408]{1,0:T(8,128)(2,1)S(1)}, u32[]{:S(2)}, u32[]{:S(2)}) %collective-permute-start.9) | collective-permute-done | bytes 45088 | tf_op jit(solution)/shard_map/ppermute | solution.py:749
  33.4 0.9 %shard_map.110 = (f32[16,1024]{1,0:T(8,128)}, f32[16,1024]{1,0:T(8,128)}) custom-call(bf16[128,512]{1,0:T(8,128)(2,1)S(1)} %get-tuple-element.41.solver_ref, bf16[128,2048]{1,0:T(8,128)(2,1)S(1)} %get-tuple-element.42.maps_ref, f32[8,1024]{1,0:T(8,128)S(1)} %get-tuple-element.43.live_ref, f32[16,1024]{1,0:T(8,128)S(1)} %get-tuple-element.44.loaded_ref, ...), custom_call_target="tpu_custom_call" | custom-call | bytes 393216 | tf_op jit(solution)/shard_map/pallas_call | solution.py:632
  (1 shorter events, 0.0 us)
Async XLA Ops:
  1.6 11.9 %collective-permute-start.1 = (bf16[48,1024]{1,0:T(8,128)(2,1)S(1)}, bf16[48,1024]{1,0:T(8,128)(2,1)S(1)}, u32[]{:S(2)}, u32[]{:S(2)}) collective-permute-start(bf16[48,1024]{1,0:T(8,128)(2,1)S(1)} %get-tuple-element.36.pack_ref.own_pack_ref), channel_id=1, source_target_pairs={{0,12},{2,6},{4,0},{6,10},{8,4},{10,14},{12,8},{14,2},{1,13},{3,7}... | collective-permute-start | bytes 294920 | tf_op jit(solution)/shard_map/ppermute | solution.py:659
  6.7 4.8 %collective-permute-start = (bf16[24,1024]{1,0:T(8,128)(2,1)}, bf16[24,1024]{1,0:T(8,128)(2,1)S(1)}, u32[]{:S(2)}, u32[]{:S(2)}) collective-permute-start(bf16[24,1024]{1,0:T(8,128)(2,1)} %bitcast.8), channel_id=1, source_target_pairs={{0,2},{2,0},{4,6},{6,4},{8,10},{10,8},{12,14},{14,12},{1,3},{3,1},... | collective-permute-start | bytes 147464 | tf_op jit(solution)/shard_map/ppermute | solution.py:660
  6.7 6.8 %collective-permute-start.2 = (bf16[24,1024]{1,0:T(8,128)(2,1)S(1)}, bf16[24,1024]{1,0:T(8,128)(2,1)S(1)}, u32[]{:S(2)}, u32[]{:S(2)}) collective-permute-start(bf16[24,1024]{1,0:T(8,128)(2,1)S(1)} %get-tuple-element.40), channel_id=1, source_target_pairs={{0,14},{2,4},{4,2},{6,8},{8,6},{10,12},{12,10},{14,0},{1,15},{3,5}... | collective-permute-start | bytes 147464 | tf_op jit(solution)/shard_map/ppermute | solution.py:658
  14.5 7.1 %collective-permute-start.3 = (bf16[16,2816]{1,0:T(8,128)(2,1)S(1)}, bf16[16,2816]{1,0:T(8,128)(2,1)S(1)}, u32[]{:S(2)}, u32[]{:S(2)}) collective-permute-start(bf16[16,2816]{1,0:T(8,128)(2,1)S(1)} %get-tuple-element.55), channel_id=1, source_target_pairs={{0,2},{2,0},{4,6},{6,4},{8,10},{10,8},{12,14},{14,12},{1,3},{3,1},... | collective-permute-start | bytes 270344 | tf_op jit(solution)/shard_map/ppermute | solution.py:695
  14.9 6.7 %collective-permute-start.5 = (bf16[16,1280]{1,0:T(8,128)(2,1)S(1)}, bf16[16,1280]{1,0:T(8,128)(2,1)S(1)}, u32[]{:S(2)}, u32[]{:S(2)}) collective-permute-start(bf16[16,1280]{1,0:T(8,128)(2,1)S(1)} %get-tuple-element.54.own_ref), channel_id=1, source_target_pairs={{0,14},{2,4},{4,2},{6,8},{8,6},{10,12},{12,10},{14,0},{1,15},{3,5}... | collective-permute-start | bytes 122888 | tf_op jit(solution)/shard_map/ppermute | solution.py:693
  16.7 4.9 %collective-permute-start.4 = (bf16[16,1280]{1,0:T(8,128)(2,1)S(1)}, bf16[16,1280]{1,0:T(8,128)(2,1)S(1)}, u32[]{:S(2)}, u32[]{:S(2)}) collective-permute-start(bf16[16,1280]{1,0:T(8,128)(2,1)S(1)} %get-tuple-element.54.own_ref), channel_id=1, source_target_pairs={{0,12},{2,6},{4,0},{6,10},{8,4},{10,14},{12,8},{14,2},{1,13},{3,7}... | collective-permute-start | bytes 122888 | tf_op jit(solution)/shard_map/ppermute | solution.py:694
  23.1 6.1 %collective-permute-start.6 = (bf16[16,1408]{1,0:T(8,128)(2,1)S(1)}, bf16[16,1408]{1,0:T(8,128)(2,1)S(1)}, u32[]{:S(2)}, u32[]{:S(2)}) collective-permute-start(bf16[16,1408]{1,0:T(8,128)(2,1)S(1)} %get-tuple-element.58.up_own_ref), channel_id=1, source_target_pairs={{0,4},{4,8},{8,12},{12,0},{1,5},{5,9},{9,13},{13,1},{2,6},{6,10},{... | collective-permute-start | bytes 135176 | tf_op jit(solution)/shard_map/ppermute | solution.py:21
  23.5 4.5 %collective-permute-start.8 = (f32[16,128]{1,0:T(8,128)S(1)}, f32[16,128]{1,0:T(8,128)S(1)}, u32[]{:S(2)}, u32[]{:S(2)}) collective-permute-start(f32[16,128]{1,0:T(8,128)S(1)} %get-tuple-element.59.own_ref), channel_id=1, source_target_pairs={{0,8},{4,12},{8,0},{12,4},{1,9},{5,13},{9,1},{13,5},{2,10},{6,14},... | collective-permute-start | bytes 24584 | tf_op jit(solution)/shard_map/ppermute | solution.py:21
  25.6 3.7 %collective-permute-start.7 = (f32[16,128]{1,0:T(8,128)S(1)}, f32[16,128]{1,0:T(8,128)S(1)}, u32[]{:S(2)}, u32[]{:S(2)}) collective-permute-start(f32[16,128]{1,0:T(8,128)S(1)} %get-tuple-element.59.own_ref), channel_id=1, source_target_pairs={{0,12},{4,0},{8,4},{12,8},{1,13},{5,1},{9,5},{13,9},{2,14},{6,2},{... | collective-permute-start | bytes 24584 | tf_op jit(solution)/shard_map/ppermute | solution.py:21
  29.3 4.1 %collective-permute-start.9 = (bf16[16,1408]{1,0:T(8,128)(2,1)S(1)}, bf16[16,1408]{1,0:T(8,128)(2,1)S(1)}, u32[]{:S(2)}, u32[]{:S(2)}) collective-permute-start(bf16[16,1408]{1,0:T(8,128)(2,1)S(1)} %shard_map.109.mine_ref), channel_id=1, source_target_pairs={{0,2},{2,0},{4,6},{6,4},{8,10},{10,8},{12,14},{14,12},{1,3},{3,1},... | collective-permute-start | bytes 135176 | tf_op jit(solution)/shard_map/ppermute | solution.py:749

commit v7 on v6

--- a/solution.py
+++ b/solution.py
@@ -390,7 +390,7 @@
         send_ref[:, :half] = nn(local, order_ref[...]).astype(BF16)
 
     wide = send_ref.shape[1]
-    relayed = along_ref[columns : columns + corners, :].astype(F32)
+    relayed = own_pack_ref[columns : columns + corners, :].astype(F32)
     tail = relayed[columns:]
     tail = jnp.concatenate([tail[:, : half // 2], tail[:, half // 2 :]], axis=0)
     pair_ref[:, :wide] = send_ref[...]
@@ -482,9 +482,9 @@
     image = jnp.where(live_ref[0:1] > 0.0, image, 0.0)
     wide = own_ref.shape[1]
     half_rows = columns // 2
-    tail = across_ref[:, wide + half :].astype(F32)
+    tail = slant_ref[:, wide + half :].astype(F32)
     tail = jnp.concatenate([tail[:half_rows], tail[half_rows:]], axis=1)
-    relayed = jnp.concatenate([across_ref[:, wide : wide + half].astype(F32), tail], axis=0)
+    relayed = jnp.concatenate([slant_ref[:, wide : wide + half].astype(F32), tail], axis=0)
     count = relayed.shape[0]
     more = nn(backs[:, 2 * count : 3 * count], relayed.astype(BF16))
     fix_right = fix[:, half:] + jnp.where(lower, 0.0, more)
@@ -495,20 +495,16 @@
     image_ref[...] = image
     next_ref[...] = left
     left_2, right_2 = left.astype(BF16), right.astype(BF16)
-    loaded = loaded_ref[...]
-    first = loaded * weights_ref[...]
-    sums = [
-        jnp.sum(loaded * first, axis=1, keepdims=True),
-        jnp.sum(first * image, axis=1, keepdims=True),
-        jnp.sum(image * left, axis=1, keepdims=True),
-    ]
-    lane = lax.broadcasted_iota(jnp.int32, (columns, LANES), 1)
 
     def totals(block, local, corner):
-        energy = jnp.sum(block * local, axis=1, keepdims=True)
+        loaded = loaded_ref[...]
+        first = loaded * weights_ref[...]
+        pairs = ((loaded, first), (first, image), (image, left), (block, local))
+        lane = lax.broadcasted_iota(jnp.int32, (columns, LANES), 1)
         small = selected(corner, names_ref[...])
-        for at, value in enumerate([*sums, energy]):
-            small = jnp.where(lane == LANES - len(sums) - 1 + at, value, small)
+        for at, (one, other) in enumerate(pairs):
+            value = jnp.sum(one * other, axis=1, keepdims=True)
+            small = jnp.where(lane == LANES - len(pairs) + at, value, small)
         small_ref[...] = small
         up_ref[:, half:] = jnp.concatenate(thirds(small), axis=1)
 
@@ -690,9 +686,9 @@
         moved=4 * block * half,
         room=16,
     )
-    send_slant = lax.ppermute(send, grid, slant)
+    send_slant = lax.ppermute(pair, grid, slant)
     send_along = lax.ppermute(send, grid, along)
-    send_across = lax.ppermute(pair, grid, across)
+    send_across = lax.ppermute(send, grid, across)
     maps, solver, scale_right, names, late = call(
         order_kernel,
         [ids, inverse, order, left_hot, cross, pack, map_across, pack_along, pack_slant],

time: 34.5 us -> 34.5 us (level)
  waiting for transfers between devices: 10.2 us -> 10.8 us
  starting transfers between devices: 15.4 us -> 14.8 us
    ppermute x1, waiting for transfers between devices: 0.01 us -> 2.88 us  [ring(): send_along = lax.ppermute(send, grid, along)]
    ppermute x2, waiting for transfers between devices: 3 us -> 1.16 us  [the longest x1 1.16 us: ring(): send_slant = lax.ppermute(pair, grid, slant)]
    ppermute x1, starting transfers between devices: 1.04 us -> 0.01 us  [ring(): send_along = lax.ppermute(send, grid, along)]
  transfers between devices with their start and end apart: 10 -> 10, of which waited for: 5 -> 6; matrix products, arithmetic and copies ran while one was open for 0% -> 0% of each run, Pallas kernels for 11% -> 11%
where the time goes in v7:
time: 34.5 us; the launch traced here: 34.3 us
  starting transfers between devices  14.8 us (43%)
  waiting for transfers between devices  10.8 us (31%)
  Pallas kernels  8.04 us (23%)
  between operations  0.68 us (2%)
    pallas_call x7, Pallas kernels, call(): pl.pallas_call(kernel, in_specs=specs, out_specs=[VMEM] * len(outs), out_...  8.04 us
    ppermute x1, starting transfers between devices, ring(): pack_along = lax.ppermute(pack, grid, along)  5.13 us
    ppermute x3, starting transfers between devices, shifted(): return lax.ppermute(value, axis, pairs)  3.86 us
    ppermute x1, waiting for transfers between devices, ring(): send_along = lax.ppermute(send, grid, along)  2.88 us
    ppermute x1, waiting for transfers between devices, ring(): theirs = lax.ppermute(mine, grid, across)  2.56 us
    ppermute x3, waiting for transfers between devices, shifted(): return lax.ppermute(value, axis, pairs)  2.19 us
    ppermute x1, starting transfers between devices, ring(): send_slant = lax.ppermute(pair, grid, slant)  2.12 us
    ppermute x1, waiting for transfers between devices, ring(): pack_slant = lax.ppermute(skew, grid, slant)  2.02 us
  transfers between devices with their start and end apart: 10, of which 6 were waited for; matrix products, arithmetic and copies ran while one was open for 0% of the time, Pallas kernels for 11%

profile of v7, /device:TPU:0, one launch (start us, length us, event | category | flops | bytes accessed | tf_op | source)
XLA Modules:
  0.0 34.3 jit_solution(3408367517877136668)
XLA Ops:
  0.6 1.0 %shard_map.104 = (bf16[48,1024]{1,0:T(8,128)(2,1)S(1)}, bf16[24,1024]{1,0:T(8,128)(2,1)S(1)}, f32[16,1024]{1,0:T(8,128)S(1)}, f32[8,1024]{1,0:T(8,128)S(1)}, f32...) custom-call(s32[4]{0:T(128)} %sizes_in.1, ...), custom_call_target="tpu_custom_call" | custom-call | bytes 196608 | tf_op jit(solution)/shard_map/pallas_call | solution.py:628
  1.6 5.1 %collective-permute-start.1 = (bf16[48,1024]{1,0:T(8,128)(2,1)S(1)}, bf16[48,1024]{1,0:T(8,128)(2,1)S(1)}, u32[]{:S(2)}, u32[]{:S(2)}) collective-permute-start(bf16[48,1024]{1,0:T(8,128)(2,1)S(1)} %get-tuple-element.36.pack_ref.own_pack_ref), channel_id=1, source_target_pairs={{0,12},{2,6},{4,0},{6,10},{8,4},{10,14},{12,8},{14,2},{1,13},{3,7}... | collective-permute-start | bytes 294920 | tf_op jit(solution)/shard_map/ppermute | solution.py:655
  6.7 0.0 collective-permute-start
  6.7 1.9 %collective-permute-start.2 = (bf16[24,1024]{1,0:T(8,128)(2,1)S(1)}, bf16[24,1024]{1,0:T(8,128)(2,1)S(1)}, u32[]{:S(2)}, u32[]{:S(2)}) collective-permute-start(bf16[24,1024]{1,0:T(8,128)(2,1)S(1)} %get-tuple-element.40), channel_id=1, source_target_pairs={{0,14},{2,4},{4,2},{6,8},{8,6},{10,12},{12,10},{14,0},{1,15},{3,5}... | collective-permute-start | bytes 147464 | tf_op jit(solution)/shard_map/ppermute | solution.py:654
  8.6 2.8 %shard_map.105 = (bf16[1024,1024]{1,0:T(8,128)(2,1)S(1)}, bf16[1024,1024]{1,0:T(8,128)(2,1)S(1)}, bf16[1024,1024]{1,0:T(8,128)(2,1)S(1)}, bf16[1024,1024]{1,0:T(...) custom-call(s32[1,1024]{1,0:T(1,128)S(1)} %get-tuple-element.34.righ, ...), custom_call_target="tpu_custom_call" | custom-call | flops 67108864 | bytes 4194304 | tf_op jit(solution)/shard_map/pallas_call | solution.py:628
  11.5 0.0 collective-permute-done.across_ref
  11.5 2.0 %collective-permute-done.2.slant_ref = bf16[24,1024]{1,0:T(8,128)(2,1)S(1)} collective-permute-done((bf16[24,1024]{1,0:T(8,128)(2,1)S(1)}, bf16[24,1024]{1,0:T(8,128)(2,1)S(1)}, u32[]{:S(2)}, u32[]{:S(2)}) %collective-permute-start.2) | collective-permute-done | bytes 49184 | tf_op jit(solution)/shard_map/ppermute | solution.py:654
  13.5 0.0 collective-permute-done.1.along_ref
  13.5 1.0 %shard_map.107 = (bf16[16,1280]{1,0:T(8,128)(2,1)S(1)}, bf16[16,2816]{1,0:T(8,128)(2,1)S(1)}) custom-call(s32[4,24]{1,0:T(4,128)S(1)} %get-tuple-element.32.ids_ref, bf16[1024,1024]{1,0:T(8,128)(2,1)S(1)} %get-tuple-element.48.square_ref, bf16[1024,1024]{1,0:T(8,128)(2,1)S(1)} %get-tuple-element.49.early_ref, ...), custom_call_target="tpu_custom_call" | custom-call | flops 134217728 | bytes 4194304 | tf_op jit(solution)/shard_map/pallas_call | solution.py:628
  14.5 2.1 %collective-permute-start.5 = (bf16[16,2816]{1,0:T(8,128)(2,1)S(1)}, bf16[16,2816]{1,0:T(8,128)(2,1)S(1)}, u32[]{:S(2)}, u32[]{:S(2)}) collective-permute-start(bf16[16,2816]{1,0:T(8,128)(2,1)S(1)} %get-tuple-element.55), channel_id=1, source_target_pairs={{0,14},{2,4},{4,2},{6,8},{8,6},{10,12},{12,10},{14,0},{1,15},{3,5}... | collective-permute-start | bytes 270344 | tf_op jit(solution)/shard_map/ppermute | solution.py:689
  16.6 0.0 collective-permute-start.4
  16.6 0.2 collective-permute-start.3
  16.9 0.9 %shard_map.106 = (bf16[128,2048]{1,0:T(8,128)(2,1)S(1)}, bf16[128,512]{1,0:T(8,128)(2,1)S(1)}, f32[1,1024]{1,0:T(1,128)S(1)}, bf16[128,128]{1,0:T(8,128)(2,1)S(1)}, bf16[1024,1024]{1,0:T(8,128)(2,1)S(1)}) custom-call(s32[4,24]{1,0:T(4,128)S(1)} %get-tuple-element.32.ids_ref, f32[48,48]{1,0:T(8,128)S(1)} %get-tuple-element.33.inverse_ref, ...), custom_call_target="tpu_custom_call" | custom-call | flops 100663296 | bytes 4194304 | tf_op jit(solution)/shard_map/pallas_call | solution.py:628
  17.8 2.9 %collective-permute-done.4.along_ref = bf16[16,1280]{1,0:T(8,128)(2,1)S(1)} collective-permute-done((bf16[16,1280]{1,0:T(8,128)(2,1)S(1)}, bf16[16,1280]{1,0:T(8,128)(2,1)S(1)}, u32[]{:S(2)}, u32[]{:S(2)}) %collective-permute-start.4) | collective-permute-done | bytes 40992 | tf_op jit(solution)/shard_map/ppermute | solution.py:690
  20.6 0.0 collective-permute-done.3.across_ref
  20.6 1.2 %collective-permute-done.5.slant_ref = bf16[16,2816]{1,0:T(8,128)(2,1)S(1)} collective-permute-done((bf16[16,2816]{1,0:T(8,128)(2,1)S(1)}, bf16[16,2816]{1,0:T(8,128)(2,1)S(1)}, u32[]{:S(2)}, u32[]{:S(2)}) %collective-permute-start.5) | collective-permute-done | bytes 90144 | tf_op jit(solution)/shard_map/ppermute | solution.py:689
  21.8 1.5 %shard_map.108 = (f32[16,1024]{1,0:T(8,128)S(1)}, f32[16,1024]{1,0:T(8,128)S(1)}, bf16[16,1408]{1,0:T(8,128)(2,1)S(1)}, f32[16,128]{1,0:T(8,128)S(1)}) custom-call(bf16[128,128]{1,0:T(8,128)(2,1)S(1)} %get-tuple-element.46.names_ref, bf16[128,512]{1,0:T(8,128)(2,1)S(1)} %get-tuple-element.41.solver_ref, bf16[128,2048]{1,0:T(8,128)(2,1)S(1)} %get-tuple-element.42.maps_ref, ...), custom_call_target="tpu_custom_call" | custom-call | flops 134217728 | bytes 4194304 | tf_op jit(solution)/shard_map/pallas_call | solution.py:628
  23.2 0.9 %collective-permute-start.6 = (bf16[16,1408]{1,0:T(8,128)(2,1)S(1)}, bf16[16,1408]{1,0:T(8,128)(2,1)S(1)}, u32[]{:S(2)}, u32[]{:S(2)}) collective-permute-start(bf16[16,1408]{1,0:T(8,128)(2,1)S(1)} %get-tuple-element.58.up_own_ref), channel_id=1, source_target_pairs={{0,4},{4,8},{8,12},{12,0},{1,5},{5,9},{9,13},{13,1},{2,6},{6,10},{... | collective-permute-start | bytes 135176 | tf_op jit(solution)/shard_map/ppermute | solution.py:21
  24.1 1.3 %collective-permute-start.8 = (f32[16,128]{1,0:T(8,128)S(1)}, f32[16,128]{1,0:T(8,128)S(1)}, u32[]{:S(2)}, u32[]{:S(2)}) collective-permute-start(f32[16,128]{1,0:T(8,128)S(1)} %get-tuple-element.59.own_ref), channel_id=1, source_target_pairs={{0,8},{4,12},{8,0},{12,4},{1,9},{5,13},{9,1},{13,5},{2,10},{6,14},... | collective-permute-start | bytes 24584 | tf_op jit(solution)/shard_map/ppermute | solution.py:21
  25.4 1.7 %collective-permute-start.7 = (f32[16,128]{1,0:T(8,128)S(1)}, f32[16,128]{1,0:T(8,128)S(1)}, u32[]{:S(2)}, u32[]{:S(2)}) collective-permute-start(f32[16,128]{1,0:T(8,128)S(1)} %get-tuple-element.59.own_ref), channel_id=1, source_target_pairs={{0,12},{4,0},{8,4},{12,8},{1,13},{5,1},{9,5},{13,9},{2,14},{6,2},{... | collective-permute-start | bytes 24584 | tf_op jit(solution)/shard_map/ppermute | solution.py:21
  27.1 1.6 %collective-permute-done.8.far_ref = f32[16,128]{1,0:T(8,128)S(1)} collective-permute-done((f32[16,128]{1,0:T(8,128)S(1)}, f32[16,128]{1,0:T(8,128)S(1)}, u32[]{:S(2)}, u32[]{:S(2)}) %collective-permute-start.8) | collective-permute-done | bytes 8224 | tf_op jit(solution)/shard_map/ppermute | solution.py:21
  28.7 0.6 %collective-permute-done.7.down_ref = f32[16,128]{1,0:T(8,128)S(1)} collective-permute-done((f32[16,128]{1,0:T(8,128)S(1)}, f32[16,128]{1,0:T(8,128)S(1)}, u32[]{:S(2)}, u32[]{:S(2)}) %collective-permute-start.7) | collective-permute-done | bytes 8224 | tf_op jit(solution)/shard_map/ppermute | solution.py:21
  29.3 0.0 collective-permute-done.6.up_ref
  29.3 1.6 %collective-permute-start.9 = (bf16[16,1408]{1,0:T(8,128)(2,1)S(1)}, bf16[16,1408]{1,0:T(8,128)(2,1)S(1)}, u32[]{:S(2)}, u32[]{:S(2)}) collective-permute-start(bf16[16,1408]{1,0:T(8,128)(2,1)S(1)} %shard_map.109.mine_ref), channel_id=1, source_target_pairs={{0,2},{2,0},{4,6},{6,4},{8,10},{10,8},{12,14},{14,12},{1,3},{3,1},... | collective-permute-start | bytes 135176 | tf_op jit(solution)/shard_map/ppermute | solution.py:745
  30.9 2.6 %collective-permute-done.9.theirs_ref = bf16[16,1408]{1,0:T(8,128)(2,1)S(1)} collective-permute-done((bf16[16,1408]{1,0:T(8,128)(2,1)S(1)}, bf16[16,1408]{1,0:T(8,128)(2,1)S(1)}, u32[]{:S(2)}, u32[]{:S(2)}) %collective-permute-start.9) | collective-permute-done | bytes 45088 | tf_op jit(solution)/shard_map/ppermute | solution.py:745
  33.4 0.9 %shard_map.110 = (f32[16,1024]{1,0:T(8,128)}, f32[16,1024]{1,0:T(8,128)}) custom-call(bf16[128,512]{1,0:T(8,128)(2,1)S(1)} %get-tuple-element.41.solver_ref, bf16[128,2048]{1,0:T(8,128)(2,1)S(1)} %get-tuple-element.42.maps_ref, f32[8,1024]{1,0:T(8,128)S(1)} %get-tuple-element.43.live_ref, f32[16,1024]{1,0:T(8,128)S(1)} %get-tuple-element.44.loaded_ref, ...), custom_call_target="tpu_custom_call" | custom-call | bytes 393216 | tf_op jit(solution)/shard_map/pallas_call | solution.py:628
  (1 shorter events, 0.0 us)
Async XLA Ops:
  1.6 11.9 %collective-permute-start.1 = (bf16[48,1024]{1,0:T(8,128)(2,1)S(1)}, bf16[48,1024]{1,0:T(8,128)(2,1)S(1)}, u32[]{:S(2)}, u32[]{:S(2)}) collective-permute-start(bf16[48,1024]{1,0:T(8,128)(2,1)S(1)} %get-tuple-element.36.pack_ref.own_pack_ref), channel_id=1, source_target_pairs={{0,12},{2,6},{4,0},{6,10},{8,4},{10,14},{12,8},{14,2},{1,13},{3,7}... | collective-permute-start | bytes 294920 | tf_op jit(solution)/shard_map/ppermute | solution.py:655
  6.7 4.8 %collective-permute-start = (bf16[24,1024]{1,0:T(8,128)(2,1)}, bf16[24,1024]{1,0:T(8,128)(2,1)S(1)}, u32[]{:S(2)}, u32[]{:S(2)}) collective-permute-start(bf16[24,1024]{1,0:T(8,128)(2,1)} %bitcast.8), channel_id=1, source_target_pairs={{0,2},{2,0},{4,6},{6,4},{8,10},{10,8},{12,14},{14,12},{1,3},{3,1},... | collective-permute-start | bytes 147464 | tf_op jit(solution)/shard_map/ppermute | solution.py:656
  6.7 6.8 %collective-permute-start.2 = (bf16[24,1024]{1,0:T(8,128)(2,1)S(1)}, bf16[24,1024]{1,0:T(8,128)(2,1)S(1)}, u32[]{:S(2)}, u32[]{:S(2)}) collective-permute-start(bf16[24,1024]{1,0:T(8,128)(2,1)S(1)} %get-tuple-element.40), channel_id=1, source_target_pairs={{0,14},{2,4},{4,2},{6,8},{8,6},{10,12},{12,10},{14,0},{1,15},{3,5}... | collective-permute-start | bytes 147464 | tf_op jit(solution)/shard_map/ppermute | solution.py:654
  14.5 7.3 %collective-permute-start.5 = (bf16[16,2816]{1,0:T(8,128)(2,1)S(1)}, bf16[16,2816]{1,0:T(8,128)(2,1)S(1)}, u32[]{:S(2)}, u32[]{:S(2)}) collective-permute-start(bf16[16,2816]{1,0:T(8,128)(2,1)S(1)} %get-tuple-element.55), channel_id=1, source_target_pairs={{0,14},{2,4},{4,2},{6,8},{8,6},{10,12},{12,10},{14,0},{1,15},{3,5}... | collective-permute-start | bytes 270344 | tf_op jit(solution)/shard_map/ppermute | solution.py:689
  16.6 4.0 %collective-permute-start.4 = (bf16[16,1280]{1,0:T(8,128)(2,1)S(1)}, bf16[16,1280]{1,0:T(8,128)(2,1)S(1)}, u32[]{:S(2)}, u32[]{:S(2)}) collective-permute-start(bf16[16,1280]{1,0:T(8,128)(2,1)S(1)} %get-tuple-element.54.own_ref), channel_id=1, source_target_pairs={{0,12},{2,6},{4,0},{6,10},{8,4},{10,14},{12,8},{14,2},{1,13},{3,7}... | collective-permute-start | bytes 122888 | tf_op jit(solution)/shard_map/ppermute | solution.py:690
  16.6 4.0 %collective-permute-start.3 = (bf16[16,1280]{1,0:T(8,128)(2,1)S(1)}, bf16[16,1280]{1,0:T(8,128)(2,1)S(1)}, u32[]{:S(2)}, u32[]{:S(2)}) collective-permute-start(bf16[16,1280]{1,0:T(8,128)(2,1)S(1)} %get-tuple-element.54.own_ref), channel_id=1, source_target_pairs={{0,2},{2,0},{4,6},{6,4},{8,10},{10,8},{12,14},{14,12},{1,3},{3,1},... | collective-permute-start | bytes 122888 | tf_op jit(solution)/shard_map/ppermute | solution.py:691
  23.2 6.0 %collective-permute-start.6 = (bf16[16,1408]{1,0:T(8,128)(2,1)S(1)}, bf16[16,1408]{1,0:T(8,128)(2,1)S(1)}, u32[]{:S(2)}, u32[]{:S(2)}) collective-permute-start(bf16[16,1408]{1,0:T(8,128)(2,1)S(1)} %get-tuple-element.58.up_own_ref), channel_id=1, source_target_pairs={{0,4},{4,8},{8,12},{12,0},{1,5},{5,9},{9,13},{13,1},{2,6},{6,10},{... | collective-permute-start | bytes 135176 | tf_op jit(solution)/shard_map/ppermute | solution.py:21
  24.1 4.6 %collective-permute-start.8 = (f32[16,128]{1,0:T(8,128)S(1)}, f32[16,128]{1,0:T(8,128)S(1)}, u32[]{:S(2)}, u32[]{:S(2)}) collective-permute-start(f32[16,128]{1,0:T(8,128)S(1)} %get-tuple-element.59.own_ref), channel_id=1, source_target_pairs={{0,8},{4,12},{8,0},{12,4},{1,9},{5,13},{9,1},{13,5},{2,10},{6,14},... | collective-permute-start | bytes 24584 | tf_op jit(solution)/shard_map/ppermute | solution.py:21
  25.4 3.8 %collective-permute-start.7 = (f32[16,128]{1,0:T(8,128)S(1)}, f32[16,128]{1,0:T(8,128)S(1)}, u32[]{:S(2)}, u32[]{:S(2)}) collective-permute-start(f32[16,128]{1,0:T(8,128)S(1)} %get-tuple-element.59.own_ref), channel_id=1, source_target_pairs={{0,12},{4,0},{8,4},{12,8},{1,13},{5,1},{9,5},{13,9},{2,14},{6,2},{... | collective-permute-start | bytes 24584 | tf_op jit(solution)/shard_map/ppermute | solution.py:21
  29.3 4.1 %collective-permute-start.9 = (bf16[16,1408]{1,0:T(8,128)(2,1)S(1)}, bf16[16,1408]{1,0:T(8,128)(2,1)S(1)}, u32[]{:S(2)}, u32[]{:S(2)}) collective-permute-start(bf16[16,1408]{1,0:T(8,128)(2,1)S(1)} %shard_map.109.mine_ref), channel_id=1, source_target_pairs={{0,2},{2,0},{4,6},{6,4},{8,10},{10,8},{12,14},{14,12},{1,3},{3,1},... | collective-permute-start | bytes 135176 | tf_op jit(solution)/shard_map/ppermute | solution.py:745

commit v8 on v6

--- a/solution.py
+++ b/solution.py
@@ -510,7 +510,7 @@
         for at, value in enumerate([*sums, energy]):
             small = jnp.where(lane == LANES - len(sums) - 1 + at, value, small)
         small_ref[...] = small
-        up_ref[:, half:] = jnp.concatenate(thirds(small), axis=1)
+        up_ref[:, half:] = jnp.concatenate(halves(small), axis=1)
 
     @pl.when(lower)
     def _():
@@ -533,11 +533,11 @@
 
 def relay_kernel(up_own_ref, up_ref, down_ref, far_ref, own_ref, out_ref):
     lower = lax.axis_index("row") == 0
-    half = up_ref.shape[1] - 3 * LANES
-    total = own_ref[...] + pieces_sum(up_ref, half, 3)
+    half = up_ref.shape[1] - 2 * LANES
+    total = own_ref[...] + pieces_sum(up_ref, half, 2)
     total = total + down_ref[...] + far_ref[...]
     out_ref[:, :half] = jnp.where(lower, up_own_ref[:, :half], up_ref[:, :half])
-    out_ref[:, half:] = jnp.concatenate(thirds(total), axis=1)
+    out_ref[:, half:] = jnp.concatenate(halves(total), axis=1)
 
 
 def close_kernel(
@@ -555,7 +555,7 @@
 ):
     lower = lax.axis_index("row") == 0
     columns, half = loaded_ref.shape
-    mine, theirs = pieces_sum(mine_ref, half, 3), pieces_sum(theirs_ref, half, 3)
+    mine, theirs = pieces_sum(mine_ref, half, 2), pieces_sum(theirs_ref, half, 2)
     total = jnp.where(lower, mine, theirs)
     lane = lax.broadcasted_iota(jnp.int32, (columns, LANES), 1)
     coarse = jnp.where(lane < LANES - 4, total, 0.0)
@@ -730,7 +730,7 @@
         [
             ((columns, half), F32),
             ((columns, half), F32),
-            ((columns, half + 3 * LANES), BF16),
+            ((columns, half + 2 * LANES), BF16),
             ((columns, LANES), F32),
         ],
         flops=2 * big,
@@ -743,7 +743,7 @@
     (mine,) = call(
         relay_kernel,
         [up, up_in, down_in, far_in, small],
-        [((columns, half + 3 * LANES), BF16)],
+        [((columns, half + 2 * LANES), BF16)],
         moved=8 * columns * half,
     )
     theirs = lax.ppermute(mine, grid, across)

time: 34.5 us -> 34.4 us (level)
  no operation moved by 1% of the time
where the time goes in v8:
time: 34.4 us; the launch traced here: 34.2 us
  starting transfers between devices  15.4 us (45%)
  waiting for transfers between devices  10.2 us (30%)
  Pallas kernels  8.04 us (23%)
  between operations  0.68 us (2%)
    pallas_call x7, Pallas kernels, call(): pl.pallas_call(kernel, in_specs=specs, out_specs=[VMEM] * len(outs), out_...  8.04 us
    ppermute x1, starting transfers between devices, ring(): pack_along = lax.ppermute(pack, grid, along)  5.13 us
    ppermute x3, starting transfers between devices, shifted(): return lax.ppermute(value, axis, pairs)  3.84 us
    ppermute x1, waiting for transfers between devices, ring(): send_slant = lax.ppermute(send, grid, slant)  2.99 us
    ppermute x1, waiting for transfers between devices, ring(): theirs = lax.ppermute(mine, grid, across)  2.84 us
    ppermute x3, waiting for transfers between devices, shifted(): return lax.ppermute(value, axis, pairs)  2.29 us
    ppermute x1, waiting for transfers between devices, ring(): pack_slant = lax.ppermute(skew, grid, slant)  2.02 us
    ppermute x1, starting transfers between devices, ring(): pack_slant = lax.ppermute(skew, grid, slant)  1.91 us
  transfers between devices with their start and end apart: 10, of which 5 were waited for; matrix products, arithmetic and copies ran while one was open for 0% of the time, Pallas kernels for 11%

profile of v8, /device:TPU:0, one launch (start us, length us, event | category | flops | bytes accessed | tf_op | source)
XLA Modules:
  0.0 34.2 jit_solution(14260213215271945360)
XLA Ops:
  0.6 1.0 %shard_map.104 = (bf16[48,1024]{1,0:T(8,128)(2,1)S(1)}, bf16[24,1024]{1,0:T(8,128)(2,1)S(1)}, f32[16,1024]{1,0:T(8,128)S(1)}, f32[8,1024]{1,0:T(8,128)S(1)}, f32...) custom-call(s32[4]{0:T(128)} %sizes_in.1, ...), custom_call_target="tpu_custom_call" | custom-call | bytes 196608 | tf_op jit(solution)/shard_map/pallas_call | solution.py:632
  1.6 5.1 %collective-permute-start.1 = (bf16[48,1024]{1,0:T(8,128)(2,1)S(1)}, bf16[48,1024]{1,0:T(8,128)(2,1)S(1)}, u32[]{:S(2)}, u32[]{:S(2)}) collective-permute-start(bf16[48,1024]{1,0:T(8,128)(2,1)S(1)} %get-tuple-element.36.pack_ref.own_pack_ref), channel_id=1, source_target_pairs={{0,12},{2,6},{4,0},{6,10},{8,4},{10,14},{12,8},{14,2},{1,13},{3,7}... | collective-permute-start | bytes 294920 | tf_op jit(solution)/shard_map/ppermute | solution.py:659
  6.7 0.0 collective-permute-start
  6.7 1.9 %collective-permute-start.2 = (bf16[24,1024]{1,0:T(8,128)(2,1)S(1)}, bf16[24,1024]{1,0:T(8,128)(2,1)S(1)}, u32[]{:S(2)}, u32[]{:S(2)}) collective-permute-start(bf16[24,1024]{1,0:T(8,128)(2,1)S(1)} %get-tuple-element.40), channel_id=1, source_target_pairs={{0,14},{2,4},{4,2},{6,8},{8,6},{10,12},{12,10},{14,0},{1,15},{3,5}... | collective-permute-start | bytes 147464 | tf_op jit(solution)/shard_map/ppermute | solution.py:658
  8.6 2.8 %shard_map.105 = (bf16[1024,1024]{1,0:T(8,128)(2,1)S(1)}, bf16[1024,1024]{1,0:T(8,128)(2,1)S(1)}, bf16[1024,1024]{1,0:T(8,128)(2,1)S(1)}, bf16[1024,1024]{1,0:T(...) custom-call(s32[1,1024]{1,0:T(1,128)S(1)} %get-tuple-element.34.righ, ...), custom_call_target="tpu_custom_call" | custom-call | flops 67108864 | bytes 4194304 | tf_op jit(solution)/shard_map/pallas_call | solution.py:632
  11.5 0.0 collective-permute-done.across_ref
  11.5 2.0 %collective-permute-done.2.slant_ref = bf16[24,1024]{1,0:T(8,128)(2,1)S(1)} collective-permute-done((bf16[24,1024]{1,0:T(8,128)(2,1)S(1)}, bf16[24,1024]{1,0:T(8,128)(2,1)S(1)}, u32[]{:S(2)}, u32[]{:S(2)}) %collective-permute-start.2) | collective-permute-done | bytes 49184 | tf_op jit(solution)/shard_map/ppermute | solution.py:658
  13.5 0.0 collective-permute-done.1.along_ref
  13.5 1.0 %shard_map.107 = (bf16[16,1280]{1,0:T(8,128)(2,1)S(1)}, bf16[16,2816]{1,0:T(8,128)(2,1)S(1)}) custom-call(s32[4,24]{1,0:T(4,128)S(1)} %get-tuple-element.32.ids_ref, bf16[1024,1024]{1,0:T(8,128)(2,1)S(1)} %get-tuple-element.48.square_ref, bf16[1024,1024]{1,0:T(8,128)(2,1)S(1)} %get-tuple-element.49.early_ref, ...), custom_call_target="tpu_custom_call" | custom-call | flops 134217728 | bytes 4194304 | tf_op jit(solution)/shard_map/pallas_call | solution.py:632
  14.5 0.4 %collective-permute-start.3 = (bf16[16,2816]{1,0:T(8,128)(2,1)S(1)}, bf16[16,2816]{1,0:T(8,128)(2,1)S(1)}, u32[]{:S(2)}, u32[]{:S(2)}) collective-permute-start(bf16[16,2816]{1,0:T(8,128)(2,1)S(1)} %get-tuple-element.55), channel_id=1, source_target_pairs={{0,2},{2,0},{4,6},{6,4},{8,10},{10,8},{12,14},{14,12},{1,3},{3,1},... | collective-permute-start | bytes 270344 | tf_op jit(solution)/shard_map/ppermute | solution.py:695
  14.9 1.8 %collective-permute-start.5 = (bf16[16,1280]{1,0:T(8,128)(2,1)S(1)}, bf16[16,1280]{1,0:T(8,128)(2,1)S(1)}, u32[]{:S(2)}, u32[]{:S(2)}) collective-permute-start(bf16[16,1280]{1,0:T(8,128)(2,1)S(1)} %get-tuple-element.54.own_ref), channel_id=1, source_target_pairs={{0,14},{2,4},{4,2},{6,8},{8,6},{10,12},{12,10},{14,0},{1,15},{3,5}... | collective-permute-start | bytes 122888 | tf_op jit(solution)/shard_map/ppermute | solution.py:693
  16.7 1.0 %collective-permute-start.4 = (bf16[16,1280]{1,0:T(8,128)(2,1)S(1)}, bf16[16,1280]{1,0:T(8,128)(2,1)S(1)}, u32[]{:S(2)}, u32[]{:S(2)}) collective-permute-start(bf16[16,1280]{1,0:T(8,128)(2,1)S(1)} %get-tuple-element.54.own_ref), channel_id=1, source_target_pairs={{0,12},{2,6},{4,0},{6,10},{8,4},{10,14},{12,8},{14,2},{1,13},{3,7}... | collective-permute-start | bytes 122888 | tf_op jit(solution)/shard_map/ppermute | solution.py:694
  17.8 0.9 %shard_map.106 = (bf16[128,2048]{1,0:T(8,128)(2,1)S(1)}, bf16[128,512]{1,0:T(8,128)(2,1)S(1)}, f32[1,1024]{1,0:T(1,128)S(1)}, bf16[128,128]{1,0:T(8,128)(2,1)S(1)}, bf16[1024,1024]{1,0:T(8,128)(2,1)S(1)}) custom-call(s32[4,24]{1,0:T(4,128)S(1)} %get-tuple-element.32.ids_ref, f32[48,48]{1,0:T(8,128)S(1)} %get-tuple-element.33.inverse_ref, ...), custom_call_target="tpu_custom_call" | custom-call | flops 100663296 | bytes 4194304 | tf_op jit(solution)/shard_map/pallas_call | solution.py:632
  18.6 3.0 %collective-permute-done.5.slant_ref = bf16[16,1280]{1,0:T(8,128)(2,1)S(1)} collective-permute-done((bf16[16,1280]{1,0:T(8,128)(2,1)S(1)}, bf16[16,1280]{1,0:T(8,128)(2,1)S(1)}, u32[]{:S(2)}, u32[]{:S(2)}) %collective-permute-start.5) | collective-permute-done | bytes 40992 | tf_op jit(solution)/shard_map/ppermute | solution.py:693
  21.6 0.0 collective-permute-done.4.along_ref
  21.6 0.0 collective-permute-done.3.across_ref
  21.7 1.4 %shard_map.108 = (f32[16,1024]{1,0:T(8,128)S(1)}, f32[16,1024]{1,0:T(8,128)S(1)}, bf16[16,1280]{1,0:T(8,128)(2,1)S(1)}, f32[16,128]{1,0:T(8,128)S(1)}) custom-call(bf16[128,128]{1,0:T(8,128)(2,1)S(1)} %get-tuple-element.46.names_ref, bf16[128,512]{1,0:T(8,128)(2,1)S(1)} %get-tuple-element.41.solver_ref, bf16[128,2048]{1,0:T(8,128)(2,1)S(1)} %get-tuple-element.42.maps_ref, ...), custom_call_target="tpu_custom_call" | custom-call | flops 134217728 | bytes 4194304 | tf_op jit(solution)/shard_map/pallas_call | solution.py:632
  23.1 0.4 %collective-permute-start.6 = (bf16[16,1280]{1,0:T(8,128)(2,1)S(1)}, bf16[16,1280]{1,0:T(8,128)(2,1)S(1)}, u32[]{:S(2)}, u32[]{:S(2)}) collective-permute-start(bf16[16,1280]{1,0:T(8,128)(2,1)S(1)} %get-tuple-element.58.up_own_ref), channel_id=1, source_target_pairs={{0,4},{4,8},{8,12},{12,0},{1,5},{5,9},{9,13},{13,1},{2,6},{6,10},{... | collective-permute-start | bytes 122888 | tf_op jit(solution)/shard_map/ppermute | solution.py:21
  23.5 2.1 %collective-permute-start.8 = (f32[16,128]{1,0:T(8,128)S(1)}, f32[16,128]{1,0:T(8,128)S(1)}, u32[]{:S(2)}, u32[]{:S(2)}) collective-permute-start(f32[16,128]{1,0:T(8,128)S(1)} %get-tuple-element.59.own_ref), channel_id=1, source_target_pairs={{0,8},{4,12},{8,0},{12,4},{1,9},{5,13},{9,1},{13,5},{2,10},{6,14},... | collective-permute-start | bytes 24584 | tf_op jit(solution)/shard_map/ppermute | solution.py:21
  25.6 1.4 %collective-permute-start.7 = (f32[16,128]{1,0:T(8,128)S(1)}, f32[16,128]{1,0:T(8,128)S(1)}, u32[]{:S(2)}, u32[]{:S(2)}) collective-permute-start(f32[16,128]{1,0:T(8,128)S(1)} %get-tuple-element.59.own_ref), channel_id=1, source_target_pairs={{0,12},{4,0},{8,4},{12,8},{1,13},{5,1},{9,5},{13,9},{2,14},{6,2},{... | collective-permute-start | bytes 24584 | tf_op jit(solution)/shard_map/ppermute | solution.py:21
  26.9 1.1 %collective-permute-done.8.far_ref = f32[16,128]{1,0:T(8,128)S(1)} collective-permute-done((f32[16,128]{1,0:T(8,128)S(1)}, f32[16,128]{1,0:T(8,128)S(1)}, u32[]{:S(2)}, u32[]{:S(2)}) %collective-permute-start.8) | collective-permute-done | bytes 8224 | tf_op jit(solution)/shard_map/ppermute | solution.py:21
  28.1 1.2 %collective-permute-done.7.down_ref = f32[16,128]{1,0:T(8,128)S(1)} collective-permute-done((f32[16,128]{1,0:T(8,128)S(1)}, f32[16,128]{1,0:T(8,128)S(1)}, u32[]{:S(2)}, u32[]{:S(2)}) %collective-permute-start.7) | collective-permute-done | bytes 8224 | tf_op jit(solution)/shard_map/ppermute | solution.py:21
  29.2 0.0 collective-permute-done.6.up_ref
  29.3 1.2 %collective-permute-start.9 = (bf16[16,1280]{1,0:T(8,128)(2,1)S(1)}, bf16[16,1280]{1,0:T(8,128)(2,1)S(1)}, u32[]{:S(2)}, u32[]{:S(2)}) collective-permute-start(bf16[16,1280]{1,0:T(8,128)(2,1)S(1)} %shard_map.109.mine_ref), channel_id=1, source_target_pairs={{0,2},{2,0},{4,6},{6,4},{8,10},{10,8},{12,14},{14,12},{1,3},{3,1},... | collective-permute-start | bytes 122888 | tf_op jit(solution)/shard_map/ppermute | solution.py:749
  30.5 2.8 %collective-permute-done.9.theirs_ref = bf16[16,1280]{1,0:T(8,128)(2,1)S(1)} collective-permute-done((bf16[16,1280]{1,0:T(8,128)(2,1)S(1)}, bf16[16,1280]{1,0:T(8,128)(2,1)S(1)}, u32[]{:S(2)}, u32[]{:S(2)}) %collective-permute-start.9) | collective-permute-done | bytes 40992 | tf_op jit(solution)/shard_map/ppermute | solution.py:749
  33.3 0.9 %shard_map.110 = (f32[16,1024]{1,0:T(8,128)}, f32[16,1024]{1,0:T(8,128)}) custom-call(bf16[128,512]{1,0:T(8,128)(2,1)S(1)} %get-tuple-element.41.solver_ref, bf16[128,2048]{1,0:T(8,128)(2,1)S(1)} %get-tuple-element.42.maps_ref, f32[8,1024]{1,0:T(8,128)S(1)} %get-tuple-element.43.live_ref, f32[16,1024]{1,0:T(8,128)S(1)} %get-tuple-element.44.loaded_ref, ...), custom_call_target="tpu_custom_call" | custom-call | bytes 393216 | tf_op jit(solution)/shard_map/pallas_call | solution.py:632
  (1 shorter events, 0.0 us)
Async XLA Ops:
  1.6 11.9 %collective-permute-start.1 = (bf16[48,1024]{1,0:T(8,128)(2,1)S(1)}, bf16[48,1024]{1,0:T(8,128)(2,1)S(1)}, u32[]{:S(2)}, u32[]{:S(2)}) collective-permute-start(bf16[48,1024]{1,0:T(8,128)(2,1)S(1)} %get-tuple-element.36.pack_ref.own_pack_ref), channel_id=1, source_target_pairs={{0,12},{2,6},{4,0},{6,10},{8,4},{10,14},{12,8},{14,2},{1,13},{3,7}... | collective-permute-start | bytes 294920 | tf_op jit(solution)/shard_map/ppermute | solution.py:659
  6.7 4.8 %collective-permute-start = (bf16[24,1024]{1,0:T(8,128)(2,1)}, bf16[24,1024]{1,0:T(8,128)(2,1)S(1)}, u32[]{:S(2)}, u32[]{:S(2)}) collective-permute-start(bf16[24,1024]{1,0:T(8,128)(2,1)} %bitcast.8), channel_id=1, source_target_pairs={{0,2},{2,0},{4,6},{6,4},{8,10},{10,8},{12,14},{14,12},{1,3},{3,1},... | collective-permute-start | bytes 147464 | tf_op jit(solution)/shard_map/ppermute | solution.py:660
  6.7 6.8 %collective-permute-start.2 = (bf16[24,1024]{1,0:T(8,128)(2,1)S(1)}, bf16[24,1024]{1,0:T(8,128)(2,1)S(1)}, u32[]{:S(2)}, u32[]{:S(2)}) collective-permute-start(bf16[24,1024]{1,0:T(8,128)(2,1)S(1)} %get-tuple-element.40), channel_id=1, source_target_pairs={{0,14},{2,4},{4,2},{6,8},{8,6},{10,12},{12,10},{14,0},{1,15},{3,5}... | collective-permute-start | bytes 147464 | tf_op jit(solution)/shard_map/ppermute | solution.py:658
  14.5 7.1 %collective-permute-start.3 = (bf16[16,2816]{1,0:T(8,128)(2,1)S(1)}, bf16[16,2816]{1,0:T(8,128)(2,1)S(1)}, u32[]{:S(2)}, u32[]{:S(2)}) collective-permute-start(bf16[16,2816]{1,0:T(8,128)(2,1)S(1)} %get-tuple-element.55), channel_id=1, source_target_pairs={{0,2},{2,0},{4,6},{6,4},{8,10},{10,8},{12,14},{14,12},{1,3},{3,1},... | collective-permute-start | bytes 270344 | tf_op jit(solution)/shard_map/ppermute | solution.py:695
  14.9 6.7 %collective-permute-start.5 = (bf16[16,1280]{1,0:T(8,128)(2,1)S(1)}, bf16[16,1280]{1,0:T(8,128)(2,1)S(1)}, u32[]{:S(2)}, u32[]{:S(2)}) collective-permute-start(bf16[16,1280]{1,0:T(8,128)(2,1)S(1)} %get-tuple-element.54.own_ref), channel_id=1, source_target_pairs={{0,14},{2,4},{4,2},{6,8},{8,6},{10,12},{12,10},{14,0},{1,15},{3,5}... | collective-permute-start | bytes 122888 | tf_op jit(solution)/shard_map/ppermute | solution.py:693
  16.7 4.9 %collective-permute-start.4 = (bf16[16,1280]{1,0:T(8,128)(2,1)S(1)}, bf16[16,1280]{1,0:T(8,128)(2,1)S(1)}, u32[]{:S(2)}, u32[]{:S(2)}) collective-permute-start(bf16[16,1280]{1,0:T(8,128)(2,1)S(1)} %get-tuple-element.54.own_ref), channel_id=1, source_target_pairs={{0,12},{2,6},{4,0},{6,10},{8,4},{10,14},{12,8},{14,2},{1,13},{3,7}... | collective-permute-start | bytes 122888 | tf_op jit(solution)/shard_map/ppermute | solution.py:694
  23.1 6.1 %collective-permute-start.6 = (bf16[16,1280]{1,0:T(8,128)(2,1)S(1)}, bf16[16,1280]{1,0:T(8,128)(2,1)S(1)}, u32[]{:S(2)}, u32[]{:S(2)}) collective-permute-start(bf16[16,1280]{1,0:T(8,128)(2,1)S(1)} %get-tuple-element.58.up_own_ref), channel_id=1, source_target_pairs={{0,4},{4,8},{8,12},{12,0},{1,5},{5,9},{9,13},{13,1},{2,6},{6,10},{... | collective-permute-start | bytes 122888 | tf_op jit(solution)/shard_map/ppermute | solution.py:21
  23.5 4.5 %collective-permute-start.8 = (f32[16,128]{1,0:T(8,128)S(1)}, f32[16,128]{1,0:T(8,128)S(1)}, u32[]{:S(2)}, u32[]{:S(2)}) collective-permute-start(f32[16,128]{1,0:T(8,128)S(1)} %get-tuple-element.59.own_ref), channel_id=1, source_target_pairs={{0,8},{4,12},{8,0},{12,4},{1,9},{5,13},{9,1},{13,5},{2,10},{6,14},... | collective-permute-start | bytes 24584 | tf_op jit(solution)/shard_map/ppermute | solution.py:21
  25.6 3.7 %collective-permute-start.7 = (f32[16,128]{1,0:T(8,128)S(1)}, f32[16,128]{1,0:T(8,128)S(1)}, u32[]{:S(2)}, u32[]{:S(2)}) collective-permute-start(f32[16,128]{1,0:T(8,128)S(1)} %get-tuple-element.59.own_ref), channel_id=1, source_target_pairs={{0,12},{4,0},{8,4},{12,8},{1,13},{5,1},{9,5},{13,9},{2,14},{6,2},{... | collective-permute-start | bytes 24584 | tf_op jit(solution)/shard_map/ppermute | solution.py:21
  29.3 4.1 %collective-permute-start.9 = (bf16[16,1280]{1,0:T(8,128)(2,1)S(1)}, bf16[16,1280]{1,0:T(8,128)(2,1)S(1)}, u32[]{:S(2)}, u32[]{:S(2)}) collective-permute-start(bf16[16,1280]{1,0:T(8,128)(2,1)S(1)} %shard_map.109.mine_ref), channel_id=1, source_target_pairs={{0,2},{2,0},{4,6},{6,4},{8,10},{10,8},{12,14},{14,12},{1,3},{3,1},... | collective-permute-start | bytes 122888 | tf_op jit(solution)/shard_map/ppermute | solution.py:749
